TPU v7x, 256 devices: a whole 4x4x8 slice. The times are simulated.
256 devices in a mesh: tm: 16 (over z, core), space: 16 (over y, x).
Axes of the slice: x: 4, y: 4, z: 8, core: 2. Of those that a mesh axis runs over, the one named last changes fastest.
Arguments:
- starts: float32 [16, 192, 64, 128], P('tm', 'space'), may hold values from -45 to 45
- vel_x: float32 [192, 64, 128], P('space'), may hold values from -0.15 to 0.15
- vel_y: float32 [192, 64, 128], P('space'), may hold values from -0.15 to 0.15
- vel_z: float32 [192, 64, 128], P('space'), may hold values from -0.5 to 0.5
- kappa: float32 [192, 64, 128], P('space'), may hold values from 0.01 to 0.03
Outputs:
- new_starts: float32 [16, 192, 64, 128], P('tm', 'space')
- change_norm: float32 [], replicated
All inputs are finite; a program needn't handle non-finite values.
Results may differ from a plain program's by a relative error of at most 0.0003.
Values sent between devices are 32-bit elements; how exact they have to be, the bound alone decides.
No kernel may reach another device: no remote copies, remote signals or barrier semaphores. Data moves between devices by JAX's collectives and lax.ppermute only.
A program may use at most 128 MiB of HBM per device.

v0:
```python
import jax
import jax.numpy as jnp
from jax import lax
from jax.sharding import PartitionSpec as P

FSTEPS = 6
GC = 2


def padded_2(value, sides, width):
    for axis, dim in sides:
        size, length = (lax.axis_size(axis), value.shape[dim])
        up = [(i, (i + 1) % size) for i in range(size - 1)]
        down = [(j, i) for i, j in up]
        last = lax.slice_in_dim(value, length - width, length, axis=dim)
        first = lax.slice_in_dim(value, 0, width, axis=dim)
        before = lax.ppermute(last, axis, up)
        after = lax.ppermute(first, axis, down)
        value = jnp.concatenate([before, value, after], axis=dim)
    return value


def from_behind(value, axis, steps):
    count = lax.axis_size(axis)
    first, last = (max(0, -steps), min(count, count - steps))
    return lax.ppermute(value, axis, [(source, source + steps) for source in range(first, last)])


def advance(extended, vel_x, vel_y, vel_z, kappa):
    padded = jnp.pad(extended, ((0, 0), (1, 1), (1, 1)))
    center = padded[1:-1, 1:-1, 1:-1]
    z_minus = padded[:-2, 1:-1, 1:-1]
    z_plus = padded[2:, 1:-1, 1:-1]
    y_minus = padded[1:-1, :-2, 1:-1]
    y_plus = padded[1:-1, 2:, 1:-1]
    x_minus = padded[1:-1, 1:-1, :-2]
    x_plus = padded[1:-1, 1:-1, 2:]
    transport = jnp.maximum(vel_x, 0.0) * (center - x_minus) + jnp.minimum(vel_x, 0.0) * (
        x_plus - center
    )
    transport = transport + (
        jnp.maximum(vel_y, 0.0) * (center - y_minus) + jnp.minimum(vel_y, 0.0) * (y_plus - center)
    )
    transport = transport + (
        jnp.maximum(vel_z, 0.0) * (center - z_minus) + jnp.minimum(vel_z, 0.0) * (z_plus - center)
    )
    diffusion = kappa * (x_minus + x_plus + y_minus + y_plus + z_minus + z_plus - 6.0 * center)
    return center - transport + diffusion


def restrict(field):
    depth, rows, cols = field.shape
    return field.reshape(depth // 4, 4, rows // 4, 4, cols // 4, 4).mean(axis=(1, 3, 5))


def prolong(field):
    depth, rows, cols = field.shape
    wide = jnp.broadcast_to(field[:, None, :, None, :, None], (depth, 4, rows, 4, cols, 4))
    return wide.reshape(depth * 4, rows * 4, cols * 4)


def per_device(starts, vel_x, vel_y, vel_z, kappa):
    start_state = starts[0]
    field = start_state
    for step_index in range(FSTEPS):
        extended = padded_2(field, (("space", 0),), 1)
        field = advance(extended, vel_x, vel_y, vel_z, kappa)
    courant_scale = FSTEPS / (4.0 * GC)
    diffusion_scale = FSTEPS / (16.0 * GC)
    coarse_set = jnp.stack(
        [
            restrict(start_state),
            restrict(field),
            restrict(vel_x) * courant_scale,
            restrict(vel_y) * courant_scale,
            restrict(vel_z) * courant_scale,
            restrict(kappa) * diffusion_scale,
        ]
    )

    def borders(coarse_field):
        return padded_2(coarse_field, (("space", 0),), 1)

    coarse_start = coarse_set[0]
    fine_coarse = coarse_set[1]

    def coarse(coarse_field):
        for step_index in range(GC):
            coarse_field = advance(
                borders(coarse_field), coarse_set[2], coarse_set[3], coarse_set[4], coarse_set[5]
            )
        return coarse_field

    drift_term = fine_coarse - coarse(coarse_start)
    slice_index = lax.axis_index("tm")
    chain_turns = lax.axis_size("tm") - 1

    def sweep_turn(turn_index, coarse_now):
        received = from_behind(coarse(coarse_now) + drift_term, "tm", 1)
        return jnp.where(slice_index == 0, coarse_start, received)

    current = lax.fori_loop(0, chain_turns, sweep_turn, coarse_start)
    received_end = from_behind(field, "tm", 1)
    corrected = received_end + prolong(current - restrict(received_end))
    new_state = jnp.where(slice_index == 0, start_state, corrected)
    local_sum = jnp.sum((new_state - start_state) ** 2)
    total_sum = lax.psum(local_sum, ("tm", "space"))
    cell_count = lax.axis_size("tm") * lax.axis_size("space") * new_state.size
    change = jnp.sqrt(total_sum / cell_count + 1e-06)
    return (new_state[None], change)


def solution(mesh):
    return jax.shard_map(
        per_device,
        mesh=mesh,
        in_specs=(
            P("tm", "space", None, None),
            P("space", None, None),
            P("space", None, None),
            P("space", None, None),
            P("space", None, None),
        ),
        out_specs=(P("tm", "space", None, None), P()),
        check_vma=False,
    )
```

profile of v0, /device:TPU:1, one launch (start us, length us, event | category | flops | bytes accessed | tf_op | source)
XLA Modules:
  0.0 719.2 jit_solution(9589758726818669204)
XLA Ops:
  18.4 15.2 %reshape_squeeze.3 = f32[3,4,16,4,32,4]{5,4,3,2,1,0:T(8,128)} reshape(f32[1,12,64,128]{3,2,1,0:T(8,128)} %param.7) | data formatting | bytes 786432 | tf_op jit(solution)/shard_map/reshape;squeeze | solution.py:53
  33.5 5.6 reduce_sum.72
  59.8 14.3 %reshape.28 = f32[3,4,16,4,32,4]{5,4,3,2,1,0:T(8,128)} reshape(f32[12,64,128]{2,1,0:T(8,128)S(1)} %copy-done.3) | data formatting | bytes 786432 | tf_op jit(solution)/shard_map/reshape | solution.py:53
  74.2 14.3 %reshape.29 = f32[3,4,16,4,32,4]{5,4,3,2,1,0:T(8,128)} reshape(f32[12,64,128]{2,1,0:T(8,128)S(1)} %copy-done.2) | data formatting | bytes 786432 | tf_op jit(solution)/shard_map/reshape | solution.py:53
  88.5 14.4 %reshape.30 = f32[3,4,16,4,32,4]{5,4,3,2,1,0:T(8,128)} reshape(f32[12,64,128]{2,1,0:T(8,128)S(1)} %copy-done.1) | data formatting | bytes 786432 | tf_op jit(solution)/shard_map/reshape | solution.py:53
  102.9 14.3 %reshape.31 = f32[3,4,16,4,32,4]{5,4,3,2,1,0:T(8,128)} reshape(f32[12,64,128]{2,1,0:T(8,128)S(1)} %copy-done) | data formatting | bytes 786432 | tf_op jit(solution)/shard_map/reshape | solution.py:53
  117.1 5.6 reduce_sum.73
  122.7 5.6 reduce_sum.74
  128.3 5.6 reduce_sum.75
  133.8 5.6 reduce_sum.76
  140.4 5.8 collective-permute-start.13
  147.7 5.6 collective-permute-done.14
  154.3 5.5 collective-permute-start.15
  167.5 10.9 %collective-permute-start.17 = (f32[12,64,128]{2,1,0:T(8,128)S(1)}, f32[12,64,128]{2,1,0:T(8,128)S(1)}, u32[]{:S(2)}, u32[]{:S(2)}) collective-permute-start(f32[12,64,128]{2,1,0:T(8,128)S(1)} %fusion.35), channel_id=1, source_target_pairs={{0,16},{16,32},{32,48},{48,64},{64,80},{80,96},{96,112},{112,128},... | collective-permute-start | bytes 1179656 | tf_op jit(solution)/shard_map/ppermute | solution.py:26
  178.5 5.7 collective-permute-start.20
  189.0 14.3 %reshape.32 = f32[3,4,16,4,32,4]{5,4,3,2,1,0:T(8,128)} reshape(f32[12,64,128]{2,1,0:T(8,128)S(1)} %fusion.35) | data formatting | bytes 786432 | tf_op jit(solution)/shard_map/reshape | solution.py:53
  203.3 5.6 reduce_sum.77
  209.0 14.3 %reshape.33 = f32[3,4,16,4,32,4]{5,4,3,2,1,0:T(8,128)} reshape(f32[12,64,128]{2,1,0:T(8,128)S(1)} %collective-permute-done.17) | data formatting | bytes 786432 | tf_op jit(solution)/shard_map/reshape | solution.py:53
  223.4 5.6 reduce_sum.78
  228.9 362.6 %while.12 = (s32[]{:T(128)}, f32[3,16,32]{2,1,0:T(8,128)S(1)}, pred[]{:T(512)}, f32[3,16,32]{2,1,0:T(8,128)S(1)}, f32[3,16,32]{2,1,0:T(8,128)S(1)}, /*index=5*/f...) while((s32[]{:T(128)}, f32[3,16,32]{2,1,0:T(8,128)S(1)}, ...), condition=%wide.region_7.8_spmd, body=%wide.region_6.7_spmd.sunk | while | flops 202394 | bytes 274638 | solution.py:102
  256.3 5.9 collective-permute-start.3
  263.2 5.9 collective-permute-start.4
  271.3 6.6 collective-permute-start.1
  280.3 6.6 collective-permute-start.3
  287.9 5.9 collective-permute-start.4
  296.1 6.6 collective-permute-start.1
  305.0 6.6 collective-permute-start.3
  312.6 5.9 collective-permute-start.4
  320.8 6.6 collective-permute-start.1
  329.7 6.6 collective-permute-start.3
  337.4 5.9 collective-permute-start.4
  345.5 6.6 collective-permute-start.1
  354.5 6.6 collective-permute-start.3
  362.1 5.9 collective-permute-start.4
  370.3 6.6 collective-permute-start.1
  379.2 6.6 collective-permute-start.3
  386.8 5.9 collective-permute-start.4
  395.0 6.6 collective-permute-start.1
  403.9 6.6 collective-permute-start.3
  411.6 5.9 collective-permute-start.4
  419.7 6.6 collective-permute-start.1
  428.7 6.6 collective-permute-start.3
  436.3 5.9 collective-permute-start.4
  444.5 6.6 collective-permute-start.1
  453.4 6.6 collective-permute-start.3
  461.0 5.9 collective-permute-start.4
  469.2 6.6 collective-permute-start.1
  478.1 6.6 collective-permute-start.3
  485.8 5.9 collective-permute-start.4
  493.9 6.6 collective-permute-start.1
  502.9 6.6 collective-permute-start.3
  510.5 5.9 collective-permute-start.4
  518.7 6.6 collective-permute-start.1
  527.6 6.6 collective-permute-start.3
  535.2 5.9 collective-permute-start.4
  543.4 6.6 collective-permute-start.1
  552.3 6.6 collective-permute-start.3
  559.9 5.9 collective-permute-start.4
  568.1 6.6 collective-permute-start.1
  577.1 6.6 collective-permute-start.3
  584.7 5.9 collective-permute-start.4
  591.6 6.2 broadcast_in_dim.4
  597.8 11.5 %reshape.34 = f32[12,64,128]{2,1,0:T(8,128)S(1)} reshape(f32[3,4,16,4,32,4]{5,4,3,2,1,0:T(8,128)} %broadcast_in_dim.4) | data formatting | bytes 786432 | tf_op jit(solution)/shard_map/reshape | solution.py:59
  610.7 106.7 %psum.7 = f32[]{:T(128)} all-reduce(f32[]{:T(128)} %get-tuple-element.140), channel_id=1, replica_groups=mesh['tm'=16,'space'=16] {'tm','space'}, use_global_device_ids=true, to_apply=%region_10.11 | all-reduce | flops 1 | bytes 8 | tf_op jit(solution)/shard_map/psum | solution.py:107
  (281 shorter events, 155.1 us)
Async XLA Ops:
  13.7 25.3 %collective-permute-start.7 = (f32[1,64,128]{2,1,0:T(8,128)S(1)}, f32[1,64,128]{2,1,0:T(8,128)S(1)}, u32[]{:S(2)}, u32[]{:S(2)}) collective-permute-start(f32[1,64,128]{2,1,0:T(8,128)S(1)} %get-tuple-element.150), channel_id=1, source_target_pairs={{0,1},{1,2},{2,3},{3,4},{4,5},{5,6},{6,7},{7,8},{8,9},{9,10},{10,1... | collective-permute-start | bytes 98312 | tf_op jit(solution)/shard_map/ppermute | solution.py:17
  16.9 22.2 %collective-permute-start.8 = (f32[1,64,128]{2,1,0:T(8,128)S(1)}, f32[1,64,128]{2,1,0:T(8,128)S(1)}, u32[]{:S(2)}, u32[]{:S(2)}) collective-permute-start(f32[1,64,128]{2,1,0:T(8,128)S(1)} %get-tuple-element.151), channel_id=1, source_target_pairs={{1,0},{2,1},{3,2},{4,3},{5,4},{6,5},{7,6},{8,7},{9,8},{10,9},{11,1... | collective-permute-start | bytes 98312 | tf_op jit(solution)/shard_map/ppermute | solution.py:18
  48.0 91.4 %collective-permute-start.11 = (f32[1,64,128]{2,1,0:T(8,128)S(1)}, f32[1,64,128]{2,1,0:T(8,128)S(1)}, u32[]{:S(2)}, u32[]{:S(2)}) collective-permute-start(f32[1,64,128]{2,1,0:T(8,128)S(1)} %get-tuple-element.146), channel_id=1, source_target_pairs={{0,1},{1,2},{2,3},{3,4},{4,5},{5,6},{6,7},{7,8},{8,9},{9,10},{10,1... | collective-permute-start | bytes 98312 | tf_op jit(solution)/shard_map/ppermute | solution.py:17
  52.7 86.7 %collective-permute-start.12 = (f32[1,64,128]{2,1,0:T(8,128)S(1)}, f32[1,64,128]{2,1,0:T(8,128)S(1)}, u32[]{:S(2)}, u32[]{:S(2)}) collective-permute-start(f32[1,64,128]{2,1,0:T(8,128)S(1)} %get-tuple-element.147), channel_id=1, source_target_pairs={{1,0},{2,1},{3,2},{4,3},{5,4},{6,5},{7,6},{8,7},{9,8},{10,9},{11,1... | collective-permute-start | bytes 98312 | tf_op jit(solution)/shard_map/ppermute | solution.py:18
  54.1 93.5 %collective-permute-start.18 = (f32[1,16,32]{2,1,0:T(8,128)S(1)}, f32[1,16,32]{2,1,0:T(8,128)S(1)}, u32[]{:S(2)}, u32[]{:S(2)}) collective-permute-start(f32[1,16,32]{2,1,0:T(8,128)S(1)} %get-tuple-element.161), channel_id=1, source_target_pairs={{0,1},{1,2},{2,3},{3,4},{4,5},{5,6},{6,7},{7,8},{8,9},{9,10},{10,1... | collective-permute-start | bytes 6152 | tf_op jit(solution)/shard_map/ppermute | solution.py:17
  58.3 89.2 %collective-permute-start.19 = (f32[1,16,32]{2,1,0:T(8,128)S(1)}, f32[1,16,32]{2,1,0:T(8,128)S(1)}, u32[]{:S(2)}, u32[]{:S(2)}) collective-permute-start(f32[1,16,32]{2,1,0:T(8,128)S(1)} %get-tuple-element.162), channel_id=1, source_target_pairs={{1,0},{2,1},{3,2},{4,3},{5,4},{6,5},{7,6},{8,7},{9,8},{10,9},{11,1... | collective-permute-start | bytes 6152 | tf_op jit(solution)/shard_map/ppermute | solution.py:18
  140.4 7.2 %collective-permute-start.13 = (f32[1,64,128]{2,1,0:T(8,128)S(1)}, f32[1,64,128]{2,1,0:T(8,128)S(1)}, u32[]{:S(2)}, u32[]{:S(2)}) collective-permute-start(f32[1,64,128]{2,1,0:T(8,128)S(1)} %get-tuple-element.144), channel_id=1, source_target_pairs={{0,1},{1,2},{2,3},{3,4},{4,5},{5,6},{6,7},{7,8},{8,9},{9,10},{10,1... | collective-permute-start | bytes 98312 | tf_op jit(solution)/shard_map/ppermute | solution.py:17
  146.2 7.1 collective-permute-start.14
  154.3 7.1 collective-permute-start.15
  167.5 41.5 %collective-permute-start.17 = (f32[12,64,128]{2,1,0:T(8,128)S(1)}, f32[12,64,128]{2,1,0:T(8,128)S(1)}, u32[]{:S(2)}, u32[]{:S(2)}) collective-permute-start(f32[12,64,128]{2,1,0:T(8,128)S(1)} %fusion.35), channel_id=1, source_target_pairs={{0,16},{16,32},{32,48},{48,64},{64,80},{80,96},{96,112},{112,128},... | collective-permute-start | bytes 1179656 | tf_op jit(solution)/shard_map/ppermute | solution.py:26
  178.5 7.1 collective-permute-start.20
  255.0 7.3 %collective-permute-start.2 = (f32[1,16,32]{2,1,0:T(8,128)S(1)}, f32[1,16,32]{2,1,0:T(8,128)S(1)}, u32[]{:S(2)}, u32[]{:S(2)}) collective-permute-start(f32[1,16,32]{2,1,0:T(8,128)S(1)} %get-tuple-element.224), channel_id=1, source_target_pairs={{1,0},{2,1},{3,2},{4,3},{5,4},{6,5},{7,6},{8,7},{9,8},{10,9},{11,1... | collective-permute-start | bytes 6152 | tf_op jit(solution)/shard_map/while/body/eval_jaxpr/ppermute | solution.py:18
  270.1 7.9 %collective-permute-start = (f32[1,16,32]{2,1,0:T(8,128)S(1)}, f32[1,16,32]{2,1,0:T(8,128)S(1)}, u32[]{:S(2)}, u32[]{:S(2)}) collective-permute-start(f32[1,16,32]{2,1,0:T(8,128)S(1)} %get-tuple-element.222), channel_id=1, source_target_pairs={{1,0},{2,1},{3,2},{4,3},{5,4},{6,5},{7,6},{8,7},{9,8},{10,9},{11,1... | collective-permute-start | bytes 6152 | tf_op jit(solution)/shard_map/while/body/eval_jaxpr/ppermute | solution.py:18
  271.3 7.4 %collective-permute-start.1 = (f32[1,16,32]{2,1,0:T(8,128)S(1)}, f32[1,16,32]{2,1,0:T(8,128)S(1)}, u32[]{:S(2)}, u32[]{:S(2)}) collective-permute-start(f32[1,16,32]{2,1,0:T(8,128)S(1)} %get-tuple-element.223), channel_id=1, source_target_pairs={{0,1},{1,2},{2,3},{3,4},{4,5},{5,6},{6,7},{7,8},{8,9},{9,10},{10,1... | collective-permute-start | bytes 6152 | tf_op jit(solution)/shard_map/while/body/eval_jaxpr/ppermute | solution.py:17
  279.0 8.0 %collective-permute-start.2 = (f32[1,16,32]{2,1,0:T(8,128)S(1)}, f32[1,16,32]{2,1,0:T(8,128)S(1)}, u32[]{:S(2)}, u32[]{:S(2)}) collective-permute-start(f32[1,16,32]{2,1,0:T(8,128)S(1)} %get-tuple-element.224), channel_id=1, source_target_pairs={{1,0},{2,1},{3,2},{4,3},{5,4},{6,5},{7,6},{8,7},{9,8},{10,9},{11,1... | collective-permute-start | bytes 6152 | tf_op jit(solution)/shard_map/while/body/eval_jaxpr/ppermute | solution.py:18
  280.3 7.4 %collective-permute-start.3 = (f32[1,16,32]{2,1,0:T(8,128)S(1)}, f32[1,16,32]{2,1,0:T(8,128)S(1)}, u32[]{:S(2)}, u32[]{:S(2)}) collective-permute-start(f32[1,16,32]{2,1,0:T(8,128)S(1)} %get-tuple-element.225), channel_id=1, source_target_pairs={{0,1},{1,2},{2,3},{3,4},{4,5},{5,6},{6,7},{7,8},{8,9},{9,10},{10,1... | collective-permute-start | bytes 6152 | tf_op jit(solution)/shard_map/while/body/eval_jaxpr/ppermute | solution.py:17
  294.8 7.9 %collective-permute-start = (f32[1,16,32]{2,1,0:T(8,128)S(1)}, f32[1,16,32]{2,1,0:T(8,128)S(1)}, u32[]{:S(2)}, u32[]{:S(2)}) collective-permute-start(f32[1,16,32]{2,1,0:T(8,128)S(1)} %get-tuple-element.222), channel_id=1, source_target_pairs={{1,0},{2,1},{3,2},{4,3},{5,4},{6,5},{7,6},{8,7},{9,8},{10,9},{11,1... | collective-permute-start | bytes 6152 | tf_op jit(solution)/shard_map/while/body/eval_jaxpr/ppermute | solution.py:18
  296.1 7.4 %collective-permute-start.1 = (f32[1,16,32]{2,1,0:T(8,128)S(1)}, f32[1,16,32]{2,1,0:T(8,128)S(1)}, u32[]{:S(2)}, u32[]{:S(2)}) collective-permute-start(f32[1,16,32]{2,1,0:T(8,128)S(1)} %get-tuple-element.223), channel_id=1, source_target_pairs={{0,1},{1,2},{2,3},{3,4},{4,5},{5,6},{6,7},{7,8},{8,9},{9,10},{10,1... | collective-permute-start | bytes 6152 | tf_op jit(solution)/shard_map/while/body/eval_jaxpr/ppermute | solution.py:17
  303.7 8.0 %collective-permute-start.2 = (f32[1,16,32]{2,1,0:T(8,128)S(1)}, f32[1,16,32]{2,1,0:T(8,128)S(1)}, u32[]{:S(2)}, u32[]{:S(2)}) collective-permute-start(f32[1,16,32]{2,1,0:T(8,128)S(1)} %get-tuple-element.224), channel_id=1, source_target_pairs={{1,0},{2,1},{3,2},{4,3},{5,4},{6,5},{7,6},{8,7},{9,8},{10,9},{11,1... | collective-permute-start | bytes 6152 | tf_op jit(solution)/shard_map/while/body/eval_jaxpr/ppermute | solution.py:18
  305.0 7.4 %collective-permute-start.3 = (f32[1,16,32]{2,1,0:T(8,128)S(1)}, f32[1,16,32]{2,1,0:T(8,128)S(1)}, u32[]{:S(2)}, u32[]{:S(2)}) collective-permute-start(f32[1,16,32]{2,1,0:T(8,128)S(1)} %get-tuple-element.225), channel_id=1, source_target_pairs={{0,1},{1,2},{2,3},{3,4},{4,5},{5,6},{6,7},{7,8},{8,9},{9,10},{10,1... | collective-permute-start | bytes 6152 | tf_op jit(solution)/shard_map/while/body/eval_jaxpr/ppermute | solution.py:17
  319.5 7.9 %collective-permute-start = (f32[1,16,32]{2,1,0:T(8,128)S(1)}, f32[1,16,32]{2,1,0:T(8,128)S(1)}, u32[]{:S(2)}, u32[]{:S(2)}) collective-permute-start(f32[1,16,32]{2,1,0:T(8,128)S(1)} %get-tuple-element.222), channel_id=1, source_target_pairs={{1,0},{2,1},{3,2},{4,3},{5,4},{6,5},{7,6},{8,7},{9,8},{10,9},{11,1... | collective-permute-start | bytes 6152 | tf_op jit(solution)/shard_map/while/body/eval_jaxpr/ppermute | solution.py:18
  320.8 7.4 %collective-permute-start.1 = (f32[1,16,32]{2,1,0:T(8,128)S(1)}, f32[1,16,32]{2,1,0:T(8,128)S(1)}, u32[]{:S(2)}, u32[]{:S(2)}) collective-permute-start(f32[1,16,32]{2,1,0:T(8,128)S(1)} %get-tuple-element.223), channel_id=1, source_target_pairs={{0,1},{1,2},{2,3},{3,4},{4,5},{5,6},{6,7},{7,8},{8,9},{9,10},{10,1... | collective-permute-start | bytes 6152 | tf_op jit(solution)/shard_map/while/body/eval_jaxpr/ppermute | solution.py:17
  328.4 8.0 %collective-permute-start.2 = (f32[1,16,32]{2,1,0:T(8,128)S(1)}, f32[1,16,32]{2,1,0:T(8,128)S(1)}, u32[]{:S(2)}, u32[]{:S(2)}) collective-permute-start(f32[1,16,32]{2,1,0:T(8,128)S(1)} %get-tuple-element.224), channel_id=1, source_target_pairs={{1,0},{2,1},{3,2},{4,3},{5,4},{6,5},{7,6},{8,7},{9,8},{10,9},{11,1... | collective-permute-start | bytes 6152 | tf_op jit(solution)/shard_map/while/body/eval_jaxpr/ppermute | solution.py:18
  329.7 7.4 %collective-permute-start.3 = (f32[1,16,32]{2,1,0:T(8,128)S(1)}, f32[1,16,32]{2,1,0:T(8,128)S(1)}, u32[]{:S(2)}, u32[]{:S(2)}) collective-permute-start(f32[1,16,32]{2,1,0:T(8,128)S(1)} %get-tuple-element.225), channel_id=1, source_target_pairs={{0,1},{1,2},{2,3},{3,4},{4,5},{5,6},{6,7},{7,8},{8,9},{9,10},{10,1... | collective-permute-start | bytes 6152 | tf_op jit(solution)/shard_map/while/body/eval_jaxpr/ppermute | solution.py:17
  344.2 7.9 %collective-permute-start = (f32[1,16,32]{2,1,0:T(8,128)S(1)}, f32[1,16,32]{2,1,0:T(8,128)S(1)}, u32[]{:S(2)}, u32[]{:S(2)}) collective-permute-start(f32[1,16,32]{2,1,0:T(8,128)S(1)} %get-tuple-element.222), channel_id=1, source_target_pairs={{1,0},{2,1},{3,2},{4,3},{5,4},{6,5},{7,6},{8,7},{9,8},{10,9},{11,1... | collective-permute-start | bytes 6152 | tf_op jit(solution)/shard_map/while/body/eval_jaxpr/ppermute | solution.py:18
  345.5 7.4 %collective-permute-start.1 = (f32[1,16,32]{2,1,0:T(8,128)S(1)}, f32[1,16,32]{2,1,0:T(8,128)S(1)}, u32[]{:S(2)}, u32[]{:S(2)}) collective-permute-start(f32[1,16,32]{2,1,0:T(8,128)S(1)} %get-tuple-element.223), channel_id=1, source_target_pairs={{0,1},{1,2},{2,3},{3,4},{4,5},{5,6},{6,7},{7,8},{8,9},{9,10},{10,1... | collective-permute-start | bytes 6152 | tf_op jit(solution)/shard_map/while/body/eval_jaxpr/ppermute | solution.py:17
  353.2 8.0 %collective-permute-start.2 = (f32[1,16,32]{2,1,0:T(8,128)S(1)}, f32[1,16,32]{2,1,0:T(8,128)S(1)}, u32[]{:S(2)}, u32[]{:S(2)}) collective-permute-start(f32[1,16,32]{2,1,0:T(8,128)S(1)} %get-tuple-element.224), channel_id=1, source_target_pairs={{1,0},{2,1},{3,2},{4,3},{5,4},{6,5},{7,6},{8,7},{9,8},{10,9},{11,1... | collective-permute-start | bytes 6152 | tf_op jit(solution)/shard_map/while/body/eval_jaxpr/ppermute | solution.py:18
  354.5 7.4 %collective-permute-start.3 = (f32[1,16,32]{2,1,0:T(8,128)S(1)}, f32[1,16,32]{2,1,0:T(8,128)S(1)}, u32[]{:S(2)}, u32[]{:S(2)}) collective-permute-start(f32[1,16,32]{2,1,0:T(8,128)S(1)} %get-tuple-element.225), channel_id=1, source_target_pairs={{0,1},{1,2},{2,3},{3,4},{4,5},{5,6},{6,7},{7,8},{8,9},{9,10},{10,1... | collective-permute-start | bytes 6152 | tf_op jit(solution)/shard_map/while/body/eval_jaxpr/ppermute | solution.py:17
  369.0 7.9 %collective-permute-start = (f32[1,16,32]{2,1,0:T(8,128)S(1)}, f32[1,16,32]{2,1,0:T(8,128)S(1)}, u32[]{:S(2)}, u32[]{:S(2)}) collective-permute-start(f32[1,16,32]{2,1,0:T(8,128)S(1)} %get-tuple-element.222), channel_id=1, source_target_pairs={{1,0},{2,1},{3,2},{4,3},{5,4},{6,5},{7,6},{8,7},{9,8},{10,9},{11,1... | collective-permute-start | bytes 6152 | tf_op jit(solution)/shard_map/while/body/eval_jaxpr/ppermute | solution.py:18
  370.3 7.4 %collective-permute-start.1 = (f32[1,16,32]{2,1,0:T(8,128)S(1)}, f32[1,16,32]{2,1,0:T(8,128)S(1)}, u32[]{:S(2)}, u32[]{:S(2)}) collective-permute-start(f32[1,16,32]{2,1,0:T(8,128)S(1)} %get-tuple-element.223), channel_id=1, source_target_pairs={{0,1},{1,2},{2,3},{3,4},{4,5},{5,6},{6,7},{7,8},{8,9},{9,10},{10,1... | collective-permute-start | bytes 6152 | tf_op jit(solution)/shard_map/while/body/eval_jaxpr/ppermute | solution.py:17
  377.9 8.0 %collective-permute-start.2 = (f32[1,16,32]{2,1,0:T(8,128)S(1)}, f32[1,16,32]{2,1,0:T(8,128)S(1)}, u32[]{:S(2)}, u32[]{:S(2)}) collective-permute-start(f32[1,16,32]{2,1,0:T(8,128)S(1)} %get-tuple-element.224), channel_id=1, source_target_pairs={{1,0},{2,1},{3,2},{4,3},{5,4},{6,5},{7,6},{8,7},{9,8},{10,9},{11,1... | collective-permute-start | bytes 6152 | tf_op jit(solution)/shard_map/while/body/eval_jaxpr/ppermute | solution.py:18
  379.2 7.4 %collective-permute-start.3 = (f32[1,16,32]{2,1,0:T(8,128)S(1)}, f32[1,16,32]{2,1,0:T(8,128)S(1)}, u32[]{:S(2)}, u32[]{:S(2)}) collective-permute-start(f32[1,16,32]{2,1,0:T(8,128)S(1)} %get-tuple-element.225), channel_id=1, source_target_pairs={{0,1},{1,2},{2,3},{3,4},{4,5},{5,6},{6,7},{7,8},{8,9},{9,10},{10,1... | collective-permute-start | bytes 6152 | tf_op jit(solution)/shard_map/while/body/eval_jaxpr/ppermute | solution.py:17
  393.7 7.9 %collective-permute-start = (f32[1,16,32]{2,1,0:T(8,128)S(1)}, f32[1,16,32]{2,1,0:T(8,128)S(1)}, u32[]{:S(2)}, u32[]{:S(2)}) collective-permute-start(f32[1,16,32]{2,1,0:T(8,128)S(1)} %get-tuple-element.222), channel_id=1, source_target_pairs={{1,0},{2,1},{3,2},{4,3},{5,4},{6,5},{7,6},{8,7},{9,8},{10,9},{11,1... | collective-permute-start | bytes 6152 | tf_op jit(solution)/shard_map/while/body/eval_jaxpr/ppermute | solution.py:18
  395.0 7.4 %collective-permute-start.1 = (f32[1,16,32]{2,1,0:T(8,128)S(1)}, f32[1,16,32]{2,1,0:T(8,128)S(1)}, u32[]{:S(2)}, u32[]{:S(2)}) collective-permute-start(f32[1,16,32]{2,1,0:T(8,128)S(1)} %get-tuple-element.223), channel_id=1, source_target_pairs={{0,1},{1,2},{2,3},{3,4},{4,5},{5,6},{6,7},{7,8},{8,9},{9,10},{10,1... | collective-permute-start | bytes 6152 | tf_op jit(solution)/shard_map/while/body/eval_jaxpr/ppermute | solution.py:17
  402.6 8.0 %collective-permute-start.2 = (f32[1,16,32]{2,1,0:T(8,128)S(1)}, f32[1,16,32]{2,1,0:T(8,128)S(1)}, u32[]{:S(2)}, u32[]{:S(2)}) collective-permute-start(f32[1,16,32]{2,1,0:T(8,128)S(1)} %get-tuple-element.224), channel_id=1, source_target_pairs={{1,0},{2,1},{3,2},{4,3},{5,4},{6,5},{7,6},{8,7},{9,8},{10,9},{11,1... | collective-permute-start | bytes 6152 | tf_op jit(solution)/shard_map/while/body/eval_jaxpr/ppermute | solution.py:18
  403.9 7.4 %collective-permute-start.3 = (f32[1,16,32]{2,1,0:T(8,128)S(1)}, f32[1,16,32]{2,1,0:T(8,128)S(1)}, u32[]{:S(2)}, u32[]{:S(2)}) collective-permute-start(f32[1,16,32]{2,1,0:T(8,128)S(1)} %get-tuple-element.225), channel_id=1, source_target_pairs={{0,1},{1,2},{2,3},{3,4},{4,5},{5,6},{6,7},{7,8},{8,9},{9,10},{10,1... | collective-permute-start | bytes 6152 | tf_op jit(solution)/shard_map/while/body/eval_jaxpr/ppermute | solution.py:17
  418.4 7.9 %collective-permute-start = (f32[1,16,32]{2,1,0:T(8,128)S(1)}, f32[1,16,32]{2,1,0:T(8,128)S(1)}, u32[]{:S(2)}, u32[]{:S(2)}) collective-permute-start(f32[1,16,32]{2,1,0:T(8,128)S(1)} %get-tuple-element.222), channel_id=1, source_target_pairs={{1,0},{2,1},{3,2},{4,3},{5,4},{6,5},{7,6},{8,7},{9,8},{10,9},{11,1... | collective-permute-start | bytes 6152 | tf_op jit(solution)/shard_map/while/body/eval_jaxpr/ppermute | solution.py:18
  419.7 7.4 %collective-permute-start.1 = (f32[1,16,32]{2,1,0:T(8,128)S(1)}, f32[1,16,32]{2,1,0:T(8,128)S(1)}, u32[]{:S(2)}, u32[]{:S(2)}) collective-permute-start(f32[1,16,32]{2,1,0:T(8,128)S(1)} %get-tuple-element.223), channel_id=1, source_target_pairs={{0,1},{1,2},{2,3},{3,4},{4,5},{5,6},{6,7},{7,8},{8,9},{9,10},{10,1... | collective-permute-start | bytes 6152 | tf_op jit(solution)/shard_map/while/body/eval_jaxpr/ppermute | solution.py:17
  427.4 8.0 %collective-permute-start.2 = (f32[1,16,32]{2,1,0:T(8,128)S(1)}, f32[1,16,32]{2,1,0:T(8,128)S(1)}, u32[]{:S(2)}, u32[]{:S(2)}) collective-permute-start(f32[1,16,32]{2,1,0:T(8,128)S(1)} %get-tuple-element.224), channel_id=1, source_target_pairs={{1,0},{2,1},{3,2},{4,3},{5,4},{6,5},{7,6},{8,7},{9,8},{10,9},{11,1... | collective-permute-start | bytes 6152 | tf_op jit(solution)/shard_map/while/body/eval_jaxpr/ppermute | solution.py:18
  428.7 7.4 %collective-permute-start.3 = (f32[1,16,32]{2,1,0:T(8,128)S(1)}, f32[1,16,32]{2,1,0:T(8,128)S(1)}, u32[]{:S(2)}, u32[]{:S(2)}) collective-permute-start(f32[1,16,32]{2,1,0:T(8,128)S(1)} %get-tuple-element.225), channel_id=1, source_target_pairs={{0,1},{1,2},{2,3},{3,4},{4,5},{5,6},{6,7},{7,8},{8,9},{9,10},{10,1... | collective-permute-start | bytes 6152 | tf_op jit(solution)/shard_map/while/body/eval_jaxpr/ppermute | solution.py:17
  443.2 7.9 %collective-permute-start = (f32[1,16,32]{2,1,0:T(8,128)S(1)}, f32[1,16,32]{2,1,0:T(8,128)S(1)}, u32[]{:S(2)}, u32[]{:S(2)}) collective-permute-start(f32[1,16,32]{2,1,0:T(8,128)S(1)} %get-tuple-element.222), channel_id=1, source_target_pairs={{1,0},{2,1},{3,2},{4,3},{5,4},{6,5},{7,6},{8,7},{9,8},{10,9},{11,1... | collective-permute-start | bytes 6152 | tf_op jit(solution)/shard_map/while/body/eval_jaxpr/ppermute | solution.py:18
  444.5 7.4 %collective-permute-start.1 = (f32[1,16,32]{2,1,0:T(8,128)S(1)}, f32[1,16,32]{2,1,0:T(8,128)S(1)}, u32[]{:S(2)}, u32[]{:S(2)}) collective-permute-start(f32[1,16,32]{2,1,0:T(8,128)S(1)} %get-tuple-element.223), channel_id=1, source_target_pairs={{0,1},{1,2},{2,3},{3,4},{4,5},{5,6},{6,7},{7,8},{8,9},{9,10},{10,1... | collective-permute-start | bytes 6152 | tf_op jit(solution)/shard_map/while/body/eval_jaxpr/ppermute | solution.py:17
  452.1 8.0 %collective-permute-start.2 = (f32[1,16,32]{2,1,0:T(8,128)S(1)}, f32[1,16,32]{2,1,0:T(8,128)S(1)}, u32[]{:S(2)}, u32[]{:S(2)}) collective-permute-start(f32[1,16,32]{2,1,0:T(8,128)S(1)} %get-tuple-element.224), channel_id=1, source_target_pairs={{1,0},{2,1},{3,2},{4,3},{5,4},{6,5},{7,6},{8,7},{9,8},{10,9},{11,1... | collective-permute-start | bytes 6152 | tf_op jit(solution)/shard_map/while/body/eval_jaxpr/ppermute | solution.py:18
  453.4 7.4 %collective-permute-start.3 = (f32[1,16,32]{2,1,0:T(8,128)S(1)}, f32[1,16,32]{2,1,0:T(8,128)S(1)}, u32[]{:S(2)}, u32[]{:S(2)}) collective-permute-start(f32[1,16,32]{2,1,0:T(8,128)S(1)} %get-tuple-element.225), channel_id=1, source_target_pairs={{0,1},{1,2},{2,3},{3,4},{4,5},{5,6},{6,7},{7,8},{8,9},{9,10},{10,1... | collective-permute-start | bytes 6152 | tf_op jit(solution)/shard_map/while/body/eval_jaxpr/ppermute | solution.py:17
  467.9 7.9 %collective-permute-start = (f32[1,16,32]{2,1,0:T(8,128)S(1)}, f32[1,16,32]{2,1,0:T(8,128)S(1)}, u32[]{:S(2)}, u32[]{:S(2)}) collective-permute-start(f32[1,16,32]{2,1,0:T(8,128)S(1)} %get-tuple-element.222), channel_id=1, source_target_pairs={{1,0},{2,1},{3,2},{4,3},{5,4},{6,5},{7,6},{8,7},{9,8},{10,9},{11,1... | collective-permute-start | bytes 6152 | tf_op jit(solution)/shard_map/while/body/eval_jaxpr/ppermute | solution.py:18
  469.2 7.4 %collective-permute-start.1 = (f32[1,16,32]{2,1,0:T(8,128)S(1)}, f32[1,16,32]{2,1,0:T(8,128)S(1)}, u32[]{:S(2)}, u32[]{:S(2)}) collective-permute-start(f32[1,16,32]{2,1,0:T(8,128)S(1)} %get-tuple-element.223), channel_id=1, source_target_pairs={{0,1},{1,2},{2,3},{3,4},{4,5},{5,6},{6,7},{7,8},{8,9},{9,10},{10,1... | collective-permute-start | bytes 6152 | tf_op jit(solution)/shard_map/while/body/eval_jaxpr/ppermute | solution.py:17
  476.8 8.0 %collective-permute-start.2 = (f32[1,16,32]{2,1,0:T(8,128)S(1)}, f32[1,16,32]{2,1,0:T(8,128)S(1)}, u32[]{:S(2)}, u32[]{:S(2)}) collective-permute-start(f32[1,16,32]{2,1,0:T(8,128)S(1)} %get-tuple-element.224), channel_id=1, source_target_pairs={{1,0},{2,1},{3,2},{4,3},{5,4},{6,5},{7,6},{8,7},{9,8},{10,9},{11,1... | collective-permute-start | bytes 6152 | tf_op jit(solution)/shard_map/while/body/eval_jaxpr/ppermute | solution.py:18
  478.1 7.4 %collective-permute-start.3 = (f32[1,16,32]{2,1,0:T(8,128)S(1)}, f32[1,16,32]{2,1,0:T(8,128)S(1)}, u32[]{:S(2)}, u32[]{:S(2)}) collective-permute-start(f32[1,16,32]{2,1,0:T(8,128)S(1)} %get-tuple-element.225), channel_id=1, source_target_pairs={{0,1},{1,2},{2,3},{3,4},{4,5},{5,6},{6,7},{7,8},{8,9},{9,10},{10,1... | collective-permute-start | bytes 6152 | tf_op jit(solution)/shard_map/while/body/eval_jaxpr/ppermute | solution.py:17
  492.6 7.9 %collective-permute-start = (f32[1,16,32]{2,1,0:T(8,128)S(1)}, f32[1,16,32]{2,1,0:T(8,128)S(1)}, u32[]{:S(2)}, u32[]{:S(2)}) collective-permute-start(f32[1,16,32]{2,1,0:T(8,128)S(1)} %get-tuple-element.222), channel_id=1, source_target_pairs={{1,0},{2,1},{3,2},{4,3},{5,4},{6,5},{7,6},{8,7},{9,8},{10,9},{11,1... | collective-permute-start | bytes 6152 | tf_op jit(solution)/shard_map/while/body/eval_jaxpr/ppermute | solution.py:18
  493.9 7.4 %collective-permute-start.1 = (f32[1,16,32]{2,1,0:T(8,128)S(1)}, f32[1,16,32]{2,1,0:T(8,128)S(1)}, u32[]{:S(2)}, u32[]{:S(2)}) collective-permute-start(f32[1,16,32]{2,1,0:T(8,128)S(1)} %get-tuple-element.223), channel_id=1, source_target_pairs={{0,1},{1,2},{2,3},{3,4},{4,5},{5,6},{6,7},{7,8},{8,9},{9,10},{10,1... | collective-permute-start | bytes 6152 | tf_op jit(solution)/shard_map/while/body/eval_jaxpr/ppermute | solution.py:17
  501.6 8.0 %collective-permute-start.2 = (f32[1,16,32]{2,1,0:T(8,128)S(1)}, f32[1,16,32]{2,1,0:T(8,128)S(1)}, u32[]{:S(2)}, u32[]{:S(2)}) collective-permute-start(f32[1,16,32]{2,1,0:T(8,128)S(1)} %get-tuple-element.224), channel_id=1, source_target_pairs={{1,0},{2,1},{3,2},{4,3},{5,4},{6,5},{7,6},{8,7},{9,8},{10,9},{11,1... | collective-permute-start | bytes 6152 | tf_op jit(solution)/shard_map/while/body/eval_jaxpr/ppermute | solution.py:18
  502.9 7.4 %collective-permute-start.3 = (f32[1,16,32]{2,1,0:T(8,128)S(1)}, f32[1,16,32]{2,1,0:T(8,128)S(1)}, u32[]{:S(2)}, u32[]{:S(2)}) collective-permute-start(f32[1,16,32]{2,1,0:T(8,128)S(1)} %get-tuple-element.225), channel_id=1, source_target_pairs={{0,1},{1,2},{2,3},{3,4},{4,5},{5,6},{6,7},{7,8},{8,9},{9,10},{10,1... | collective-permute-start | bytes 6152 | tf_op jit(solution)/shard_map/while/body/eval_jaxpr/ppermute | solution.py:17
  517.4 7.9 %collective-permute-start = (f32[1,16,32]{2,1,0:T(8,128)S(1)}, f32[1,16,32]{2,1,0:T(8,128)S(1)}, u32[]{:S(2)}, u32[]{:S(2)}) collective-permute-start(f32[1,16,32]{2,1,0:T(8,128)S(1)} %get-tuple-element.222), channel_id=1, source_target_pairs={{1,0},{2,1},{3,2},{4,3},{5,4},{6,5},{7,6},{8,7},{9,8},{10,9},{11,1... | collective-permute-start | bytes 6152 | tf_op jit(solution)/shard_map/while/body/eval_jaxpr/ppermute | solution.py:18
  518.7 7.4 %collective-permute-start.1 = (f32[1,16,32]{2,1,0:T(8,128)S(1)}, f32[1,16,32]{2,1,0:T(8,128)S(1)}, u32[]{:S(2)}, u32[]{:S(2)}) collective-permute-start(f32[1,16,32]{2,1,0:T(8,128)S(1)} %get-tuple-element.223), channel_id=1, source_target_pairs={{0,1},{1,2},{2,3},{3,4},{4,5},{5,6},{6,7},{7,8},{8,9},{9,10},{10,1... | collective-permute-start | bytes 6152 | tf_op jit(solution)/shard_map/while/body/eval_jaxpr/ppermute | solution.py:17
  526.3 8.0 %collective-permute-start.2 = (f32[1,16,32]{2,1,0:T(8,128)S(1)}, f32[1,16,32]{2,1,0:T(8,128)S(1)}, u32[]{:S(2)}, u32[]{:S(2)}) collective-permute-start(f32[1,16,32]{2,1,0:T(8,128)S(1)} %get-tuple-element.224), channel_id=1, source_target_pairs={{1,0},{2,1},{3,2},{4,3},{5,4},{6,5},{7,6},{8,7},{9,8},{10,9},{11,1... | collective-permute-start | bytes 6152 | tf_op jit(solution)/shard_map/while/body/eval_jaxpr/ppermute | solution.py:18
  527.6 7.4 %collective-permute-start.3 = (f32[1,16,32]{2,1,0:T(8,128)S(1)}, f32[1,16,32]{2,1,0:T(8,128)S(1)}, u32[]{:S(2)}, u32[]{:S(2)}) collective-permute-start(f32[1,16,32]{2,1,0:T(8,128)S(1)} %get-tuple-element.225), channel_id=1, source_target_pairs={{0,1},{1,2},{2,3},{3,4},{4,5},{5,6},{6,7},{7,8},{8,9},{9,10},{10,1... | collective-permute-start | bytes 6152 | tf_op jit(solution)/shard_map/while/body/eval_jaxpr/ppermute | solution.py:17
  542.1 7.9 %collective-permute-start = (f32[1,16,32]{2,1,0:T(8,128)S(1)}, f32[1,16,32]{2,1,0:T(8,128)S(1)}, u32[]{:S(2)}, u32[]{:S(2)}) collective-permute-start(f32[1,16,32]{2,1,0:T(8,128)S(1)} %get-tuple-element.222), channel_id=1, source_target_pairs={{1,0},{2,1},{3,2},{4,3},{5,4},{6,5},{7,6},{8,7},{9,8},{10,9},{11,1... | collective-permute-start | bytes 6152 | tf_op jit(solution)/shard_map/while/body/eval_jaxpr/ppermute | solution.py:18
  543.4 7.4 %collective-permute-start.1 = (f32[1,16,32]{2,1,0:T(8,128)S(1)}, f32[1,16,32]{2,1,0:T(8,128)S(1)}, u32[]{:S(2)}, u32[]{:S(2)}) collective-permute-start(f32[1,16,32]{2,1,0:T(8,128)S(1)} %get-tuple-element.223), channel_id=1, source_target_pairs={{0,1},{1,2},{2,3},{3,4},{4,5},{5,6},{6,7},{7,8},{8,9},{9,10},{10,1... | collective-permute-start | bytes 6152 | tf_op jit(solution)/shard_map/while/body/eval_jaxpr/ppermute | solution.py:17
  551.0 8.0 %collective-permute-start.2 = (f32[1,16,32]{2,1,0:T(8,128)S(1)}, f32[1,16,32]{2,1,0:T(8,128)S(1)}, u32[]{:S(2)}, u32[]{:S(2)}) collective-permute-start(f32[1,16,32]{2,1,0:T(8,128)S(1)} %get-tuple-element.224), channel_id=1, source_target_pairs={{1,0},{2,1},{3,2},{4,3},{5,4},{6,5},{7,6},{8,7},{9,8},{10,9},{11,1... | collective-permute-start | bytes 6152 | tf_op jit(solution)/shard_map/while/body/eval_jaxpr/ppermute | solution.py:18
  552.3 7.4 %collective-permute-start.3 = (f32[1,16,32]{2,1,0:T(8,128)S(1)}, f32[1,16,32]{2,1,0:T(8,128)S(1)}, u32[]{:S(2)}, u32[]{:S(2)}) collective-permute-start(f32[1,16,32]{2,1,0:T(8,128)S(1)} %get-tuple-element.225), channel_id=1, source_target_pairs={{0,1},{1,2},{2,3},{3,4},{4,5},{5,6},{6,7},{7,8},{8,9},{9,10},{10,1... | collective-permute-start | bytes 6152 | tf_op jit(solution)/shard_map/while/body/eval_jaxpr/ppermute | solution.py:17
  566.8 7.9 %collective-permute-start = (f32[1,16,32]{2,1,0:T(8,128)S(1)}, f32[1,16,32]{2,1,0:T(8,128)S(1)}, u32[]{:S(2)}, u32[]{:S(2)}) collective-permute-start(f32[1,16,32]{2,1,0:T(8,128)S(1)} %get-tuple-element.222), channel_id=1, source_target_pairs={{1,0},{2,1},{3,2},{4,3},{5,4},{6,5},{7,6},{8,7},{9,8},{10,9},{11,1... | collective-permute-start | bytes 6152 | tf_op jit(solution)/shard_map/while/body/eval_jaxpr/ppermute | solution.py:18
  568.1 7.4 %collective-permute-start.1 = (f32[1,16,32]{2,1,0:T(8,128)S(1)}, f32[1,16,32]{2,1,0:T(8,128)S(1)}, u32[]{:S(2)}, u32[]{:S(2)}) collective-permute-start(f32[1,16,32]{2,1,0:T(8,128)S(1)} %get-tuple-element.223), channel_id=1, source_target_pairs={{0,1},{1,2},{2,3},{3,4},{4,5},{5,6},{6,7},{7,8},{8,9},{9,10},{10,1... | collective-permute-start | bytes 6152 | tf_op jit(solution)/shard_map/while/body/eval_jaxpr/ppermute | solution.py:17
  575.8 8.0 %collective-permute-start.2 = (f32[1,16,32]{2,1,0:T(8,128)S(1)}, f32[1,16,32]{2,1,0:T(8,128)S(1)}, u32[]{:S(2)}, u32[]{:S(2)}) collective-permute-start(f32[1,16,32]{2,1,0:T(8,128)S(1)} %get-tuple-element.224), channel_id=1, source_target_pairs={{1,0},{2,1},{3,2},{4,3},{5,4},{6,5},{7,6},{8,7},{9,8},{10,9},{11,1... | collective-permute-start | bytes 6152 | tf_op jit(solution)/shard_map/while/body/eval_jaxpr/ppermute | solution.py:18
  577.1 7.4 %collective-permute-start.3 = (f32[1,16,32]{2,1,0:T(8,128)S(1)}, f32[1,16,32]{2,1,0:T(8,128)S(1)}, u32[]{:S(2)}, u32[]{:S(2)}) collective-permute-start(f32[1,16,32]{2,1,0:T(8,128)S(1)} %get-tuple-element.225), channel_id=1, source_target_pairs={{0,1},{1,2},{2,3},{3,4},{4,5},{5,6},{6,7},{7,8},{8,9},{9,10},{10,1... | collective-permute-start | bytes 6152 | tf_op jit(solution)/shard_map/while/body/eval_jaxpr/ppermute | solution.py:17
  (33 other events, 282.2 us)
where the time goes:
time: 722 us; the launch traced here: 719 us
  starting transfers between devices  378 us (52%)
  local copies, waits for them, and re-layouts  120 us (17%)
  blocking collectives  107 us (15%)
  waiting for transfers between devices  55.4 us (8%)
  other arithmetic  55 us (8%)
    ppermute x38, starting transfers between devices, padded_2(): before = lax.ppermute(last, axis, up)  230 us
    psum x1, blocking collectives, per_device(): total_sum = lax.psum(local_sum, ('tm', 'space'))  107 us
    ppermute x16, starting transfers between devices, from_behind(): lax.ppermute(value, axis, [(source, source + steps) for source in range(f...  99.1 us
    reshape x6, local copies, waits for them, and re-layouts, restrict(): field.reshape(depth // 4, 4, rows // 4, 4, cols // 4, 4)  86 us
    ppermute x38, starting transfers between devices, padded_2(): after = lax.ppermute(first, axis, down)  49.5 us
    reduce_sum x7, other arithmetic, restrict(): field.reshape(depth // 4, 4, rows // 4, 4, cols // 4, 4)  39 us
    ppermute x38, waiting for transfers between devices, padded_2(): before = lax.ppermute(last, axis, up)  23.9 us
    ppermute x38, waiting for transfers between devices, padded_2(): after = lax.ppermute(first, axis, down)  17.6 us
  transfers between devices with their start and end apart: 92, of which 50 were waited for; matrix products, arithmetic and copies ran while one was open for 17% of the time, Pallas kernels for 0%

commit v1 on v0

v1 whole, which is shorter than its diff:
```python
import jax
import jax.numpy as jnp
from jax import lax
from jax.experimental import pallas as pl
from jax.experimental.pallas import tpu as pltpu
from jax.sharding import PartitionSpec as P


FSTEPS = 6
GC = 2
NZL, NY, NX = 12, 64, 128
SL = 16
SP = 16
NCELL = SL * 192 * NY * NX
COURANT = FSTEPS / (4.0 * GC)
DIFFUSE = FSTEPS / (16.0 * GC)

F32 = jnp.float32
ANY = pl.BlockSpec(memory_space=pl.ANY)
VM = pl.BlockSpec(memory_space=pltpu.VMEM)


def near(x):
    return pltpu.with_memory_space_constraint(x, pltpu.VMEM)


def run_all(copies):
    for c in copies:
        c.start()
    for c in copies:
        c.wait()


def pack_kernel(st, vx, vy, vz, ka, pa, pb, sem):
    core = lax.rem(lax.axis_index("tm"), 2)
    odd = lax.rem(lax.axis_index("space"), 2)
    au, ac = 6 * (1 - odd), 7 * (1 - odd)
    bu, bc = 6 * odd, 7 * odd

    def go(f0, f1):
        pairs = [
            (st.at[0, pl.ds(au, 6)], pa.at[0:6]),
            (f0.at[pl.ds(ac, 5)], pa.at[6:11]),
            (f1.at[pl.ds(ac, 5)], pa.at[11:16]),
            (st.at[0, pl.ds(bu, 6)], pb.at[0:6]),
            (f0.at[pl.ds(bc, 5)], pb.at[6:11]),
            (f1.at[pl.ds(bc, 5)], pb.at[11:16]),
        ]
        run_all([pltpu.make_async_copy(a, b, sem.at[i]) for i, (a, b) in enumerate(pairs)])

    @pl.when(core == 0)
    def _():
        go(vx, vy)

    @pl.when(core == 1)
    def _():
        go(vz, ka)


def block_sum(v):
    row = lax.broadcasted_iota(jnp.int32, v.shape, 1)
    lane = lax.broadcasted_iota(jnp.int32, v.shape, 2)
    v = v + jnp.where((row & 1) == 0, pltpu.roll(v, 7, 1), pltpu.roll(v, 1, 1))
    v = v + jnp.where((row & 2) == 0, pltpu.roll(v, 6, 1), pltpu.roll(v, 2, 1))
    v = v + jnp.where((lane & 1) == 0, pltpu.roll(v, 127, 2), pltpu.roll(v, 1, 2))
    v = v + jnp.where((lane & 2) == 0, pltpu.roll(v, 126, 2), pltpu.roll(v, 2, 2))
    return v


def fine_kernel(st, nx, vx, vy, vz, ka, ra, rb, sa, sb, fine, pay, u, c, w, rows, ck, sem):
    n = lax.axis_index("tm")
    s = lax.axis_index("space")
    core = lax.rem(n, 2)
    odd = lax.rem(s, 2)
    au, ac = 18 * (1 - odd), 17 * (1 - odd)
    bu, bc = 18 * odd, 17 * odd
    own = 2 * core
    oth = 2 - own
    pairs = [
        (vx, c.at[0, 5:17]),
        (vy, c.at[1, 5:17]),
        (vz, c.at[2, 5:17]),
        (ka, c.at[3, 5:17]),
        (ra.at[6:11], c.at[own, pl.ds(ac, 5)]),
        (ra.at[11:16], c.at[own + 1, pl.ds(ac, 5)]),
        (rb.at[6:11], c.at[own, pl.ds(bc, 5)]),
        (rb.at[11:16], c.at[own + 1, pl.ds(bc, 5)]),
        (sa.at[6:11], c.at[oth, pl.ds(ac, 5)]),
        (sa.at[11:16], c.at[oth + 1, pl.ds(ac, 5)]),
        (sb.at[6:11], c.at[oth, pl.ds(bc, 5)]),
        (sb.at[11:16], c.at[oth + 1, pl.ds(bc, 5)]),
        (st.at[0], u.at[0, 6:18]),
        (ra.at[0:6], u.at[0, pl.ds(au, 6)]),
        (rb.at[0:6], u.at[0, pl.ds(bu, 6)]),
    ]
    run_all([pltpu.make_async_copy(a, b, sem.at[i]) for i, (a, b) in enumerate(pairs)])

    row = lax.broadcasted_iota(jnp.int32, (NY, NX), 0)
    lane = lax.broadcasted_iota(jnp.int32, (NY, NX), 1)

    def weights(i, _):
        k = c[3, i]
        cx, cy, cz = c[0, i], c[1, i], c[2, i]
        xm, xp = k + jnp.maximum(cx, 0.0), k - jnp.minimum(cx, 0.0)
        ym, yp = k + jnp.maximum(cy, 0.0), k - jnp.minimum(cy, 0.0)
        zm, zp = k + jnp.maximum(cz, 0.0), k - jnp.minimum(cz, 0.0)
        w[0, i] = 1.0 - ((xm + xp) + (ym + yp) + (zm + zp))
        w[1, i] = jnp.where(lane == 0, 0.0, xm)
        w[2, i] = jnp.where(lane == NX - 1, 0.0, xp)
        w[3, i] = jnp.where(row == 0, 0.0, ym)
        w[4, i] = jnp.where(row == NY - 1, 0.0, yp)
        w[5, i] = zm
        w[6, i] = zp
        return 0

    lax.fori_loop(0, 22, weights, 0)

    for t in range(FSTEPS):
        a, b = t % 2, (t + 1) % 2

        def plane(p, _, a=a, b=b, last=t == FSTEPS - 1):
            v = u[a, p]
            i = p - 1
            x = w[1, i] * pltpu.roll(v, 1, 1) + w[2, i] * pltpu.roll(v, NX - 1, 1)
            y = w[3, i] * pltpu.roll(v, 1, 0) + w[4, i] * pltpu.roll(v, NY - 1, 0)
            z = w[5, i] * u[a, p - 1] + w[6, i] * u[a, p + 1]
            new = w[0, i] * v + (x + (y + z))
            if last:
                fine[p - 6] = new
            else:
                u[b, p] = new
            return 0

        lax.fori_loop(1 + t, 23 - t, plane, 0, unroll=2)


    lane8 = lax.broadcasted_iota(jnp.int32, (8, NX), 1)
    live = jnp.where(n < SL - 1, 1.0, 0.0).astype(F32)
    f = n // 4
    scale = jnp.where(f < 3, COURANT / 64.0, DIFFUSE / 64.0).astype(F32)
    var = jnp.zeros((8, NX), F32)

    def pack(m, base):
        for h in range(2):
            d = jnp.zeros((8, NX), F32)
            for q in range(4):
                d = d + jnp.where((lane8 & 3) == q, m[2 * q + h], 0.0)
            rows[base + 8 * h : base + 8 * h + 8, :] = d

    for zl in range(3):
        ds = [
            (fine[4 * zl + i] - nx[4 * zl + i]).reshape(8, 8, NX) for i in range(4)
        ]
        m = block_sum((ds[0] + ds[1]) + (ds[2] + ds[3])) * (1.0 / 64.0)
        for d in ds:
            r = d - m
            var = var + jnp.sum(r * r, axis=0)
        pack(m, 16 * zl)
        cs = [c[f, 5 + 4 * zl + i].reshape(8, 8, NX) for i in range(4)]
        pack(block_sum((cs[0] + cs[1]) + (cs[2] + cs[3])) * scale, 48 + 16 * zl)

    src = lax.broadcasted_iota(jnp.int32, (NX, NX), 0)
    dst = lax.broadcasted_iota(jnp.int32, (NX, NX), 1)
    perm = jnp.where(src == 4 * (dst & 31) + (dst >> 5), 1.0, 0.0).astype(F32)
    ck[...] = jnp.dot(rows[...], perm, precision=lax.Precision.HIGHEST, preferred_element_type=F32)
    for r in range(4):
        for zl in range(3):
            pay[0, r * 3 + zl : r * 3 + zl + 1, :] = ck[16 * zl + 4 * r : 16 * zl + 4 * r + 1, :]
    rr = lax.rem(n, 4)
    for zl in range(3):
        pay[0, 12 + zl : 13 + zl, :] = ck[pl.ds(48 + 16 * zl + 4 * rr, 1), :]
    pay[0, 15:16, :] = jnp.sum(var, axis=0, keepdims=True) * live
    for z in range(1, 8):
        pay[z] = pay[0]


def sweep_kernel(ga, gb, fine, st, out, change, jj, w, gs, base, sem):
    nd = lax.axis_index("tm")
    s = lax.axis_index("space")
    core = lax.rem(nd, 2)

    @pl.when(core == 0)
    def _():
        run_all([pltpu.make_async_copy(ga, jj.at[0], sem.at[0]), pltpu.make_async_copy(gb, jj.at[1], sem.at[1])])

    @pl.when(core == 1)
    def _():
        run_all([pltpu.make_async_copy(ga, jj.at[1], sem.at[0]), pltpu.make_async_copy(gb, jj.at[0], sem.at[1])])

    @pl.when(nd == 0)
    def _():
        run_all([pltpu.make_async_copy(st.at[0], base, sem.at[2])])

    @pl.when(nd > 0)
    def _():
        run_all([pltpu.make_async_copy(fine, base, sem.at[2])])

    def load(n, q, h):
        start = h * 1024 + (n // 2) * 16 + q
        return jj[lax.rem(n, 2), pl.ds(start, 8, stride=128), :]

    row = lax.broadcasted_iota(jnp.int32, (8, NX), 0)
    lane = lax.broadcasted_iota(jnp.int32, (8, NX), 1)
    x_lo, x_hi = (lane & 31) == 0, (lane & 31) == 31
    y_lo, y_hi = lane < 32, lane >= 96
    z_lo, z_hi = row == 0, row == 7

    def at(r, zl, h):
        return (r * 3 + zl) * 2 + h

    cells = [(r, zl, h) for r in range(4) for zl in range(3) for h in range(2)]
    for r, zl, h in cells:
        cx, cy, cz, k = (load(4 * f + r, 12 + zl, h) for f in range(4))
        xm, xp = k + jnp.maximum(cx, 0.0), k - jnp.minimum(cx, 0.0)
        ym, yp = k + jnp.maximum(cy, 0.0), k - jnp.minimum(cy, 0.0)
        zm, zp = k + jnp.maximum(cz, 0.0), k - jnp.minimum(cz, 0.0)
        i = at(r, zl, h)
        w[0, i] = 1.0 - ((xm + xp) + (ym + yp) + (zm + zp))
        w[1, i] = jnp.where(x_lo, 0.0, xm)
        w[2, i] = jnp.where(x_hi, 0.0, xp)
        w[3, i] = jnp.where(y_lo, 0.0, ym) if r == 0 else ym
        w[4, i] = jnp.where(y_hi, 0.0, yp) if r == 3 else yp
        w[5, i] = jnp.where(z_lo, 0.0, zm) if zl == 0 and h == 0 else zm
        w[6, i] = jnp.where(z_hi, 0.0, zp) if zl == 2 and h == 1 else zp

    def coarse_step(e):
        new = []
        low = {}
        high = {}
        for r in range(4):
            dn = [pltpu.roll(e[at(r, 2, h)], 1, 0) for h in range(2)]
            low[r] = [dn[0], jnp.where(z_lo, dn[0], dn[1])]
            up = [pltpu.roll(e[at(r, 0, h)], 7, 0) for h in range(2)]
            high[r] = [jnp.where(z_hi, up[1], up[0]), up[1]]
        for r, zl, h in cells:
            i = at(r, zl, h)
            v = e[i]
            y0 = e[at(r - 1, zl, h)] if r > 0 else pltpu.roll(e[at(3, zl, h)], 32, 1)
            y1 = e[at(r + 1, zl, h)] if r < 3 else pltpu.roll(e[at(0, zl, h)], 96, 1)
            z0 = e[at(r, zl - 1, h)] if zl > 0 else low[r][h]
            z1 = e[at(r, zl + 1, h)] if zl < 2 else high[r][h]
            x = w[1, i] * pltpu.roll(v, 1, 1) + w[2, i] * pltpu.roll(v, NX - 1, 1)
            y = w[3, i] * y0 + w[4, i] * y1
            z = w[5, i] * z0 + w[6, i] * z1
            new.append(w[0, i] * v + (x + (y + z)))
        return tuple(new)

    zero = jnp.zeros((8, NX), F32)
    e = tuple(load(0, r * 3 + zl, h) for r, zl, h in cells)
    acc = zero
    for v in e:
        acc = acc + v * v
    for q in range(12):
        gs[0, q] = jnp.zeros((16, NX), F32)

    def turn(n, carry):
        e, acc = carry
        for _ in range(GC):
            e = coarse_step(e)
        new = []
        for r, zl, h in cells:
            g = e[at(r, zl, h)]
            gs[n, r * 3 + zl, 8 * h : 8 * h + 8, :] = g
            v = g + load(n, r * 3 + zl, h)
            acc = acc + v * v
            new.append(v)
        return tuple(new), acc

    e, acc = lax.fori_loop(1, SL - 1, turn, (e, acc))

    part = zero
    for cc in range(2):
        for b in range(16):
            part = part + jj[cc, pl.ds(b * 128 + 15, 8, stride=16), :]
    total = jnp.sum(part + 64.0 * acc)
    value = jnp.sqrt(jnp.full((8, NX), total / NCELL, F32) + 1e-06)
    change[0, 0] = jnp.max(value)

    prev = jnp.maximum(nd - 1, 0)
    g12 = jnp.concatenate([gs[prev, q, pl.ds(s, 1), :] for q in range(12)] + [jnp.zeros((4, NX), F32)], axis=0)
    src = lax.broadcasted_iota(jnp.int32, (NX, 4 * NX), 0)
    dst = lax.broadcasted_iota(jnp.int32, (NX, 4 * NX), 1)
    spread = jnp.where(src == 32 * (dst >> 7) + ((dst & 127) >> 2), 1.0, 0.0).astype(F32)
    wide = jnp.dot(g12, spread, precision=lax.Precision.HIGHEST, preferred_element_type=F32)

    for zl in range(3):
        for q in range(4):
            for h in range(2):
                lo = wide[2 * h * 3 + zl : 2 * h * 3 + zl + 1, q * NX : (q + 1) * NX]
                hi = wide[(2 * h + 1) * 3 + zl : (2 * h + 1) * 3 + zl + 1, q * NX : (q + 1) * NX]
                tile = jnp.where(row < 4, jnp.broadcast_to(lo, (8, NX)), jnp.broadcast_to(hi, (8, NX)))
                y = 8 * (2 * q + h)
                for i in range(4):
                    out[0, 4 * zl + i, y : y + 8, :] = base[4 * zl + i, y : y + 8, :] + tile


def per_device(starts, vel_x, vel_y, vel_z, kappa):
    plane = (NY, NX)
    shape = jax.ShapeDtypeStruct
    even = [(i, i ^ 1) for i in range(SP)]
    odd = [(i, i + 1) for i in range(1, SP - 1, 2)] + [(i + 1, i) for i in range(1, SP - 1, 2)]
    swap = [(i, i ^ 1) for i in range(SL)]
    down = [(i + 1, i) for i in range(SL - 1)]
    up = [(i, i + 1) for i in range(SL - 1)]
    zgroups = [[c + 2 * z for z in range(8)] for c in range(2)]

    pay_a, pay_b = pl.pallas_call(
        pack_kernel,
        out_shape=(pltpu.VMEM((16,) + plane, F32),) * 2,
        in_specs=[ANY] * 5,
        out_specs=(VM, VM),
        scratch_shapes=[pltpu.SemaphoreType.DMA((6,))],
        name="pack",
    )(starts, vel_x, vel_y, vel_z, kappa)
    nxt = lax.ppermute(starts[0], "tm", down)
    ra = lax.ppermute(pay_a, "space", even)
    rb = lax.ppermute(pay_b, "space", odd)
    sa = lax.ppermute(ra, "tm", swap)
    sb = lax.ppermute(rb, "tm", swap)

    fine, pay = pl.pallas_call(
        fine_kernel,
        out_shape=(pltpu.VMEM((NZL,) + plane, F32), pltpu.VMEM((8, 16, NX), F32)),
        in_specs=[ANY, VM] + [ANY] * 4 + [VM] * 4,
        out_specs=(VM, VM),
        scratch_shapes=[
            pltpu.VMEM((2, 24) + plane, F32),
            pltpu.VMEM((4, 22) + plane, F32),
            pltpu.VMEM((7, 22) + plane, F32),
            pltpu.VMEM((96, NX), F32),
            pltpu.VMEM((96, NX), F32),
            pltpu.SemaphoreType.DMA((15,)),
        ],
        name="fine",
    )(starts, near(nxt), vel_x, vel_y, vel_z, kappa, near(ra), near(rb), near(sa), near(sb))

    gz = lax.all_to_all(pay, "tm", 0, 0, axis_index_groups=zgroups)
    fine, gz = lax.optimization_barrier((fine, gz))
    moved = lax.ppermute(fine, "tm", up)
    ga = lax.all_to_all(jnp.broadcast_to(gz[None], (16, 8, 16, NX)), "space", 0, 0)
    gb = lax.ppermute(ga, "tm", swap)

    new, change = pl.pallas_call(
        sweep_kernel,
        out_shape=(shape((1, NZL) + plane, F32), shape((1, 1), F32)),
        in_specs=[VM, VM, VM, ANY],
        out_specs=(VM, pl.BlockSpec(memory_space=pltpu.SMEM)),
        scratch_shapes=[
            pltpu.VMEM((2, 2048, NX), F32),
            pltpu.VMEM((7, 24, 8, NX), F32),
            pltpu.VMEM((15, 12, 16, NX), F32),
            pltpu.VMEM((12,) + plane, F32),
            pltpu.SemaphoreType.DMA((3,)),
        ],
        name="sweep",
    )(near(ga.reshape(2048, NX)), near(gb.reshape(2048, NX)), near(moved), starts)
    return new, change.reshape(())


def solution(mesh):
    return jax.shard_map(
        per_device,
        mesh=mesh,
        in_specs=(
            P("tm", "space", None, None),
            P("space", None, None),
            P("space", None, None),
            P("space", None, None),
            P("space", None, None),
        ),
        out_specs=(P("tm", "space", None, None), P()),
        check_vma=False,
    )
```

time: 722 us -> 92.9 us (0.13)
  starting transfers between devices: 378 us -> 11.5 us
  local copies, waits for them, and re-layouts: 120 us -> 0.11 us
  blocking collectives: 107 us -> 42.4 us
  other arithmetic: 55 us -> 0 us
  waiting for transfers between devices: 55.4 us -> 21.9 us
  Pallas kernels: 0 us -> 15.9 us
    ppermute x92 -> x7, starting transfers between devices: 378 us -> 11.5 us  [the longest x1 2.48 us: per_device(): sa = lax.ppermute(ra, 'tm', swap)]
    psum x1 -> x0, blocking collectives: 107 us -> none  [per_device(): total_sum = lax.psum(local_sum, ('tm', 'space'))]
    reshape x7 -> x0, local copies, waits for them, and re-layouts: 97.5 us -> none  [the longest x6 86 us: restrict(): field.reshape(depth // 4, 4, rows // 4, 4, cols // 4, 4)]
    all_to_all x0 -> x2, blocking collectives: none -> 42.4 us  [the longest x1 27.3 us: per_device(): lax.all_to_all(jnp.broadcast_to(gz[None], (16, 8, 16, NX)), 'space', 0, 0)]
    reduce_sum x8 -> x0, other arithmetic: 40.4 us -> none  [the longest x7 39 us: restrict(): field.reshape(depth // 4, 4, rows // 4, 4, cols // 4, 4)]
    ppermute x92 -> x7, waiting for transfers between devices: 55.4 us -> 21.9 us  [the longest x1 9.7 us: per_device(): ra = lax.ppermute(pay_a, 'space', even)]
    pallas_call x0 -> x3, Pallas kernels: none -> 15.9 us  [the longest x1 9.23 us: per_device(): pl.pallas_call(fine_kernel, out_shape=(pltpu.VMEM((NZL,) + plane, F32), p...]
    another operation x1 -> x0, local copies, waits for them, and re-layouts: 15.2 us -> none  [restrict(): field.reshape(depth // 4, 4, rows // 4, 4, cols // 4, 4)]
  transfers between devices with their start and end apart: 92 -> 7, of which waited for: 50 -> 3; matrix products, arithmetic and copies ran while one was open for 17% -> 0% of each run, Pallas kernels for 0% -> 0%
where the time goes in v1:
time: 92.9 us; the launch traced here: 92.5 us
  blocking collectives  42.4 us (46%)
  waiting for transfers between devices  21.9 us (24%)
  Pallas kernels  15.9 us (17%)
  starting transfers between devices  11.5 us (12%)
    all_to_all x1, blocking collectives, per_device(): lax.all_to_all(jnp.broadcast_to(gz[None], (16, 8, 16, NX)), 'space', 0, 0)  27.3 us
    all_to_all x1, blocking collectives, per_device(): gz = lax.all_to_all(pay, 'tm', 0, 0, axis_index_groups=zgroups)  15.1 us
    ppermute x1, waiting for transfers between devices, per_device(): ra = lax.ppermute(pay_a, 'space', even)  9.7 us
    pallas_call x1, Pallas kernels, per_device(): pl.pallas_call(fine_kernel, out_shape=(pltpu.VMEM((NZL,) + plane, F32), p...  9.23 us
    ppermute x1, waiting for transfers between devices, per_device(): nxt = lax.ppermute(starts[0], 'tm', down)  7.22 us
    pallas_call x1, Pallas kernels, per_device(): pl.pallas_call(sweep_kernel, out_shape=(shape((1, NZL) + plane, F32), sha...  5.28 us
    ppermute x1, waiting for transfers between devices, per_device(): moved = lax.ppermute(fine, 'tm', up)  5.02 us
    ppermute x1, starting transfers between devices, per_device(): sa = lax.ppermute(ra, 'tm', swap)  2.48 us
  transfers between devices with their start and end apart: 7, of which 3 were waited for; matrix products, arithmetic and copies ran while one was open for 0% of the time, Pallas kernels for 0%

profile of v1, /device:TPU:1, one launch (start us, length us, event | category | flops | bytes accessed | tf_op | source)
XLA Modules:
  0.0 92.5 jit_solution(1149866470203614109)
XLA Ops:
  0.6 0.0 copy-start.1
  0.6 1.4 %pack.1 = (f32[16,64,128]{2,1,0:T(8,128)S(1)}, f32[16,64,128]{2,1,0:T(8,128)S(1)}) custom-call(f32[1,12,64,128]{3,2,1,0:T(8,128)} %st.5, f32[12,64,128]{2,1,0:T(8,128)} %vx.3, f32[12,64,128]{2,1,0:T(8,128)} %vy.3, f32[12,64,128]{2,1,0:T(8,128)} %vz.3, f32[12,64,128]{2,1,0:T(8,128)} %ka.3), custom_call_target="tpu_custom_call" | custom-call | tf_op jit(solution)/shard_map/pack/pallas_call | solution.py:307
  2.0 2.1 %collective-permute-start.1 = (f32[16,64,128]{2,1,0:T(8,128)S(1)}, f32[16,64,128]{2,1,0:T(8,128)S(1)}, u32[]{:S(2)}, u32[]{:S(2)}) collective-permute-start(f32[16,64,128]{2,1,0:T(8,128)S(1)} %get-tuple-element.10), channel_id=1, source_target_pairs={{0,1},{1,0},{2,3},{3,2},{4,5},{5,4},{6,7},{7,6},{8,9},{9,8},{10,11... | collective-permute-start | bytes 1572872 | tf_op jit(solution)/shard_map/ppermute | solution.py:316
  4.2 0.7 collective-permute-start.2
  4.9 9.7 %collective-permute-done.1.ra = f32[16,64,128]{2,1,0:T(8,128)S(1)} collective-permute-done((f32[16,64,128]{2,1,0:T(8,128)S(1)}, f32[16,64,128]{2,1,0:T(8,128)S(1)}, u32[]{:S(2)}, u32[]{:S(2)}) %collective-permute-start.1) | collective-permute-done | bytes 524320 | tf_op jit(solution)/shard_map/ppermute | solution.py:316
  14.6 2.5 %collective-permute-start.3 = (f32[16,64,128]{2,1,0:T(8,128)S(1)}, f32[16,64,128]{2,1,0:T(8,128)S(1)}, u32[]{:S(2)}, u32[]{:S(2)}) collective-permute-start(f32[16,64,128]{2,1,0:T(8,128)S(1)} %collective-permute-done.1.ra), channel_id=1, source_target_pairs={{0,16},{16,0},{32,48},{48,32},{64,80},{80,64},{96,112},{112,96},{1... | collective-permute-start | bytes 1572872 | tf_op jit(solution)/shard_map/ppermute | solution.py:318
  17.0 0.0 collective-permute-done.2.rb
  17.0 0.0 collective-permute-start.4
  17.0 0.0 copy-done.1
  17.1 2.4 %collective-permute-start = (f32[12,64,128]{2,1,0:T(8,128)S(1)}, f32[12,64,128]{2,1,0:T(8,128)S(1)}, u32[]{:S(2)}, u32[]{:S(2)}) collective-permute-start(f32[12,64,128]{2,1,0:T(8,128)S(1)} %bitcast.6), channel_id=1, source_target_pairs={{16,0},{32,16},{48,32},{64,48},{80,64},{96,80},{112,96},{128,112},... | collective-permute-start | bytes 1179656 | tf_op jit(solution)/shard_map/ppermute | solution.py:315
  19.5 7.2 %collective-permute-done.nx = f32[12,64,128]{2,1,0:T(8,128)S(1)} collective-permute-done((f32[12,64,128]{2,1,0:T(8,128)S(1)}, f32[12,64,128]{2,1,0:T(8,128)S(1)}, u32[]{:S(2)}, u32[]{:S(2)}) %collective-permute-start) | collective-permute-done | bytes 393248 | tf_op jit(solution)/shard_map/ppermute | solution.py:315
  26.7 0.0 collective-permute-done.3.sa
  26.7 0.0 collective-permute-done.4.sb
  26.7 9.2 %fine.1 = (f32[12,64,128]{2,1,0:T(8,128)S(1)}, f32[8,16,128]{2,1,0:T(8,128)S(1)}) custom-call(f32[1,12,64,128]{3,2,1,0:T(8,128)} %st.5, f32[12,64,128]{2,1,0:T(8,128)S(1)} %collective-permute-done.nx, f32[12,64,128]{2,1,0:T(8,128)} %vx.3, f32[12,64,128]{2,1,0:T(8,128)} %vy.3, f32[12,64,128]{2,1,0:T(8,128)} %vz.3, f32[12,64,128]{2,1,0:T(8,128)} %ka.3, ...), custom_call_target="tpu_custom_call" | custom-call | tf_op jit(solution)/shard_map/fine/pallas_call | solution.py:321
  35.9 0.0 copy-start
  35.9 15.1 %all_to_all.10 = f32[8,16,128]{2,1,0:T(8,128)S(1)} all-to-all(f32[8,16,128]{2,1,0:T(8,128)S(1)} %get-tuple-element.13), channel_id=1, replica_groups={{0,32,64,96,128,160,192,224},{16,48,80,112,144,176,208,240},{1,33,65,97..., dimensions={0} | all-to-all | bytes 131072 | tf_op jit(solution)/shard_map/all_to_all | solution.py:337
  51.1 0.1 broadcast_in_dim.2
  51.2 0.0 copy-done
  51.2 27.3 %all_to_all.11 = f32[16,8,16,128]{3,2,1,0:T(8,128)S(1)} all-to-all(f32[16,8,16,128]{3,2,1,0:T(8,128)S(1)} %broadcast_in_dim.2), channel_id=1, replica_groups=mesh['tm'=16,'space'=16] {'space'}, dimensions={0} | all-to-all | bytes 2097152 | tf_op jit(solution)/shard_map/all_to_all | solution.py:340
  78.4 1.7 %collective-permute-start.5 = (f32[16,8,16,128]{3,2,1,0:T(8,128)S(1)}, f32[16,8,16,128]{3,2,1,0:T(8,128)S(1)}, u32[]{:S(2)}, u32[]{:S(2)}) collective-permute-start(f32[16,8,16,128]{3,2,1,0:T(8,128)S(1)} %all_to_all.11), channel_id=1, source_target_pairs={{0,16},{16,0},{32,48},{48,32},{64,80},{80,64},{96,112},{112,96},{1... | collective-permute-start | bytes 3145736 | tf_op jit(solution)/shard_map/ppermute | solution.py:341
  80.1 2.1 %collective-permute-start.6 = (f32[12,64,128]{2,1,0:T(8,128)}, f32[12,64,128]{2,1,0:T(8,128)S(1)}, u32[]{:S(2)}, u32[]{:S(2)}) collective-permute-start(f32[12,64,128]{2,1,0:T(8,128)} %copy-done), channel_id=1, source_target_pairs={{0,16},{16,32},{32,48},{48,64},{64,80},{80,96},{96,112},{112,128},... | collective-permute-start | bytes 1179656 | tf_op jit(solution)/shard_map/ppermute | solution.py:339
  82.2 5.0 %collective-permute-done.6.fine = f32[12,64,128]{2,1,0:T(8,128)S(1)} collective-permute-done((f32[12,64,128]{2,1,0:T(8,128)}, f32[12,64,128]{2,1,0:T(8,128)S(1)}, u32[]{:S(2)}, u32[]{:S(2)}) %collective-permute-start.6) | collective-permute-done | bytes 393248 | tf_op jit(solution)/shard_map/ppermute | solution.py:339
  87.3 0.0 collective-permute-done.5
  87.3 5.3 %sweep.1 = (f32[1,12,64,128]{3,2,1,0:T(8,128)}, f32[1,1]{1,0:T(1,128)}) custom-call(f32[2048,128]{1,0:T(8,128)S(1)} %bitcast.4, f32[2048,128]{1,0:T(8,128)S(1)} %bitcast.5, f32[12,64,128]{2,1,0:T(8,128)S(1)} %collective-permute-done.6.fine, f32[1,12,64,128]{3,2,1,0:T(8,128)} %st.5), custom_call_target="tpu_custom_call" | custom-call | tf_op jit(solution)/shard_map/sweep/pallas_call | solution.py:343
Async XLA Ops:
  0.6 16.4 %copy-start.1 = (f32[1,12,64,128]{3,2,1,0:T(8,128)S(1)}, f32[1,12,64,128]{3,2,1,0:T(8,128)}, u32[]{:S(2)}) copy-start(f32[1,12,64,128]{3,2,1,0:T(8,128)} %st.5) | copy-start | bytes 1179652
  2.0 12.5 %collective-permute-start.1 = (f32[16,64,128]{2,1,0:T(8,128)S(1)}, f32[16,64,128]{2,1,0:T(8,128)S(1)}, u32[]{:S(2)}, u32[]{:S(2)}) collective-permute-start(f32[16,64,128]{2,1,0:T(8,128)S(1)} %get-tuple-element.10), channel_id=1, source_target_pairs={{0,1},{1,0},{2,3},{3,2},{4,5},{5,4},{6,7},{7,6},{8,9},{9,8},{10,11... | collective-permute-start | bytes 1572872 | tf_op jit(solution)/shard_map/ppermute | solution.py:316
  4.2 12.9 %collective-permute-start.2 = (f32[16,64,128]{2,1,0:T(8,128)S(1)}, f32[16,64,128]{2,1,0:T(8,128)S(1)}, u32[]{:S(2)}, u32[]{:S(2)}) collective-permute-start(f32[16,64,128]{2,1,0:T(8,128)S(1)} %get-tuple-element.11), channel_id=1, source_target_pairs={{1,2},{3,4},{5,6},{7,8},{9,10},{11,12},{13,14},{2,1},{4,3},{6,5},{... | collective-permute-start | bytes 1572872 | tf_op jit(solution)/shard_map/ppermute | solution.py:317
  14.6 12.1 %collective-permute-start.3 = (f32[16,64,128]{2,1,0:T(8,128)S(1)}, f32[16,64,128]{2,1,0:T(8,128)S(1)}, u32[]{:S(2)}, u32[]{:S(2)}) collective-permute-start(f32[16,64,128]{2,1,0:T(8,128)S(1)} %collective-permute-done.1.ra), channel_id=1, source_target_pairs={{0,16},{16,0},{32,48},{48,32},{64,80},{80,64},{96,112},{112,96},{1... | collective-permute-start | bytes 1572872 | tf_op jit(solution)/shard_map/ppermute | solution.py:318
  17.0 9.6 %collective-permute-start.4 = (f32[16,64,128]{2,1,0:T(8,128)S(1)}, f32[16,64,128]{2,1,0:T(8,128)S(1)}, u32[]{:S(2)}, u32[]{:S(2)}) collective-permute-start(f32[16,64,128]{2,1,0:T(8,128)S(1)} %collective-permute-done.2.rb), channel_id=1, source_target_pairs={{0,16},{16,0},{32,48},{48,32},{64,80},{80,64},{96,112},{112,96},{1... | collective-permute-start | bytes 1572872 | tf_op jit(solution)/shard_map/ppermute | solution.py:319
  17.1 9.6 %collective-permute-start = (f32[12,64,128]{2,1,0:T(8,128)S(1)}, f32[12,64,128]{2,1,0:T(8,128)S(1)}, u32[]{:S(2)}, u32[]{:S(2)}) collective-permute-start(f32[12,64,128]{2,1,0:T(8,128)S(1)} %bitcast.6), channel_id=1, source_target_pairs={{16,0},{32,16},{48,32},{64,48},{80,64},{96,80},{112,96},{128,112},... | collective-permute-start | bytes 1179656 | tf_op jit(solution)/shard_map/ppermute | solution.py:315
  35.9 15.2 %copy-start = (f32[12,64,128]{2,1,0:T(8,128)}, f32[12,64,128]{2,1,0:T(8,128)S(1)}, u32[]{:S(2)}) copy-start(f32[12,64,128]{2,1,0:T(8,128)S(1)} %get-tuple-element.15) | copy-start | bytes 1179652
  78.4 8.8 %collective-permute-start.5 = (f32[16,8,16,128]{3,2,1,0:T(8,128)S(1)}, f32[16,8,16,128]{3,2,1,0:T(8,128)S(1)}, u32[]{:S(2)}, u32[]{:S(2)}) collective-permute-start(f32[16,8,16,128]{3,2,1,0:T(8,128)S(1)} %all_to_all.11), channel_id=1, source_target_pairs={{0,16},{16,0},{32,48},{48,32},{64,80},{80,64},{96,112},{112,96},{1... | collective-permute-start | bytes 3145736 | tf_op jit(solution)/shard_map/ppermute | solution.py:341
  80.1 7.2 %collective-permute-start.6 = (f32[12,64,128]{2,1,0:T(8,128)}, f32[12,64,128]{2,1,0:T(8,128)S(1)}, u32[]{:S(2)}, u32[]{:S(2)}) collective-permute-start(f32[12,64,128]{2,1,0:T(8,128)} %copy-done), channel_id=1, source_target_pairs={{0,16},{16,32},{32,48},{48,64},{64,80},{80,96},{96,112},{112,128},... | collective-permute-start | bytes 1179656 | tf_op jit(solution)/shard_map/ppermute | solution.py:339

commit v2 on v1

v2 whole, which is shorter than its diff:
```python
import jax
import jax.numpy as jnp
from jax import lax
from jax.experimental import pallas as pl
from jax.experimental.pallas import tpu as pltpu
from jax.sharding import PartitionSpec as P


FSTEPS = 6
GC = 2
NZL, NY, NX = 12, 64, 128
SL = 16
SP = 16
NCELL = SL * 192 * NY * NX
COURANT = FSTEPS / (4.0 * GC)
DIFFUSE = FSTEPS / (16.0 * GC)

F32 = jnp.float32
LIMIT = 24 << 20
HBM = pl.BlockSpec(memory_space=pltpu.HBM)
VM = pl.BlockSpec(memory_space=pltpu.VMEM)


def near(x):
    return pltpu.with_memory_space_constraint(x, pltpu.VMEM)


def far(x):
    return pltpu.with_memory_space_constraint(x, pltpu.HBM)


def run_all(copies):
    for c in copies:
        c.start()
    for c in copies:
        c.wait()


def pack_kernel(st, vx, vy, vz, ka, pa, pb, sem):
    core = lax.rem(lax.axis_index("tm"), 2)
    odd = lax.rem(lax.axis_index("space"), 2)
    au, ac = 6 * (1 - odd), 7 * (1 - odd)
    bu, bc = 6 * odd, 7 * odd

    def go(f0, f1):
        pairs = [
            (st.at[0, pl.ds(au, 6)], pa.at[0:6]),
            (f0.at[pl.ds(ac, 5)], pa.at[6:11]),
            (f1.at[pl.ds(ac, 5)], pa.at[11:16]),
            (st.at[0, pl.ds(bu, 6)], pb.at[0:6]),
            (f0.at[pl.ds(bc, 5)], pb.at[6:11]),
            (f1.at[pl.ds(bc, 5)], pb.at[11:16]),
        ]
        run_all([pltpu.make_async_copy(a, b, sem.at[i]) for i, (a, b) in enumerate(pairs)])

    @pl.when(core == 0)
    def _():
        go(vx, vy)

    @pl.when(core == 1)
    def _():
        go(vz, ka)


def block_sum(v):
    row = lax.broadcasted_iota(jnp.int32, v.shape, 1)
    lane = lax.broadcasted_iota(jnp.int32, v.shape, 2)
    v = v + jnp.where((row & 1) == 0, pltpu.roll(v, 7, 1), pltpu.roll(v, 1, 1))
    v = v + jnp.where((row & 2) == 0, pltpu.roll(v, 6, 1), pltpu.roll(v, 2, 1))
    v = v + jnp.where((lane & 1) == 0, pltpu.roll(v, 127, 2), pltpu.roll(v, 1, 2))
    v = v + jnp.where((lane & 2) == 0, pltpu.roll(v, 126, 2), pltpu.roll(v, 2, 2))
    return v


def coarse_rows(m, rows, base):
    lane = lax.broadcasted_iota(jnp.int32, (8, NX), 1)
    for h in range(2):
        d = jnp.zeros((8, NX), F32)
        for q in range(4):
            d = d + jnp.where((lane & 3) == q, m[2 * q + h], 0.0)
        rows[base + 8 * h : base + 8 * h + 8, :] = d


def spread_lanes(rows):
    src = lax.broadcasted_iota(jnp.int32, (NX, NX), 0)
    dst = lax.broadcasted_iota(jnp.int32, (NX, NX), 1)
    perm = jnp.where(src == 4 * (dst & 31) + (dst >> 5), 1.0, 0.0).astype(F32)
    return jnp.dot(rows, perm, precision=lax.Precision.HIGHEST, preferred_element_type=F32)


def mix(v, before, after, w, i):
    x = w[1, i] * pltpu.roll(v, 1, 1) + w[2, i] * pltpu.roll(v, NX - 1, 1)
    y = w[3, i] * pltpu.roll(v, 1, 0) + w[4, i] * pltpu.roll(v, NY - 1, 0)
    z = w[5, i] * before + w[6, i] * after
    return w[0, i] * v + (x + (y + z))


def put_weights(w, i, cx, cy, cz, k):
    row = lax.broadcasted_iota(jnp.int32, (NY, NX), 0)
    lane = lax.broadcasted_iota(jnp.int32, (NY, NX), 1)
    xm, xp = k + jnp.maximum(cx, 0.0), k - jnp.minimum(cx, 0.0)
    ym, yp = k + jnp.maximum(cy, 0.0), k - jnp.minimum(cy, 0.0)
    zm, zp = k + jnp.maximum(cz, 0.0), k - jnp.minimum(cz, 0.0)
    w[0, i] = 1.0 - ((xm + xp) + (ym + yp) + (zm + zp))
    w[1, i] = jnp.where(lane == 0, 0.0, xm)
    w[2, i] = jnp.where(lane == NX - 1, 0.0, xp)
    w[3, i] = jnp.where(row == 0, 0.0, ym)
    w[4, i] = jnp.where(row == NY - 1, 0.0, yp)
    w[5, i] = zm
    w[6, i] = zp


def prep_kernel(st, vx, vy, vz, ka, w, lev, part, c, rows, ck, sem):
    n = lax.axis_index("tm")
    pairs = [(vx, c.at[0]), (vy, c.at[1]), (vz, c.at[2]), (ka, c.at[3]), (st.at[0], lev.at[0])]
    run_all([pltpu.make_async_copy(a, b, sem.at[i]) for i, (a, b) in enumerate(pairs)])

    def weights(i, _):
        put_weights(w, i, c[0, i], c[1, i], c[2, i], c[3, i])
        return 0

    lax.fori_loop(0, NZL, weights, 0)

    for t in range(1, FSTEPS):

        def plane(q, _, t=t):
            lev[t, q] = mix(lev[t - 1, q], lev[t - 1, q - 1], lev[t - 1, q + 1], w, q)
            return 0

        lax.fori_loop(t, NZL - t, plane, 0, unroll=2)

    f = n // 4
    scale = jnp.where(f < 3, COURANT / 64.0, DIFFUSE / 64.0).astype(F32)
    for zl in range(3):
        cs = [c[f, 4 * zl + i].reshape(8, 8, NX) for i in range(4)]
        coarse_rows(block_sum((cs[0] + cs[1]) + (cs[2] + cs[3])) * scale, rows, 16 * zl)
    ck[...] = spread_lanes(rows[...])
    for zl in range(3):
        part[zl : zl + 1, :] = ck[pl.ds(16 * zl + 4 * lax.rem(n, 4), 1), :]


def wedge(hi, own, other, w, lev, put, u, wk):
    first = lax.rem(lax.axis_index("tm"), 2) == 0
    sign = (1 - 2 * hi).astype(F32)

    def slab(k):
        return (k - 6) + hi * (23 - 2 * k)

    def halo(k, _):
        j = (k - 1) + hi * (6 - 2 * k)
        a0, a1, b0, b1 = own[6 + j], own[11 + j], other[6 + j], other[11 + j]
        put_weights(
            wk,
            k,
            jnp.where(first, a0, b0),
            jnp.where(first, a1, b1),
            jnp.where(first, b0, a0) * sign,
            jnp.where(first, b1, a1),
        )
        return 0

    def center(k, _):
        q = slab(k)
        for i in range(5):
            wk[i, k] = w[i, q]
        wk[5, k] = w[5 + hi, q]
        wk[6, k] = w[6 - hi, q]
        return 0

    lax.fori_loop(1, 6, halo, 0)
    lax.fori_loop(6, 12, center, 0)
    for k in range(6):
        u[0, k] = own[k + hi * (5 - 2 * k)]

    for t in range(1, FSTEPS + 1):
        a, b = (t - 1) % 2, t % 2
        for k in (5 + t, 6 + t):
            u[a, k] = lev[t - 1, slab(k)]

        def plane(k, _, a=a, b=b, t=t):
            new = mix(u[a, k], u[a, k - 1], u[a, k + 1], wk, k)
            if t == FSTEPS:
                put(k, slab(k), new)
            else:
                u[b, k] = new
            return 0

        lax.fori_loop(t, t + 6, plane, 0, unroll=2)
    return slab


def first_kernel(own, other, w, lev, half, u, wk):
    def put(k, q, new):
        half[k - 6] = new

    wedge(1 - lax.rem(lax.axis_index("space"), 2), own, other, w, lev, put, u, wk)


def second_kernel(own, other, w, lev, half, part, nx, fine, pay, u, wk, rows, ck):
    n = lax.axis_index("tm")
    hi = lax.rem(lax.axis_index("space"), 2)

    def put(k, q, new):
        fine[q] = new

    wedge(hi, own, other, w, lev, put, u, wk)
    for i in range(6):
        fine[i * (2 * hi - 1) + 11 * (1 - hi)] = half[i]

    live = jnp.where(n < SL - 1, 1.0, 0.0).astype(F32)
    var = jnp.zeros((8, NX), F32)
    for zl in range(3):
        ds = [(fine[4 * zl + i] - nx[4 * zl + i]).reshape(8, 8, NX) for i in range(4)]
        m = block_sum((ds[0] + ds[1]) + (ds[2] + ds[3])) * (1.0 / 64.0)
        for d in ds:
            r = d - m
            var = var + jnp.sum(r * r, axis=0)
        coarse_rows(m, rows, 16 * zl)
    ck[...] = spread_lanes(rows[...])
    for r in range(4):
        for zl in range(3):
            pay[0, r * 3 + zl : r * 3 + zl + 1, :] = ck[16 * zl + 4 * r : 16 * zl + 4 * r + 1, :]
    pay[0, 12:15, :] = part[0:3, :]
    pay[0, 15:16, :] = jnp.sum(var, axis=0, keepdims=True) * live
    for z in range(1, 8):
        pay[z] = pay[0]


def sweep_kernel(ga, gb, fine, st, out, change, w, gs, accs, sem):
    core = lax.rem(lax.axis_index("tm"), 2)

    @pl.when(core == 0)
    def _():
        sweep(ga, gb, w, gs, accs)

    @pl.when(core == 1)
    def _():
        sweep(gb, ga, w, gs, accs)

    finish(fine, st, out, change, gs, accs, sem)


def sweep(even, odd, w, gs, accs):
    def load(ref, z, q, h):
        return ref[pl.ds(h * 1024 + z * 16 + q, 8, stride=128), :]

    row = lax.broadcasted_iota(jnp.int32, (8, NX), 0)
    lane = lax.broadcasted_iota(jnp.int32, (8, NX), 1)
    x_lo, x_hi = (lane & 31) == 0, (lane & 31) == 31
    y_lo, y_hi = lane < 32, lane >= 96
    z_lo, z_hi = row == 0, row == 7

    def at(r, zl, h):
        return (r * 3 + zl) * 2 + h

    cells = [(r, zl, h) for r in range(4) for zl in range(3) for h in range(2)]
    for r, zl, h in cells:
        cx, cy, cz, k = (load((even, odd)[r % 2], 2 * f + r // 2, 12 + zl, h) for f in range(4))
        xm, xp = k + jnp.maximum(cx, 0.0), k - jnp.minimum(cx, 0.0)
        ym, yp = k + jnp.maximum(cy, 0.0), k - jnp.minimum(cy, 0.0)
        zm, zp = k + jnp.maximum(cz, 0.0), k - jnp.minimum(cz, 0.0)
        i = at(r, zl, h)
        w[0, i] = 1.0 - ((xm + xp) + (ym + yp) + (zm + zp))
        w[1, i] = jnp.where(x_lo, 0.0, xm)
        w[2, i] = jnp.where(x_hi, 0.0, xp)
        w[3, i] = jnp.where(y_lo, 0.0, ym) if r == 0 else ym
        w[4, i] = jnp.where(y_hi, 0.0, yp) if r == 3 else yp
        w[5, i] = jnp.where(z_lo, 0.0, zm) if zl == 0 and h == 0 else zm
        w[6, i] = jnp.where(z_hi, 0.0, zp) if zl == 2 and h == 1 else zp

    def coarse_step(e):
        new = []
        low = {}
        high = {}
        for r in range(4):
            dn = [pltpu.roll(e[at(r, 2, h)], 1, 0) for h in range(2)]
            low[r] = [dn[0], jnp.where(z_lo, dn[0], dn[1])]
            up = [pltpu.roll(e[at(r, 0, h)], 7, 0) for h in range(2)]
            high[r] = [jnp.where(z_hi, up[1], up[0]), up[1]]
        for r, zl, h in cells:
            i = at(r, zl, h)
            v = e[i]
            y0 = e[at(r - 1, zl, h)] if r > 0 else pltpu.roll(e[at(3, zl, h)], 32, 1)
            y1 = e[at(r + 1, zl, h)] if r < 3 else pltpu.roll(e[at(0, zl, h)], 96, 1)
            z0 = e[at(r, zl - 1, h)] if zl > 0 else low[r][h]
            z1 = e[at(r, zl + 1, h)] if zl < 2 else high[r][h]
            x = w[1, i] * pltpu.roll(v, 1, 1) + w[2, i] * pltpu.roll(v, NX - 1, 1)
            y = w[3, i] * y0 + w[4, i] * y1
            z = w[5, i] * z0 + w[6, i] * z1
            new.append(w[0, i] * v + (x + (y + z)))
        return tuple(new)

    e = tuple(load(even, 0, r * 3 + zl, h) for r, zl, h in cells)
    acc = jnp.zeros((8, NX), F32)
    for v in e:
        acc = acc + v * v
    for q in range(12):
        gs[0, q] = jnp.zeros((16, NX), F32)

    def turn(ref, z, n, e, acc):
        for _ in range(GC):
            e = coarse_step(e)
        new = []
        for r, zl, h in cells:
            g = e[at(r, zl, h)]
            gs[n, r * 3 + zl, 8 * h : 8 * h + 8, :] = g
            v = g + load(ref, z, r * 3 + zl, h)
            acc = acc + v * v
            new.append(v)
        return tuple(new), acc

    def two(z, carry):
        e, acc = turn(odd, z, 2 * z + 1, *carry)
        return turn(even, z + 1, 2 * z + 2, e, acc)

    e, acc = lax.fori_loop(0, 7, two, (e, acc))

    part = jnp.zeros((8, NX), F32)
    for ref in (even, odd):
        for b in range(16):
            part = part + ref[pl.ds(b * 128 + 15, 8, stride=16), :]
    accs[...] = part + 64.0 * acc


def finish(fine, st, out, change, gs, accs, sem):
    nd = lax.axis_index("tm")
    s = lax.axis_index("space")
    row = lax.broadcasted_iota(jnp.int32, (8, NX), 0)
    value = jnp.sqrt(jnp.full((8, NX), jnp.sum(accs[...]) / NCELL, F32) + 1e-06)
    change[0, 0] = jnp.max(value)

    prev = jnp.maximum(nd - 1, 0)
    g12 = jnp.concatenate([gs[prev, q, pl.ds(s, 1), :] for q in range(12)] + [jnp.zeros((4, NX), F32)], axis=0)
    src = lax.broadcasted_iota(jnp.int32, (NX, 4 * NX), 0)
    dst = lax.broadcasted_iota(jnp.int32, (NX, 4 * NX), 1)
    spread = jnp.where(src == 32 * (dst >> 7) + ((dst & 127) >> 2), 1.0, 0.0).astype(F32)
    wide = jnp.dot(g12, spread, precision=lax.Precision.HIGHEST, preferred_element_type=F32)

    @pl.when(nd == 0)
    def _():
        run_all([pltpu.make_async_copy(st.at[0], out.at[0], sem.at[0])])

    @pl.when(nd > 0)
    def _():
        for zl in range(3):
            for q in range(4):
                for h in range(2):
                    i0, i1 = 6 * h + zl, 6 * h + 3 + zl
                    lo = wide[i0 : i0 + 1, q * NX : (q + 1) * NX]
                    hi = wide[i1 : i1 + 1, q * NX : (q + 1) * NX]
                    tile = jnp.where(row < 4, jnp.broadcast_to(lo, (8, NX)), jnp.broadcast_to(hi, (8, NX)))
                    y = 8 * (2 * q + h)
                    for i in range(4):
                        out[0, 4 * zl + i, y : y + 8, :] = fine[4 * zl + i, y : y + 8, :] + tile


def per_device(starts, vel_x, vel_y, vel_z, kappa):
    plane = (NY, NX)
    shape = jax.ShapeDtypeStruct
    even = [(i, i ^ 1) for i in range(SP)]
    odd = [(i, i + 1) for i in range(1, SP - 1, 2)] + [(i + 1, i) for i in range(1, SP - 1, 2)]
    swap = [(i, i ^ 1) for i in range(SL)]
    down = [(i + 1, i) for i in range(SL - 1)]
    up = [(i, i + 1) for i in range(SL - 1)]
    zgroups = [[c + 2 * z for z in range(8)] for c in range(2)]

    pay_a, pay_b = pl.pallas_call(
        pack_kernel,
        out_shape=(pltpu.VMEM((16,) + plane, F32),) * 2,
        in_specs=[HBM] * 5,
        out_specs=(VM, VM),
        scratch_shapes=[pltpu.SemaphoreType.DMA((6,))],
        compiler_params=pltpu.CompilerParams(vmem_limit_bytes=LIMIT),
        name="pack",
    )(*(far(x) for x in (starts, vel_x, vel_y, vel_z, kappa)))
    rb = lax.ppermute(pay_b, "space", odd)
    ra = lax.ppermute(pay_a, "space", even)
    nxt = lax.ppermute(starts[0], "tm", down)
    w, lev, part = pl.pallas_call(
        prep_kernel,
        out_shape=(
            pltpu.VMEM((7, NZL) + plane, F32),
            pltpu.VMEM((FSTEPS, NZL) + plane, F32),
            pltpu.VMEM((8, NX), F32),
        ),
        in_specs=[HBM] * 5,
        out_specs=(VM, VM, VM),
        scratch_shapes=[
            pltpu.VMEM((4, NZL) + plane, F32),
            pltpu.VMEM((48, NX), F32),
            pltpu.VMEM((48, NX), F32),
            pltpu.SemaphoreType.DMA((5,)),
        ],
        compiler_params=pltpu.CompilerParams(vmem_limit_bytes=LIMIT),
        name="prep",
    )(*(far(x) for x in (starts, vel_x, vel_y, vel_z, kappa)))
    work = [pltpu.VMEM((2, 13) + plane, F32), pltpu.VMEM((7, 12) + plane, F32)]
    sa = lax.ppermute(ra, "tm", swap)
    half = pl.pallas_call(
        first_kernel,
        out_shape=pltpu.VMEM((6,) + plane, F32),
        in_specs=[VM] * 4,
        out_specs=VM,
        scratch_shapes=work,
        compiler_params=pltpu.CompilerParams(vmem_limit_bytes=LIMIT),
        name="first",
    )(near(ra), near(sa), near(w), near(lev))
    sb = lax.ppermute(rb, "tm", swap)
    fine, pay = pl.pallas_call(
        second_kernel,
        out_shape=(pltpu.VMEM((NZL,) + plane, F32), pltpu.VMEM((8, 16, NX), F32)),
        in_specs=[VM] * 7,
        out_specs=(VM, VM),
        scratch_shapes=work + [pltpu.VMEM((48, NX), F32), pltpu.VMEM((48, NX), F32)],
        compiler_params=pltpu.CompilerParams(vmem_limit_bytes=LIMIT),
        name="second",
    )(near(rb), near(sb), near(w), near(lev), near(half), near(part), near(nxt))

    gz = lax.all_to_all(pay, "tm", 0, 0, axis_index_groups=zgroups)
    fine, gz = lax.optimization_barrier((fine, gz))
    moved = lax.ppermute(fine, "tm", up)
    ga = lax.all_to_all(jnp.broadcast_to(gz[None], (16, 8, 16, NX)), "space", 0, 0)
    gb = lax.ppermute(ga, "tm", swap)

    new, change = pl.pallas_call(
        sweep_kernel,
        out_shape=(shape((1, NZL) + plane, F32), shape((1, 1), F32)),
        in_specs=[VM, VM, VM, HBM],
        out_specs=(VM, pl.BlockSpec(memory_space=pltpu.SMEM)),
        scratch_shapes=[
            pltpu.VMEM((7, 24, 8, NX), F32),
            pltpu.VMEM((15, 12, 16, NX), F32),
            pltpu.VMEM((8, NX), F32),
            pltpu.SemaphoreType.DMA((1,)),
        ],
        compiler_params=pltpu.CompilerParams(vmem_limit_bytes=LIMIT),
        name="sweep",
    )(near(ga.reshape(2048, NX)), near(gb.reshape(2048, NX)), near(moved), far(starts))
    return new, change.reshape(())


def solution(mesh):
    return jax.shard_map(
        per_device,
        mesh=mesh,
        in_specs=(
            P("tm", "space", None, None),
            P("space", None, None),
            P("space", None, None),
            P("space", None, None),
            P("space", None, None),
        ),
        out_specs=(P("tm", "space", None, None), P()),
        check_vma=False,
    )
```

time: 92.9 us -> 86.7 us (0.933)
  waiting for transfers between devices: 21.9 us -> 15.9 us
    ppermute x1, waiting for transfers between devices: 7.22 us -> 1.46 us  [per_device(): nxt = lax.ppermute(starts[0], 'tm', down)]
    pallas_call x1 -> x3, Pallas kernels: 9.23 us -> 8.57 us  [the longest x1 3.69 us: per_device(): pl.pallas_call(prep_kernel, out_shape=(pltpu.VMEM((7, NZL) + plane, F32),...]
  transfers between devices with their start and end apart: 7 -> 7, of which waited for: 3 -> 3; matrix products, arithmetic and copies ran while one was open for 0% -> 0% of each run, Pallas kernels for 0% -> 7%
where the time goes in v2:
time: 86.7 us; the launch traced here: 86.4 us
  blocking collectives  43 us (50%)
  waiting for transfers between devices  15.9 us (18%)
  Pallas kernels  15.1 us (17%)
  starting transfers between devices  11.6 us (13%)
    all_to_all x1, blocking collectives, per_device(): lax.all_to_all(jnp.broadcast_to(gz[None], (16, 8, 16, NX)), 'space', 0, 0)  27.1 us
    all_to_all x1, blocking collectives, per_device(): gz = lax.all_to_all(pay, 'tm', 0, 0, axis_index_groups=zgroups)  15.9 us
    ppermute x1, waiting for transfers between devices, per_device(): ra = lax.ppermute(pay_a, 'space', even)  9.7 us
    pallas_call x1, Pallas kernels, per_device(): pl.pallas_call(sweep_kernel, out_shape=(shape((1, NZL) + plane, F32), sha...  5.2 us
    ppermute x1, waiting for transfers between devices, per_device(): moved = lax.ppermute(fine, 'tm', up)  4.7 us
    pallas_call x1, Pallas kernels, per_device(): pl.pallas_call(prep_kernel, out_shape=(pltpu.VMEM((7, NZL) + plane, F32),...  3.69 us
    pallas_call x1, Pallas kernels, per_device(): pl.pallas_call(second_kernel, out_shape=(pltpu.VMEM((NZL,) + plane, F32),...  2.63 us
    ppermute x1, starting transfers between devices, per_device(): sa = lax.ppermute(ra, 'tm', swap)  2.48 us
  transfers between devices with their start and end apart: 7, of which 3 were waited for; matrix products, arithmetic and copies ran while one was open for 0% of the time, Pallas kernels for 7%

profile of v2, /device:TPU:1, one launch (start us, length us, event | category | flops | bytes accessed | tf_op | source)
XLA Modules:
  0.0 86.4 jit_solution(9115066738205582228)
XLA Ops:
  0.6 1.4 %pack.1 = (f32[16,64,128]{2,1,0:T(8,128)S(1)}, f32[16,64,128]{2,1,0:T(8,128)S(1)}) custom-call(f32[1,12,64,128]{3,2,1,0:T(8,128)} %st.5, f32[12,64,128]{2,1,0:T(8,128)} %vx.3, f32[12,64,128]{2,1,0:T(8,128)} %vy.3, f32[12,64,128]{2,1,0:T(8,128)} %vz.3, f32[12,64,128]{2,1,0:T(8,128)} %ka.3), custom_call_target="tpu_custom_call" | custom-call | tf_op jit(solution)/shard_map/pack/pallas_call | solution.py:367
  2.0 2.1 %collective-permute-start.2 = (f32[16,64,128]{2,1,0:T(8,128)S(1)}, f32[16,64,128]{2,1,0:T(8,128)S(1)}, u32[]{:S(2)}, u32[]{:S(2)}) collective-permute-start(f32[16,64,128]{2,1,0:T(8,128)S(1)} %get-tuple-element.16), channel_id=1, source_target_pairs={{0,1},{1,0},{2,3},{3,2},{4,5},{5,4},{6,7},{7,6},{8,9},{9,8},{10,11... | collective-permute-start | bytes 1572872 | tf_op jit(solution)/shard_map/ppermute | solution.py:377
  4.1 0.7 collective-permute-start
  4.8 9.7 %collective-permute-done.2.own = f32[16,64,128]{2,1,0:T(8,128)S(1)} collective-permute-done((f32[16,64,128]{2,1,0:T(8,128)S(1)}, f32[16,64,128]{2,1,0:T(8,128)S(1)}, u32[]{:S(2)}, u32[]{:S(2)}) %collective-permute-start.2) | collective-permute-done | bytes 524320 | tf_op jit(solution)/shard_map/ppermute | solution.py:377
  14.5 2.5 %collective-permute-start.3 = (f32[16,64,128]{2,1,0:T(8,128)S(1)}, f32[16,64,128]{2,1,0:T(8,128)S(1)}, u32[]{:S(2)}, u32[]{:S(2)}) collective-permute-start(f32[16,64,128]{2,1,0:T(8,128)S(1)} %collective-permute-done.2.own), channel_id=1, source_target_pairs={{0,16},{16,0},{32,48},{48,32},{64,80},{80,64},{96,112},{112,96},{1... | collective-permute-start | bytes 1572872 | tf_op jit(solution)/shard_map/ppermute | solution.py:398
  17.0 0.0 collective-permute-done.own
  17.0 0.0 collective-permute-start.1
  17.0 2.4 %collective-permute-start.4 = (f32[12,64,128]{2,1,0:T(8,128)}, f32[12,64,128]{2,1,0:T(8,128)S(1)}, u32[]{:S(2)}, u32[]{:S(2)}) collective-permute-start(f32[12,64,128]{2,1,0:T(8,128)} %bitcast.6), channel_id=1, source_target_pairs={{16,0},{32,16},{48,32},{64,48},{80,64},{96,80},{112,96},{128,112},... | collective-permute-start | bytes 1179656 | tf_op jit(solution)/shard_map/ppermute | solution.py:378
  19.4 3.7 %prep.1 = (f32[7,12,64,128]{3,2,1,0:T(8,128)S(1)}, f32[6,12,64,128]{3,2,1,0:T(8,128)S(1)}, f32[8,128]{1,0:T(8,128)S(1)}) custom-call(f32[1,12,64,128]{3,2,1,0:T(8,128)} %st.5, f32[12,64,128]{2,1,0:T(8,128)} %vx.3, f32[12,64,128]{2,1,0:T(8,128)} %vy.3, f32[12,64,128]{2,1,0:T(8,128)} %vz.3, f32[12,64,128]{2,1,0:T(8,128)} %ka.3), custom_call_target="tpu_custom_call" | custom-call | tf_op jit(solution)/shard_map/prep/pallas_call | solution.py:379
  23.1 0.0 collective-permute-done.3.other
  23.1 2.2 %first.1.half = f32[6,64,128]{2,1,0:T(8,128)S(1)} custom-call(f32[16,64,128]{2,1,0:T(8,128)S(1)} %collective-permute-done.2.own, f32[16,64,128]{2,1,0:T(8,128)S(1)} %collective-permute-done.3.other, f32[7,12,64,128]{3,2,1,0:T(8,128)S(1)} %get-tuple-element.14.w, f32[6,12,64,128]{3,2,1,0:T(8,128)S(1)} %get-tuple-element.15.lev), custom_call_target="tpu_custom_call" | custom-call | tf_op jit(solution)/shard_map/first/pallas_call | solution.py:399
  25.4 1.5 %collective-permute-done.4.nx = f32[12,64,128]{2,1,0:T(8,128)S(1)} collective-permute-done((f32[12,64,128]{2,1,0:T(8,128)}, f32[12,64,128]{2,1,0:T(8,128)S(1)}, u32[]{:S(2)}, u32[]{:S(2)}) %collective-permute-start.4) | collective-permute-done | bytes 393248 | tf_op jit(solution)/shard_map/ppermute | solution.py:378
  26.8 0.0 collective-permute-done.1.other
  26.8 2.6 %second.1 = (f32[12,64,128]{2,1,0:T(8,128)S(1)}, f32[8,16,128]{2,1,0:T(8,128)S(1)}) custom-call(f32[16,64,128]{2,1,0:T(8,128)S(1)} %collective-permute-done.own, f32[16,64,128]{2,1,0:T(8,128)S(1)} %collective-permute-done.1.other, f32[7,12,64,128]{3,2,1,0:T(8,128)S(1)} %get-tuple-element.14.w, f32[6,12,64,128]{3,2,1,0:T(8,128)S(1)} %get-tuple-element.15.lev, ...), custom_call_target="tpu_custom_call" | custom-call | tf_op jit(solution)/shard_map/second/pallas_call | solution.py:409
  29.5 15.9 %all_to_all.10 = f32[8,16,128]{2,1,0:T(8,128)S(1)} all-to-all(f32[8,16,128]{2,1,0:T(8,128)S(1)} %get-tuple-element.19), channel_id=1, replica_groups={{0,32,64,96,128,160,192,224},{16,48,80,112,144,176,208,240},{1,33,65,97..., dimensions={0} | all-to-all | bytes 131072 | tf_op jit(solution)/shard_map/all_to_all | solution.py:419
  45.4 0.1 broadcast_in_dim.2
  45.5 27.1 %all_to_all.11 = f32[16,8,16,128]{3,2,1,0:T(8,128)S(1)} all-to-all(f32[16,8,16,128]{3,2,1,0:T(8,128)S(1)} %broadcast_in_dim.2), channel_id=1, replica_groups=mesh['tm'=16,'space'=16] {'space'}, dimensions={0} | all-to-all | bytes 2097152 | tf_op jit(solution)/shard_map/all_to_all | solution.py:422
  72.6 1.8 %collective-permute-start.5 = (f32[16,8,16,128]{3,2,1,0:T(8,128)S(1)}, f32[16,8,16,128]{3,2,1,0:T(8,128)S(1)}, u32[]{:S(2)}, u32[]{:S(2)}) collective-permute-start(f32[16,8,16,128]{3,2,1,0:T(8,128)S(1)} %all_to_all.11), channel_id=1, source_target_pairs={{0,16},{16,0},{32,48},{48,32},{64,80},{80,64},{96,112},{112,96},{1... | collective-permute-start | bytes 3145736 | tf_op jit(solution)/shard_map/ppermute | solution.py:423
  74.4 2.1 %collective-permute-start.6 = (f32[12,64,128]{2,1,0:T(8,128)S(1)}, f32[12,64,128]{2,1,0:T(8,128)S(1)}, u32[]{:S(2)}, u32[]{:S(2)}) collective-permute-start(f32[12,64,128]{2,1,0:T(8,128)S(1)} %get-tuple-element.21), channel_id=1, source_target_pairs={{0,16},{16,32},{32,48},{48,64},{64,80},{80,96},{96,112},{112,128},... | collective-permute-start | bytes 1179656 | tf_op jit(solution)/shard_map/ppermute | solution.py:421
  76.5 4.7 %collective-permute-done.6.fine = f32[12,64,128]{2,1,0:T(8,128)S(1)} collective-permute-done((f32[12,64,128]{2,1,0:T(8,128)S(1)}, f32[12,64,128]{2,1,0:T(8,128)S(1)}, u32[]{:S(2)}, u32[]{:S(2)}) %collective-permute-start.6) | collective-permute-done | bytes 393248 | tf_op jit(solution)/shard_map/ppermute | solution.py:421
  81.2 0.0 collective-permute-done.5
  81.2 5.2 %sweep.1 = (f32[1,12,64,128]{3,2,1,0:T(8,128)}, f32[1,1]{1,0:T(1,128)}) custom-call(f32[2048,128]{1,0:T(8,128)S(1)} %bitcast.4, f32[2048,128]{1,0:T(8,128)S(1)} %bitcast.5, f32[12,64,128]{2,1,0:T(8,128)S(1)} %collective-permute-done.6.fine, f32[1,12,64,128]{3,2,1,0:T(8,128)} %st.5), custom_call_target="tpu_custom_call" | custom-call | tf_op jit(solution)/shard_map/sweep/pallas_call | solution.py:425
Async XLA Ops:
  2.0 12.5 %collective-permute-start.2 = (f32[16,64,128]{2,1,0:T(8,128)S(1)}, f32[16,64,128]{2,1,0:T(8,128)S(1)}, u32[]{:S(2)}, u32[]{:S(2)}) collective-permute-start(f32[16,64,128]{2,1,0:T(8,128)S(1)} %get-tuple-element.16), channel_id=1, source_target_pairs={{0,1},{1,0},{2,3},{3,2},{4,5},{5,4},{6,7},{7,6},{8,9},{9,8},{10,11... | collective-permute-start | bytes 1572872 | tf_op jit(solution)/shard_map/ppermute | solution.py:377
  4.1 12.9 %collective-permute-start = (f32[16,64,128]{2,1,0:T(8,128)S(1)}, f32[16,64,128]{2,1,0:T(8,128)S(1)}, u32[]{:S(2)}, u32[]{:S(2)}) collective-permute-start(f32[16,64,128]{2,1,0:T(8,128)S(1)} %get-tuple-element.13), channel_id=1, source_target_pairs={{1,2},{3,4},{5,6},{7,8},{9,10},{11,12},{13,14},{2,1},{4,3},{6,5},{... | collective-permute-start | bytes 1572872 | tf_op jit(solution)/shard_map/ppermute | solution.py:376
  14.5 8.6 %collective-permute-start.3 = (f32[16,64,128]{2,1,0:T(8,128)S(1)}, f32[16,64,128]{2,1,0:T(8,128)S(1)}, u32[]{:S(2)}, u32[]{:S(2)}) collective-permute-start(f32[16,64,128]{2,1,0:T(8,128)S(1)} %collective-permute-done.2.own), channel_id=1, source_target_pairs={{0,16},{16,0},{32,48},{48,32},{64,80},{80,64},{96,112},{112,96},{1... | collective-permute-start | bytes 1572872 | tf_op jit(solution)/shard_map/ppermute | solution.py:398
  17.0 9.8 %collective-permute-start.1 = (f32[16,64,128]{2,1,0:T(8,128)S(1)}, f32[16,64,128]{2,1,0:T(8,128)S(1)}, u32[]{:S(2)}, u32[]{:S(2)}) collective-permute-start(f32[16,64,128]{2,1,0:T(8,128)S(1)} %collective-permute-done.own), channel_id=1, source_target_pairs={{0,16},{16,0},{32,48},{48,32},{64,80},{80,64},{96,112},{112,96},{1... | collective-permute-start | bytes 1572872 | tf_op jit(solution)/shard_map/ppermute | solution.py:408
  17.0 9.8 %collective-permute-start.4 = (f32[12,64,128]{2,1,0:T(8,128)}, f32[12,64,128]{2,1,0:T(8,128)S(1)}, u32[]{:S(2)}, u32[]{:S(2)}) collective-permute-start(f32[12,64,128]{2,1,0:T(8,128)} %bitcast.6), channel_id=1, source_target_pairs={{16,0},{32,16},{48,32},{64,48},{80,64},{96,80},{112,96},{128,112},... | collective-permute-start | bytes 1179656 | tf_op jit(solution)/shard_map/ppermute | solution.py:378
  72.6 8.6 %collective-permute-start.5 = (f32[16,8,16,128]{3,2,1,0:T(8,128)S(1)}, f32[16,8,16,128]{3,2,1,0:T(8,128)S(1)}, u32[]{:S(2)}, u32[]{:S(2)}) collective-permute-start(f32[16,8,16,128]{3,2,1,0:T(8,128)S(1)} %all_to_all.11), channel_id=1, source_target_pairs={{0,16},{16,0},{32,48},{48,32},{64,80},{80,64},{96,112},{112,96},{1... | collective-permute-start | bytes 3145736 | tf_op jit(solution)/shard_map/ppermute | solution.py:423
  74.4 6.8 %collective-permute-start.6 = (f32[12,64,128]{2,1,0:T(8,128)S(1)}, f32[12,64,128]{2,1,0:T(8,128)S(1)}, u32[]{:S(2)}, u32[]{:S(2)}) collective-permute-start(f32[12,64,128]{2,1,0:T(8,128)S(1)} %get-tuple-element.21), channel_id=1, source_target_pairs={{0,16},{16,32},{32,48},{48,64},{64,80},{80,96},{96,112},{112,128},... | collective-permute-start | bytes 1179656 | tf_op jit(solution)/shard_map/ppermute | solution.py:421

commit v3 on v2

--- a/solution.py
+++ b/solution.py
@@ -119,7 +119,7 @@
         put_weights(w, i, c[0, i], c[1, i], c[2, i], c[3, i])
         return 0
 
-    lax.fori_loop(0, NZL, weights, 0)
+    lax.fori_loop(0, NZL, weights, 0, unroll=4)
 
     for t in range(1, FSTEPS):
 
@@ -127,7 +127,7 @@
             lev[t, q] = mix(lev[t - 1, q], lev[t - 1, q - 1], lev[t - 1, q + 1], w, q)
             return 0
 
-        lax.fori_loop(t, NZL - t, plane, 0, unroll=2)
+        lax.fori_loop(t, NZL - t, plane, 0, unroll=NZL - 2 * t)
 
     f = n // 4
     scale = jnp.where(f < 3, COURANT / 64.0, DIFFUSE / 64.0).astype(F32)
@@ -167,8 +167,8 @@
         wk[6, k] = w[6 - hi, q]
         return 0
 
-    lax.fori_loop(1, 6, halo, 0)
-    lax.fori_loop(6, 12, center, 0)
+    lax.fori_loop(1, 6, halo, 0, unroll=5)
+    lax.fori_loop(6, 12, center, 0, unroll=3)
     for k in range(6):
         u[0, k] = own[k + hi * (5 - 2 * k)]
 
@@ -185,7 +185,7 @@
                 u[b, k] = new
             return 0
 
-        lax.fori_loop(t, t + 6, plane, 0, unroll=2)
+        lax.fori_loop(t, t + 6, plane, 0, unroll=6)
     return slab
 
 
@@ -226,7 +226,7 @@
         pay[z] = pay[0]
 
 
-def sweep_kernel(ga, gb, fine, st, out, change, w, gs, accs, sem):
+def sweep_kernel(ga, gb, wide, change, w, gs, accs):
     core = lax.rem(lax.axis_index("tm"), 2)
 
     @pl.when(core == 0)
@@ -237,7 +237,7 @@
     def _():
         sweep(gb, ga, w, gs, accs)
 
-    finish(fine, st, out, change, gs, accs, sem)
+    summary(wide, change, gs, accs)
 
 
 def sweep(even, odd, w, gs, accs):
@@ -322,10 +322,9 @@
     accs[...] = part + 64.0 * acc
 
 
-def finish(fine, st, out, change, gs, accs, sem):
+def summary(wide, change, gs, accs):
     nd = lax.axis_index("tm")
     s = lax.axis_index("space")
-    row = lax.broadcasted_iota(jnp.int32, (8, NX), 0)
     value = jnp.sqrt(jnp.full((8, NX), jnp.sum(accs[...]) / NCELL, F32) + 1e-06)
     change[0, 0] = jnp.max(value)
 
@@ -334,7 +333,12 @@
     src = lax.broadcasted_iota(jnp.int32, (NX, 4 * NX), 0)
     dst = lax.broadcasted_iota(jnp.int32, (NX, 4 * NX), 1)
     spread = jnp.where(src == 32 * (dst >> 7) + ((dst & 127) >> 2), 1.0, 0.0).astype(F32)
-    wide = jnp.dot(g12, spread, precision=lax.Precision.HIGHEST, preferred_element_type=F32)
+    wide[...] = jnp.dot(g12, spread, precision=lax.Precision.HIGHEST, preferred_element_type=F32)
+
+
+def finish_kernel(wide, fine, st, out, sem):
+    nd = lax.axis_index("tm")
+    row = lax.broadcasted_iota(jnp.int32, (8, NX), 0)
 
     @pl.when(nd == 0)
     def _():
@@ -417,25 +421,32 @@
     )(near(rb), near(sb), near(w), near(lev), near(half), near(part), near(nxt))
 
     gz = lax.all_to_all(pay, "tm", 0, 0, axis_index_groups=zgroups)
-    fine, gz = lax.optimization_barrier((fine, gz))
     moved = lax.ppermute(fine, "tm", up)
     ga = lax.all_to_all(jnp.broadcast_to(gz[None], (16, 8, 16, NX)), "space", 0, 0)
     gb = lax.ppermute(ga, "tm", swap)
 
-    new, change = pl.pallas_call(
+    wide, change = pl.pallas_call(
         sweep_kernel,
-        out_shape=(shape((1, NZL) + plane, F32), shape((1, 1), F32)),
-        in_specs=[VM, VM, VM, HBM],
+        out_shape=(pltpu.VMEM((16, 4 * NX), F32), shape((1, 1), F32)),
+        in_specs=[VM, VM],
         out_specs=(VM, pl.BlockSpec(memory_space=pltpu.SMEM)),
         scratch_shapes=[
             pltpu.VMEM((7, 24, 8, NX), F32),
             pltpu.VMEM((15, 12, 16, NX), F32),
             pltpu.VMEM((8, NX), F32),
-            pltpu.SemaphoreType.DMA((1,)),
         ],
         compiler_params=pltpu.CompilerParams(vmem_limit_bytes=LIMIT),
         name="sweep",
-    )(near(ga.reshape(2048, NX)), near(gb.reshape(2048, NX)), near(moved), far(starts))
+    )(near(ga.reshape(2048, NX)), near(gb.reshape(2048, NX)))
+    new = pl.pallas_call(
+        finish_kernel,
+        out_shape=shape((1, NZL) + plane, F32),
+        in_specs=[VM, VM, HBM],
+        out_specs=VM,
+        scratch_shapes=[pltpu.SemaphoreType.DMA((1,))],
+        compiler_params=pltpu.CompilerParams(vmem_limit_bytes=LIMIT),
+        name="finish",
+    )(near(wide), near(moved), far(starts))
     return new, change.reshape(())
 
 

time: 86.7 us -> 80.9 us (0.933)
  Pallas kernels: 15.1 us -> 12.2 us
  waiting for transfers between devices: 15.9 us -> 13.5 us
    ppermute x1, waiting for transfers between devices: 4.7 us -> 0.01 us  [per_device(): moved = lax.ppermute(fine, 'tm', up)]
    ppermute x1, waiting for transfers between devices: 1.46 us -> 3.57 us  [per_device(): nxt = lax.ppermute(starts[0], 'tm', down)]
    pallas_call x1, Pallas kernels: 2.25 us -> 0.97 us  [per_device(): pl.pallas_call(first_kernel, out_shape=pltpu.VMEM((6,) + plane, F32), in_...]
    pallas_call x1, Pallas kernels: 2.63 us -> 1.37 us  [per_device(): pl.pallas_call(second_kernel, out_shape=(pltpu.VMEM((NZL,) + plane, F32),...]
    pallas_call x1 -> x2, Pallas kernels: 5.2 us -> 5.64 us  [the longest x1 4.84 us: per_device(): pl.pallas_call(sweep_kernel, out_shape=(pltpu.VMEM((16, 4 * NX), F32), sh...]
  transfers between devices with their start and end apart: 7 -> 7, of which waited for: 3 -> 3; matrix products, arithmetic and copies ran while one was open for 0% -> 0% of each run, Pallas kernels for 7% -> 11%
where the time goes in v3:
time: 80.9 us; the launch traced here: 80.6 us
  blocking collectives  42.5 us (53%)
  waiting for transfers between devices  13.5 us (17%)
  Pallas kernels  12.2 us (15%)
  starting transfers between devices  11.5 us (14%)
    all_to_all x1, blocking collectives, per_device(): lax.all_to_all(jnp.broadcast_to(gz[None], (16, 8, 16, NX)), 'space', 0, 0)  27.1 us
    all_to_all x1, blocking collectives, per_device(): gz = lax.all_to_all(pay, 'tm', 0, 0, axis_index_groups=zgroups)  15.4 us
    ppermute x1, waiting for transfers between devices, per_device(): ra = lax.ppermute(pay_a, 'space', even)  9.7 us
    pallas_call x1, Pallas kernels, per_device(): pl.pallas_call(sweep_kernel, out_shape=(pltpu.VMEM((16, 4 * NX), F32), sh...  4.84 us
    ppermute x1, waiting for transfers between devices, per_device(): nxt = lax.ppermute(starts[0], 'tm', down)  3.57 us
    pallas_call x1, Pallas kernels, per_device(): pl.pallas_call(prep_kernel, out_shape=(pltpu.VMEM((7, NZL) + plane, F32),...  2.86 us
    ppermute x1, starting transfers between devices, per_device(): sa = lax.ppermute(ra, 'tm', swap)  2.48 us
    ppermute x1, starting transfers between devices, per_device(): nxt = lax.ppermute(starts[0], 'tm', down)  2.4 us
  transfers between devices with their start and end apart: 7, of which 3 were waited for; matrix products, arithmetic and copies ran while one was open for 0% of the time, Pallas kernels for 11%

profile of v3, /device:TPU:1, one launch (start us, length us, event | category | flops | bytes accessed | tf_op | source)
XLA Modules:
  0.0 80.6 jit_solution(10035235385313717235)
XLA Ops:
  0.6 1.4 %pack.1 = (f32[16,64,128]{2,1,0:T(8,128)S(1)}, f32[16,64,128]{2,1,0:T(8,128)S(1)}) custom-call(f32[1,12,64,128]{3,2,1,0:T(8,128)} %st.5, f32[12,64,128]{2,1,0:T(8,128)} %vx.3, f32[12,64,128]{2,1,0:T(8,128)} %vy.3, f32[12,64,128]{2,1,0:T(8,128)} %vz.3, f32[12,64,128]{2,1,0:T(8,128)} %ka.3), custom_call_target="tpu_custom_call" | custom-call | tf_op jit(solution)/shard_map/pack/pallas_call | solution.py:371
  2.0 2.1 %collective-permute-start.2 = (f32[16,64,128]{2,1,0:T(8,128)S(1)}, f32[16,64,128]{2,1,0:T(8,128)S(1)}, u32[]{:S(2)}, u32[]{:S(2)}) collective-permute-start(f32[16,64,128]{2,1,0:T(8,128)S(1)} %get-tuple-element.14), channel_id=1, source_target_pairs={{0,1},{1,0},{2,3},{3,2},{4,5},{5,4},{6,7},{7,6},{8,9},{9,8},{10,11... | collective-permute-start | bytes 1572872 | tf_op jit(solution)/shard_map/ppermute | solution.py:381
  4.1 0.7 collective-permute-start
  4.8 9.7 %collective-permute-done.2.own = f32[16,64,128]{2,1,0:T(8,128)S(1)} collective-permute-done((f32[16,64,128]{2,1,0:T(8,128)S(1)}, f32[16,64,128]{2,1,0:T(8,128)S(1)}, u32[]{:S(2)}, u32[]{:S(2)}) %collective-permute-start.2) | collective-permute-done | bytes 524320 | tf_op jit(solution)/shard_map/ppermute | solution.py:381
  14.5 2.5 %collective-permute-start.3 = (f32[16,64,128]{2,1,0:T(8,128)S(1)}, f32[16,64,128]{2,1,0:T(8,128)S(1)}, u32[]{:S(2)}, u32[]{:S(2)}) collective-permute-start(f32[16,64,128]{2,1,0:T(8,128)S(1)} %collective-permute-done.2.own), channel_id=1, source_target_pairs={{0,16},{16,0},{32,48},{48,32},{64,80},{80,64},{96,112},{112,96},{1... | collective-permute-start | bytes 1572872 | tf_op jit(solution)/shard_map/ppermute | solution.py:402
  17.0 0.0 collective-permute-done.own
  17.0 0.0 collective-permute-start.1
  17.0 2.4 %collective-permute-start.4 = (f32[12,64,128]{2,1,0:T(8,128)}, f32[12,64,128]{2,1,0:T(8,128)S(1)}, u32[]{:S(2)}, u32[]{:S(2)}) collective-permute-start(f32[12,64,128]{2,1,0:T(8,128)} %bitcast.6), channel_id=1, source_target_pairs={{16,0},{32,16},{48,32},{64,48},{80,64},{96,80},{112,96},{128,112},... | collective-permute-start | bytes 1179656 | tf_op jit(solution)/shard_map/ppermute | solution.py:382
  19.4 2.9 %prep.1 = (f32[7,12,64,128]{3,2,1,0:T(8,128)S(1)}, f32[6,12,64,128]{3,2,1,0:T(8,128)S(1)}, f32[8,128]{1,0:T(8,128)S(1)}) custom-call(f32[1,12,64,128]{3,2,1,0:T(8,128)} %st.5, f32[12,64,128]{2,1,0:T(8,128)} %vx.3, f32[12,64,128]{2,1,0:T(8,128)} %vy.3, f32[12,64,128]{2,1,0:T(8,128)} %vz.3, f32[12,64,128]{2,1,0:T(8,128)} %ka.3), custom_call_target="tpu_custom_call" | custom-call | tf_op jit(solution)/shard_map/prep/pallas_call | solution.py:383
  22.3 0.0 collective-permute-done.3.other
  22.3 1.0 %first.1.half = f32[6,64,128]{2,1,0:T(8,128)S(1)} custom-call(f32[16,64,128]{2,1,0:T(8,128)S(1)} %collective-permute-done.2.own, f32[16,64,128]{2,1,0:T(8,128)S(1)} %collective-permute-done.3.other, f32[7,12,64,128]{3,2,1,0:T(8,128)S(1)} %get-tuple-element.12.w, f32[6,12,64,128]{3,2,1,0:T(8,128)S(1)} %get-tuple-element.13.lev), custom_call_target="tpu_custom_call" | custom-call | tf_op jit(solution)/shard_map/first/pallas_call | solution.py:403
  23.3 3.6 %collective-permute-done.4.nx = f32[12,64,128]{2,1,0:T(8,128)S(1)} collective-permute-done((f32[12,64,128]{2,1,0:T(8,128)}, f32[12,64,128]{2,1,0:T(8,128)S(1)}, u32[]{:S(2)}, u32[]{:S(2)}) %collective-permute-start.4) | collective-permute-done | bytes 393248 | tf_op jit(solution)/shard_map/ppermute | solution.py:382
  26.8 0.0 collective-permute-done.1.other
  26.8 1.4 %second.1 = (f32[12,64,128]{2,1,0:T(8,128)S(1)}, f32[8,16,128]{2,1,0:T(8,128)S(1)}) custom-call(f32[16,64,128]{2,1,0:T(8,128)S(1)} %collective-permute-done.own, f32[16,64,128]{2,1,0:T(8,128)S(1)} %collective-permute-done.1.other, f32[7,12,64,128]{3,2,1,0:T(8,128)S(1)} %get-tuple-element.12.w, f32[6,12,64,128]{3,2,1,0:T(8,128)S(1)} %get-tuple-element.13.lev, ...), custom_call_target="tpu_custom_call" | custom-call | tf_op jit(solution)/shard_map/second/pallas_call | solution.py:413
  28.2 15.4 %all_to_all.10 = f32[8,16,128]{2,1,0:T(8,128)S(1)} all-to-all(f32[8,16,128]{2,1,0:T(8,128)S(1)} %get-tuple-element.16), channel_id=1, replica_groups={{0,32,64,96,128,160,192,224},{16,48,80,112,144,176,208,240},{1,33,65,97..., dimensions={0} | all-to-all | bytes 131072 | tf_op jit(solution)/shard_map/all_to_all | solution.py:423
  43.6 0.1 broadcast_in_dim.2
  43.7 27.1 %all_to_all.11 = f32[16,8,16,128]{3,2,1,0:T(8,128)S(1)} all-to-all(f32[16,8,16,128]{3,2,1,0:T(8,128)S(1)} %broadcast_in_dim.2), channel_id=1, replica_groups=mesh['tm'=16,'space'=16] {'space'}, dimensions={0} | all-to-all | bytes 2097152 | tf_op jit(solution)/shard_map/all_to_all | solution.py:425
  70.8 1.8 %collective-permute-start.5 = (f32[16,8,16,128]{3,2,1,0:T(8,128)S(1)}, f32[16,8,16,128]{3,2,1,0:T(8,128)S(1)}, u32[]{:S(2)}, u32[]{:S(2)}) collective-permute-start(f32[16,8,16,128]{3,2,1,0:T(8,128)S(1)} %all_to_all.11), channel_id=1, source_target_pairs={{0,16},{16,0},{32,48},{48,32},{64,80},{80,64},{96,112},{112,96},{1... | collective-permute-start | bytes 3145736 | tf_op jit(solution)/shard_map/ppermute | solution.py:426
  72.6 2.0 %collective-permute-start.6 = (f32[12,64,128]{2,1,0:T(8,128)S(1)}, f32[12,64,128]{2,1,0:T(8,128)S(1)}, u32[]{:S(2)}, u32[]{:S(2)}) collective-permute-start(f32[12,64,128]{2,1,0:T(8,128)S(1)} %get-tuple-element.18), channel_id=1, source_target_pairs={{0,16},{16,32},{32,48},{48,64},{64,80},{80,96},{96,112},{112,128},... | collective-permute-start | bytes 1179656 | tf_op jit(solution)/shard_map/ppermute | solution.py:424
  74.7 0.3 collective-permute-done.5
  74.9 4.8 %sweep.1 = (f32[16,512]{1,0:T(8,128)S(1)}, f32[1,1]{1,0:T(1,128)}) custom-call(f32[2048,128]{1,0:T(8,128)S(1)} %bitcast.4, f32[2048,128]{1,0:T(8,128)S(1)} %bitcast.5), custom_call_target="tpu_custom_call" | custom-call | tf_op jit(solution)/shard_map/sweep/pallas_call | solution.py:428
  79.8 0.0 collective-permute-done.6.fine
  79.8 0.8 finish.1
Async XLA Ops:
  2.0 12.5 %collective-permute-start.2 = (f32[16,64,128]{2,1,0:T(8,128)S(1)}, f32[16,64,128]{2,1,0:T(8,128)S(1)}, u32[]{:S(2)}, u32[]{:S(2)}) collective-permute-start(f32[16,64,128]{2,1,0:T(8,128)S(1)} %get-tuple-element.14), channel_id=1, source_target_pairs={{0,1},{1,0},{2,3},{3,2},{4,5},{5,4},{6,7},{7,6},{8,9},{9,8},{10,11... | collective-permute-start | bytes 1572872 | tf_op jit(solution)/shard_map/ppermute | solution.py:381
  4.1 12.9 %collective-permute-start = (f32[16,64,128]{2,1,0:T(8,128)S(1)}, f32[16,64,128]{2,1,0:T(8,128)S(1)}, u32[]{:S(2)}, u32[]{:S(2)}) collective-permute-start(f32[16,64,128]{2,1,0:T(8,128)S(1)} %get-tuple-element.11), channel_id=1, source_target_pairs={{1,2},{3,4},{5,6},{7,8},{9,10},{11,12},{13,14},{2,1},{4,3},{6,5},{... | collective-permute-start | bytes 1572872 | tf_op jit(solution)/shard_map/ppermute | solution.py:380
  14.5 7.8 %collective-permute-start.3 = (f32[16,64,128]{2,1,0:T(8,128)S(1)}, f32[16,64,128]{2,1,0:T(8,128)S(1)}, u32[]{:S(2)}, u32[]{:S(2)}) collective-permute-start(f32[16,64,128]{2,1,0:T(8,128)S(1)} %collective-permute-done.2.own), channel_id=1, source_target_pairs={{0,16},{16,0},{32,48},{48,32},{64,80},{80,64},{96,112},{112,96},{1... | collective-permute-start | bytes 1572872 | tf_op jit(solution)/shard_map/ppermute | solution.py:402
  17.0 9.8 %collective-permute-start.1 = (f32[16,64,128]{2,1,0:T(8,128)S(1)}, f32[16,64,128]{2,1,0:T(8,128)S(1)}, u32[]{:S(2)}, u32[]{:S(2)}) collective-permute-start(f32[16,64,128]{2,1,0:T(8,128)S(1)} %collective-permute-done.own), channel_id=1, source_target_pairs={{0,16},{16,0},{32,48},{48,32},{64,80},{80,64},{96,112},{112,96},{1... | collective-permute-start | bytes 1572872 | tf_op jit(solution)/shard_map/ppermute | solution.py:412
  17.0 9.8 %collective-permute-start.4 = (f32[12,64,128]{2,1,0:T(8,128)}, f32[12,64,128]{2,1,0:T(8,128)S(1)}, u32[]{:S(2)}, u32[]{:S(2)}) collective-permute-start(f32[12,64,128]{2,1,0:T(8,128)} %bitcast.6), channel_id=1, source_target_pairs={{16,0},{32,16},{48,32},{64,48},{80,64},{96,80},{112,96},{128,112},... | collective-permute-start | bytes 1179656 | tf_op jit(solution)/shard_map/ppermute | solution.py:382
  70.8 4.1 %collective-permute-start.5 = (f32[16,8,16,128]{3,2,1,0:T(8,128)S(1)}, f32[16,8,16,128]{3,2,1,0:T(8,128)S(1)}, u32[]{:S(2)}, u32[]{:S(2)}) collective-permute-start(f32[16,8,16,128]{3,2,1,0:T(8,128)S(1)} %all_to_all.11), channel_id=1, source_target_pairs={{0,16},{16,0},{32,48},{48,32},{64,80},{80,64},{96,112},{112,96},{1... | collective-permute-start | bytes 3145736 | tf_op jit(solution)/shard_map/ppermute | solution.py:426
  72.6 7.1 %collective-permute-start.6 = (f32[12,64,128]{2,1,0:T(8,128)S(1)}, f32[12,64,128]{2,1,0:T(8,128)S(1)}, u32[]{:S(2)}, u32[]{:S(2)}) collective-permute-start(f32[12,64,128]{2,1,0:T(8,128)S(1)} %get-tuple-element.18), channel_id=1, source_target_pairs={{0,16},{16,32},{32,48},{48,64},{64,80},{80,96},{96,112},{112,128},... | collective-permute-start | bytes 1179656 | tf_op jit(solution)/shard_map/ppermute | solution.py:424

commit v4 on v3

--- a/solution.py
+++ b/solution.py
@@ -36,7 +36,7 @@
         c.wait()
 
 
-def pack_kernel(st, vx, vy, vz, ka, pa, pb, sem):
+def pack_kernel(st, vx, vy, vz, ka, ca, cb, ha, hb, sem):
     core = lax.rem(lax.axis_index("tm"), 2)
     odd = lax.rem(lax.axis_index("space"), 2)
     au, ac = 6 * (1 - odd), 7 * (1 - odd)
@@ -44,12 +44,12 @@
 
     def go(f0, f1):
         pairs = [
-            (st.at[0, pl.ds(au, 6)], pa.at[0:6]),
-            (f0.at[pl.ds(ac, 5)], pa.at[6:11]),
-            (f1.at[pl.ds(ac, 5)], pa.at[11:16]),
-            (st.at[0, pl.ds(bu, 6)], pb.at[0:6]),
-            (f0.at[pl.ds(bc, 5)], pb.at[6:11]),
-            (f1.at[pl.ds(bc, 5)], pb.at[11:16]),
+            (f0.at[pl.ds(ac, 5)], ca.at[0:5]),
+            (f1.at[pl.ds(ac, 5)], ca.at[5:10]),
+            (f0.at[pl.ds(bc, 5)], cb.at[0:5]),
+            (f1.at[pl.ds(bc, 5)], cb.at[5:10]),
+            (st.at[0, pl.ds(au, 6)], ha),
+            (st.at[0, pl.ds(bu, 6)], hb),
         ]
         run_all([pltpu.make_async_copy(a, b, sem.at[i]) for i, (a, b) in enumerate(pairs)])
 
@@ -139,7 +139,7 @@
         part[zl : zl + 1, :] = ck[pl.ds(16 * zl + 4 * lax.rem(n, 4), 1), :]
 
 
-def wedge(hi, own, other, w, lev, put, u, wk):
+def wedge(hi, edge, own, other, w, lev, put, u, wk):
     first = lax.rem(lax.axis_index("tm"), 2) == 0
     sign = (1 - 2 * hi).astype(F32)
 
@@ -148,7 +148,7 @@
 
     def halo(k, _):
         j = (k - 1) + hi * (6 - 2 * k)
-        a0, a1, b0, b1 = own[6 + j], own[11 + j], other[6 + j], other[11 + j]
+        a0, a1, b0, b1 = own[j], own[5 + j], other[j], other[5 + j]
         put_weights(
             wk,
             k,
@@ -170,7 +170,7 @@
     lax.fori_loop(1, 6, halo, 0, unroll=5)
     lax.fori_loop(6, 12, center, 0, unroll=3)
     for k in range(6):
-        u[0, k] = own[k + hi * (5 - 2 * k)]
+        u[0, k] = edge[k + hi * (5 - 2 * k)]
 
     for t in range(1, FSTEPS + 1):
         a, b = (t - 1) % 2, t % 2
@@ -189,21 +189,21 @@
     return slab
 
 
-def first_kernel(own, other, w, lev, half, u, wk):
+def first_kernel(edge, own, other, w, lev, half, u, wk):
     def put(k, q, new):
         half[k - 6] = new
 
-    wedge(1 - lax.rem(lax.axis_index("space"), 2), own, other, w, lev, put, u, wk)
-
-
-def second_kernel(own, other, w, lev, half, part, nx, fine, pay, u, wk, rows, ck):
+    wedge(1 - lax.rem(lax.axis_index("space"), 2), edge, own, other, w, lev, put, u, wk)
+
+
+def second_kernel(edge, own, other, w, lev, half, part, nx, fine, pay, u, wk, rows, ck):
     n = lax.axis_index("tm")
     hi = lax.rem(lax.axis_index("space"), 2)
 
     def put(k, q, new):
         fine[q] = new
 
-    wedge(hi, own, other, w, lev, put, u, wk)
+    wedge(hi, edge, own, other, w, lev, put, u, wk)
     for i in range(6):
         fine[i * (2 * hi - 1) + 11 * (1 - hi)] = half[i]
 
@@ -313,7 +313,7 @@
         e, acc = turn(odd, z, 2 * z + 1, *carry)
         return turn(even, z + 1, 2 * z + 2, e, acc)
 
-    e, acc = lax.fori_loop(0, 7, two, (e, acc))
+    e, acc = lax.fori_loop(0, 7, two, (e, acc), unroll=7)
 
     part = jnp.zeros((8, NX), F32)
     for ref in (even, odd):
@@ -368,17 +368,19 @@
     up = [(i, i + 1) for i in range(SL - 1)]
     zgroups = [[c + 2 * z for z in range(8)] for c in range(2)]
 
-    pay_a, pay_b = pl.pallas_call(
+    ca, cb, ha, hb = pl.pallas_call(
         pack_kernel,
-        out_shape=(pltpu.VMEM((16,) + plane, F32),) * 2,
+        out_shape=(pltpu.VMEM((10,) + plane, F32),) * 2 + (pltpu.VMEM((6,) + plane, F32),) * 2,
         in_specs=[HBM] * 5,
-        out_specs=(VM, VM),
+        out_specs=(VM,) * 4,
         scratch_shapes=[pltpu.SemaphoreType.DMA((6,))],
         compiler_params=pltpu.CompilerParams(vmem_limit_bytes=LIMIT),
         name="pack",
     )(*(far(x) for x in (starts, vel_x, vel_y, vel_z, kappa)))
-    rb = lax.ppermute(pay_b, "space", odd)
-    ra = lax.ppermute(pay_a, "space", even)
+    ca = lax.ppermute(ca, "space", even)
+    cb = lax.ppermute(cb, "space", odd)
+    ha = lax.ppermute(ha, "space", even)
+    hb = lax.ppermute(hb, "space", odd)
     nxt = lax.ppermute(starts[0], "tm", down)
     w, lev, part = pl.pallas_call(
         prep_kernel,
@@ -399,26 +401,26 @@
         name="prep",
     )(*(far(x) for x in (starts, vel_x, vel_y, vel_z, kappa)))
     work = [pltpu.VMEM((2, 13) + plane, F32), pltpu.VMEM((7, 12) + plane, F32)]
-    sa = lax.ppermute(ra, "tm", swap)
+    sa = lax.ppermute(ca, "tm", swap)
     half = pl.pallas_call(
         first_kernel,
         out_shape=pltpu.VMEM((6,) + plane, F32),
-        in_specs=[VM] * 4,
+        in_specs=[VM] * 5,
         out_specs=VM,
         scratch_shapes=work,
         compiler_params=pltpu.CompilerParams(vmem_limit_bytes=LIMIT),
         name="first",
-    )(near(ra), near(sa), near(w), near(lev))
-    sb = lax.ppermute(rb, "tm", swap)
+    )(near(ha), near(ca), near(sa), near(w), near(lev))
+    sb = lax.ppermute(cb, "tm", swap)
     fine, pay = pl.pallas_call(
         second_kernel,
         out_shape=(pltpu.VMEM((NZL,) + plane, F32), pltpu.VMEM((8, 16, NX), F32)),
-        in_specs=[VM] * 7,
+        in_specs=[VM] * 8,
         out_specs=(VM, VM),
         scratch_shapes=work + [pltpu.VMEM((48, NX), F32), pltpu.VMEM((48, NX), F32)],
         compiler_params=pltpu.CompilerParams(vmem_limit_bytes=LIMIT),
         name="second",
-    )(near(rb), near(sb), near(w), near(lev), near(half), near(part), near(nxt))
+    )(near(hb), near(cb), near(sb), near(w), near(lev), near(half), near(part), near(nxt))
 
     gz = lax.all_to_all(pay, "tm", 0, 0, axis_index_groups=zgroups)
     moved = lax.ppermute(fine, "tm", up)

time: 80.9 us -> 77.3 us (0.956)
  waiting for transfers between devices: 13.5 us -> 5.02 us
  starting transfers between devices: 11.5 us -> 18.4 us
  blocking collectives: 42.5 us -> 41.4 us
  Pallas kernels: 12.2 us -> 11.2 us
    ppermute x4 -> x6, waiting for transfers between devices: 9.71 us -> 4.15 us  [the longest x1 2.4 us: per_device(): ca = lax.ppermute(ca, 'space', even)]
    ppermute x4 -> x6, starting transfers between devices: 5.29 us -> 9.94 us  [the longest x1 4.01 us: per_device(): ha = lax.ppermute(ha, 'space', even)]
    ppermute x1, waiting for transfers between devices: 3.57 us -> 0.01 us  [per_device(): nxt = lax.ppermute(starts[0], 'tm', down)]
    ppermute x1, starting transfers between devices: 1.78 us -> 3.25 us  [per_device(): gb = lax.ppermute(ga, 'tm', swap)]
    pallas_call x1, Pallas kernels: 4.84 us -> 3.82 us  [per_device(): pl.pallas_call(sweep_kernel, out_shape=(pltpu.VMEM((16, 4 * NX), F32), sh...]
    all_to_all x1, blocking collectives: 27.1 us -> 26.1 us  [per_device(): lax.all_to_all(jnp.broadcast_to(gz[None], (16, 8, 16, NX)), 'space', 0, 0)]
  transfers between devices with their start and end apart: 7 -> 9, of which waited for: 3 -> 4; matrix products, arithmetic and copies ran while one was open for 0% -> 0% of each run, Pallas kernels for 11% -> 10%
where the time goes in v4:
time: 77.3 us; the launch traced here: 77 us
  blocking collectives  41.4 us (54%)
  starting transfers between devices  18.4 us (24%)
  Pallas kernels  11.2 us (14%)
  waiting for transfers between devices  5.02 us (6%)
  between operations  0.9 us (1%)
    all_to_all x1, blocking collectives, per_device(): lax.all_to_all(jnp.broadcast_to(gz[None], (16, 8, 16, NX)), 'space', 0, 0)  26.1 us
    all_to_all x1, blocking collectives, per_device(): gz = lax.all_to_all(pay, 'tm', 0, 0, axis_index_groups=zgroups)  15.3 us
    ppermute x1, starting transfers between devices, per_device(): ha = lax.ppermute(ha, 'space', even)  4.01 us
    pallas_call x1, Pallas kernels, per_device(): pl.pallas_call(sweep_kernel, out_shape=(pltpu.VMEM((16, 4 * NX), F32), sh...  3.82 us
    ppermute x1, starting transfers between devices, per_device(): gb = lax.ppermute(ga, 'tm', swap)  3.25 us
    ppermute x1, starting transfers between devices, per_device(): nxt = lax.ppermute(starts[0], 'tm', down)  3.1 us
    pallas_call x1, Pallas kernels, per_device(): pl.pallas_call(prep_kernel, out_shape=(pltpu.VMEM((7, NZL) + plane, F32),...  2.86 us
    ppermute x1, starting transfers between devices, per_device(): sa = lax.ppermute(ca, 'tm', swap)  2.48 us
  transfers between devices with their start and end apart: 9, of which 4 were waited for; matrix products, arithmetic and copies ran while one was open for 0% of the time, Pallas kernels for 10%

profile of v4, /device:TPU:1, one launch (start us, length us, event | category | flops | bytes accessed | tf_op | source)
XLA Modules:
  0.0 77.0 jit_solution(8825918001356626919)
XLA Ops:
  0.6 1.4 %pack.1 = (f32[10,64,128]{2,1,0:T(8,128)S(1)}, f32[10,64,128]{2,1,0:T(8,128)S(1)}, f32[6,64,128]{2,1,0:T(8,128)S(1)}, f32[6,64,128]{2,1,0:T(8,128)S(1)}) custom-call(f32[1,12,64,128]{3,2,1,0:T(8,128)} %st.5, f32[12,64,128]{2,1,0:T(8,128)} %vx.3, f32[12,64,128]{2,1,0:T(8,128)} %vy.3, f32[12,64,128]{2,1,0:T(8,128)} %vz.3, f32[12,64,128]{2,1,0:T(8,128)} %ka.3), custom_call_target="tpu_custom_call" | custom-call | tf_op jit(solution)/shard_map/pack/pallas_call | solution.py:371
  2.0 2.1 %collective-permute-start.4 = (f32[10,64,128]{2,1,0:T(8,128)S(1)}, f32[10,64,128]{2,1,0:T(8,128)S(1)}, u32[]{:S(2)}, u32[]{:S(2)}) collective-permute-start(f32[10,64,128]{2,1,0:T(8,128)S(1)} %get-tuple-element.18), channel_id=1, source_target_pairs={{0,1},{1,0},{2,3},{3,2},{4,5},{5,4},{6,7},{7,6},{8,9},{9,8},{10,11... | collective-permute-start | bytes 983048 | tf_op jit(solution)/shard_map/ppermute | solution.py:380
  4.1 0.7 collective-permute-start.1
  4.8 3.1 %collective-permute-start.6 = (f32[12,64,128]{2,1,0:T(8,128)}, f32[12,64,128]{2,1,0:T(8,128)S(1)}, u32[]{:S(2)}, u32[]{:S(2)}) collective-permute-start(f32[12,64,128]{2,1,0:T(8,128)} %bitcast.6), channel_id=1, source_target_pairs={{16,0},{32,16},{48,32},{64,48},{80,64},{96,80},{112,96},{128,112},... | collective-permute-start | bytes 1179656 | tf_op jit(solution)/shard_map/ppermute | solution.py:384
  7.9 2.4 %collective-permute-done.4.own = f32[10,64,128]{2,1,0:T(8,128)S(1)} collective-permute-done((f32[10,64,128]{2,1,0:T(8,128)S(1)}, f32[10,64,128]{2,1,0:T(8,128)S(1)}, u32[]{:S(2)}, u32[]{:S(2)}) %collective-permute-start.4) | collective-permute-done | bytes 327712 | tf_op jit(solution)/shard_map/ppermute | solution.py:380
  10.3 2.5 %collective-permute-start.5 = (f32[10,64,128]{2,1,0:T(8,128)S(1)}, f32[10,64,128]{2,1,0:T(8,128)S(1)}, u32[]{:S(2)}, u32[]{:S(2)}) collective-permute-start(f32[10,64,128]{2,1,0:T(8,128)S(1)} %collective-permute-done.4.own), channel_id=1, source_target_pairs={{0,16},{16,0},{32,48},{48,32},{64,80},{80,64},{96,112},{112,96},{1... | collective-permute-start | bytes 983048 | tf_op jit(solution)/shard_map/ppermute | solution.py:404
  12.8 0.0 collective-permute-done.1.own
  12.8 0.0 collective-permute-start.2
  12.8 4.0 %collective-permute-start.3 = (f32[6,64,128]{2,1,0:T(8,128)S(1)}, f32[6,64,128]{2,1,0:T(8,128)S(1)}, u32[]{:S(2)}, u32[]{:S(2)}) collective-permute-start(f32[6,64,128]{2,1,0:T(8,128)S(1)} %get-tuple-element.17), channel_id=1, source_target_pairs={{0,1},{1,0},{2,3},{3,2},{4,5},{5,4},{6,7},{7,6},{8,9},{9,8},{10,11... | collective-permute-start | bytes 589832 | tf_op jit(solution)/shard_map/ppermute | solution.py:382
  16.8 0.7 collective-permute-start
  17.5 2.9 %prep.1 = (f32[7,12,64,128]{3,2,1,0:T(8,128)S(1)}, f32[6,12,64,128]{3,2,1,0:T(8,128)S(1)}, f32[8,128]{1,0:T(8,128)S(1)}) custom-call(f32[1,12,64,128]{3,2,1,0:T(8,128)} %st.5, f32[12,64,128]{2,1,0:T(8,128)} %vx.3, f32[12,64,128]{2,1,0:T(8,128)} %vy.3, f32[12,64,128]{2,1,0:T(8,128)} %vz.3, f32[12,64,128]{2,1,0:T(8,128)} %ka.3), custom_call_target="tpu_custom_call" | custom-call | tf_op jit(solution)/shard_map/prep/pallas_call | solution.py:385
  20.4 1.7 %collective-permute-done.3.edge = f32[6,64,128]{2,1,0:T(8,128)S(1)} collective-permute-done((f32[6,64,128]{2,1,0:T(8,128)S(1)}, f32[6,64,128]{2,1,0:T(8,128)S(1)}, u32[]{:S(2)}, u32[]{:S(2)}) %collective-permute-start.3) | collective-permute-done | bytes 196640 | tf_op jit(solution)/shard_map/ppermute | solution.py:382
  22.1 0.0 collective-permute-done.5.other
  22.1 1.0 %first.1.half = f32[6,64,128]{2,1,0:T(8,128)S(1)} custom-call(f32[6,64,128]{2,1,0:T(8,128)S(1)} %collective-permute-done.3.edge, f32[10,64,128]{2,1,0:T(8,128)S(1)} %collective-permute-done.4.own, f32[10,64,128]{2,1,0:T(8,128)S(1)} %collective-permute-done.5.other, f32[7,12,64,128]{3,2,1,0:T(8,128)S(1)} %get-tuple-element.15.w, ...), custom_call_target="tpu_custom_call" | custom-call | tf_op jit(solution)/shard_map/first/pallas_call | solution.py:405
  23.1 0.0 collective-permute-done.edge
  23.1 0.0 collective-permute-done.6.nx
  23.1 0.0 collective-permute-done.2.other
  23.1 1.4 %second.1 = (f32[12,64,128]{2,1,0:T(8,128)S(1)}, f32[8,16,128]{2,1,0:T(8,128)S(1)}) custom-call(f32[6,64,128]{2,1,0:T(8,128)S(1)} %collective-permute-done.edge, f32[10,64,128]{2,1,0:T(8,128)S(1)} %collective-permute-done.1.own, f32[10,64,128]{2,1,0:T(8,128)S(1)} %collective-permute-done.2.other, f32[7,12,64,128]{3,2,1,0:T(8,128)S(1)} %get-tuple-element.15.w, ...), custom_call_target="tpu_custom_call" | custom-call | tf_op jit(solution)/shard_map/second/pallas_call | solution.py:415
  24.5 15.3 %all_to_all.10 = f32[8,16,128]{2,1,0:T(8,128)S(1)} all-to-all(f32[8,16,128]{2,1,0:T(8,128)S(1)} %get-tuple-element.20), channel_id=1, replica_groups={{0,32,64,96,128,160,192,224},{16,48,80,112,144,176,208,240},{1,33,65,97..., dimensions={0} | all-to-all | bytes 131072 | tf_op jit(solution)/shard_map/all_to_all | solution.py:425
  39.8 0.1 broadcast_in_dim.2
  39.9 26.1 %all_to_all.11 = f32[16,8,16,128]{3,2,1,0:T(8,128)S(1)} all-to-all(f32[16,8,16,128]{3,2,1,0:T(8,128)S(1)} %broadcast_in_dim.2), channel_id=1, replica_groups=mesh['tm'=16,'space'=16] {'space'}, dimensions={0} | all-to-all | bytes 2097152 | tf_op jit(solution)/shard_map/all_to_all | solution.py:427
  66.0 3.3 %collective-permute-start.7 = (f32[16,8,16,128]{3,2,1,0:T(8,128)S(1)}, f32[16,8,16,128]{3,2,1,0:T(8,128)S(1)}, u32[]{:S(2)}, u32[]{:S(2)}) collective-permute-start(f32[16,8,16,128]{3,2,1,0:T(8,128)S(1)} %all_to_all.11), channel_id=1, source_target_pairs={{0,16},{16,0},{32,48},{48,32},{64,80},{80,64},{96,112},{112,96},{1... | collective-permute-start | bytes 3145736 | tf_op jit(solution)/shard_map/ppermute | solution.py:428
  69.3 2.1 %collective-permute-start.8 = (f32[12,64,128]{2,1,0:T(8,128)S(1)}, f32[12,64,128]{2,1,0:T(8,128)S(1)}, u32[]{:S(2)}, u32[]{:S(2)}) collective-permute-start(f32[12,64,128]{2,1,0:T(8,128)S(1)} %get-tuple-element.22), channel_id=1, source_target_pairs={{0,16},{16,32},{32,48},{48,64},{64,80},{80,96},{96,112},{112,128},... | collective-permute-start | bytes 1179656 | tf_op jit(solution)/shard_map/ppermute | solution.py:426
  71.4 0.2 collective-permute-done.7
  71.6 3.8 %sweep.1 = (f32[16,512]{1,0:T(8,128)S(1)}, f32[1,1]{1,0:T(1,128)}) custom-call(f32[2048,128]{1,0:T(8,128)S(1)} %bitcast.4, f32[2048,128]{1,0:T(8,128)S(1)} %bitcast.5), custom_call_target="tpu_custom_call" | custom-call | tf_op jit(solution)/shard_map/sweep/pallas_call | solution.py:430
  75.4 0.7 collective-permute-done.8.fine
  76.1 0.8 %finish.1 = f32[1,12,64,128]{3,2,1,0:T(8,128)} custom-call(f32[16,512]{1,0:T(8,128)S(1)} %get-tuple-element.21.wide, f32[12,64,128]{2,1,0:T(8,128)S(1)} %collective-permute-done.8.fine, f32[1,12,64,128]{3,2,1,0:T(8,128)} %st.5), custom_call_target="tpu_custom_call" | custom-call | tf_op jit(solution)/shard_map/finish/pallas_call | solution.py:443
Async XLA Ops:
  2.0 8.3 %collective-permute-start.4 = (f32[10,64,128]{2,1,0:T(8,128)S(1)}, f32[10,64,128]{2,1,0:T(8,128)S(1)}, u32[]{:S(2)}, u32[]{:S(2)}) collective-permute-start(f32[10,64,128]{2,1,0:T(8,128)S(1)} %get-tuple-element.18), channel_id=1, source_target_pairs={{0,1},{1,0},{2,3},{3,2},{4,5},{5,4},{6,7},{7,6},{8,9},{9,8},{10,11... | collective-permute-start | bytes 983048 | tf_op jit(solution)/shard_map/ppermute | solution.py:380
  4.1 8.7 %collective-permute-start.1 = (f32[10,64,128]{2,1,0:T(8,128)S(1)}, f32[10,64,128]{2,1,0:T(8,128)S(1)}, u32[]{:S(2)}, u32[]{:S(2)}) collective-permute-start(f32[10,64,128]{2,1,0:T(8,128)S(1)} %get-tuple-element.14), channel_id=1, source_target_pairs={{1,2},{3,4},{5,6},{7,8},{9,10},{11,12},{13,14},{2,1},{4,3},{6,5},{... | collective-permute-start | bytes 983048 | tf_op jit(solution)/shard_map/ppermute | solution.py:381
  4.8 18.3 %collective-permute-start.6 = (f32[12,64,128]{2,1,0:T(8,128)}, f32[12,64,128]{2,1,0:T(8,128)S(1)}, u32[]{:S(2)}, u32[]{:S(2)}) collective-permute-start(f32[12,64,128]{2,1,0:T(8,128)} %bitcast.6), channel_id=1, source_target_pairs={{16,0},{32,16},{48,32},{64,48},{80,64},{96,80},{112,96},{128,112},... | collective-permute-start | bytes 1179656 | tf_op jit(solution)/shard_map/ppermute | solution.py:384
  10.3 11.8 %collective-permute-start.5 = (f32[10,64,128]{2,1,0:T(8,128)S(1)}, f32[10,64,128]{2,1,0:T(8,128)S(1)}, u32[]{:S(2)}, u32[]{:S(2)}) collective-permute-start(f32[10,64,128]{2,1,0:T(8,128)S(1)} %collective-permute-done.4.own), channel_id=1, source_target_pairs={{0,16},{16,0},{32,48},{48,32},{64,80},{80,64},{96,112},{112,96},{1... | collective-permute-start | bytes 983048 | tf_op jit(solution)/shard_map/ppermute | solution.py:404
  12.8 10.3 %collective-permute-start.2 = (f32[10,64,128]{2,1,0:T(8,128)S(1)}, f32[10,64,128]{2,1,0:T(8,128)S(1)}, u32[]{:S(2)}, u32[]{:S(2)}) collective-permute-start(f32[10,64,128]{2,1,0:T(8,128)S(1)} %collective-permute-done.1.own), channel_id=1, source_target_pairs={{0,16},{16,0},{32,48},{48,32},{64,80},{80,64},{96,112},{112,96},{1... | collective-permute-start | bytes 983048 | tf_op jit(solution)/shard_map/ppermute | solution.py:414
  12.8 9.3 %collective-permute-start.3 = (f32[6,64,128]{2,1,0:T(8,128)S(1)}, f32[6,64,128]{2,1,0:T(8,128)S(1)}, u32[]{:S(2)}, u32[]{:S(2)}) collective-permute-start(f32[6,64,128]{2,1,0:T(8,128)S(1)} %get-tuple-element.17), channel_id=1, source_target_pairs={{0,1},{1,0},{2,3},{3,2},{4,5},{5,4},{6,7},{7,6},{8,9},{9,8},{10,11... | collective-permute-start | bytes 589832 | tf_op jit(solution)/shard_map/ppermute | solution.py:382
  16.8 6.2 %collective-permute-start = (f32[6,64,128]{2,1,0:T(8,128)S(1)}, f32[6,64,128]{2,1,0:T(8,128)S(1)}, u32[]{:S(2)}, u32[]{:S(2)}) collective-permute-start(f32[6,64,128]{2,1,0:T(8,128)S(1)} %get-tuple-element.13), channel_id=1, source_target_pairs={{1,2},{3,4},{5,6},{7,8},{9,10},{11,12},{13,14},{2,1},{4,3},{6,5},{... | collective-permute-start | bytes 589832 | tf_op jit(solution)/shard_map/ppermute | solution.py:383
  66.0 5.5 %collective-permute-start.7 = (f32[16,8,16,128]{3,2,1,0:T(8,128)S(1)}, f32[16,8,16,128]{3,2,1,0:T(8,128)S(1)}, u32[]{:S(2)}, u32[]{:S(2)}) collective-permute-start(f32[16,8,16,128]{3,2,1,0:T(8,128)S(1)} %all_to_all.11), channel_id=1, source_target_pairs={{0,16},{16,0},{32,48},{48,32},{64,80},{80,64},{96,112},{112,96},{1... | collective-permute-start | bytes 3145736 | tf_op jit(solution)/shard_map/ppermute | solution.py:428
  69.3 6.8 %collective-permute-start.8 = (f32[12,64,128]{2,1,0:T(8,128)S(1)}, f32[12,64,128]{2,1,0:T(8,128)S(1)}, u32[]{:S(2)}, u32[]{:S(2)}) collective-permute-start(f32[12,64,128]{2,1,0:T(8,128)S(1)} %get-tuple-element.22), channel_id=1, source_target_pairs={{0,16},{16,32},{32,48},{48,64},{64,80},{80,96},{96,112},{112,128},... | collective-permute-start | bytes 1179656 | tf_op jit(solution)/shard_map/ppermute | solution.py:426

commit v5 on v4

--- a/solution.py
+++ b/solution.py
@@ -226,8 +226,11 @@
         pay[z] = pay[0]
 
 
-def sweep_kernel(ga, gb, wide, change, w, gs, accs):
-    core = lax.rem(lax.axis_index("tm"), 2)
+def sweep_kernel(ga, gb, st, wide, change, kept, w, gs, accs, sem):
+    nd = lax.axis_index("tm")
+    core = lax.rem(nd, 2)
+    keep = pltpu.make_async_copy(st.at[0], kept, sem.at[0])
+    keep.start()
 
     @pl.when(core == 0)
     def _():
@@ -238,6 +241,7 @@
         sweep(gb, ga, w, gs, accs)
 
     summary(wide, change, gs, accs)
+    keep.wait()
 
 
 def sweep(even, odd, w, gs, accs):
@@ -336,13 +340,14 @@
     wide[...] = jnp.dot(g12, spread, precision=lax.Precision.HIGHEST, preferred_element_type=F32)
 
 
-def finish_kernel(wide, fine, st, out, sem):
+def finish_kernel(wide, fine, kept, out):
     nd = lax.axis_index("tm")
     row = lax.broadcasted_iota(jnp.int32, (8, NX), 0)
 
     @pl.when(nd == 0)
     def _():
-        run_all([pltpu.make_async_copy(st.at[0], out.at[0], sem.at[0])])
+        for i in range(NZL):
+            out[0, i] = kept[i]
 
     @pl.when(nd > 0)
     def _():
@@ -427,28 +432,28 @@
     ga = lax.all_to_all(jnp.broadcast_to(gz[None], (16, 8, 16, NX)), "space", 0, 0)
     gb = lax.ppermute(ga, "tm", swap)
 
-    wide, change = pl.pallas_call(
+    wide, change, kept = pl.pallas_call(
         sweep_kernel,
-        out_shape=(pltpu.VMEM((16, 4 * NX), F32), shape((1, 1), F32)),
-        in_specs=[VM, VM],
-        out_specs=(VM, pl.BlockSpec(memory_space=pltpu.SMEM)),
+        out_shape=(pltpu.VMEM((16, 4 * NX), F32), shape((1, 1), F32), pltpu.VMEM((NZL,) + plane, F32)),
+        in_specs=[VM, VM, HBM],
+        out_specs=(VM, pl.BlockSpec(memory_space=pltpu.SMEM), VM),
         scratch_shapes=[
             pltpu.VMEM((7, 24, 8, NX), F32),
             pltpu.VMEM((15, 12, 16, NX), F32),
             pltpu.VMEM((8, NX), F32),
+            pltpu.SemaphoreType.DMA((1,)),
         ],
         compiler_params=pltpu.CompilerParams(vmem_limit_bytes=LIMIT),
         name="sweep",
-    )(near(ga.reshape(2048, NX)), near(gb.reshape(2048, NX)))
+    )(near(ga.reshape(2048, NX)), near(gb.reshape(2048, NX)), far(starts))
     new = pl.pallas_call(
         finish_kernel,
         out_shape=shape((1, NZL) + plane, F32),
-        in_specs=[VM, VM, HBM],
+        in_specs=[VM, VM, VM],
         out_specs=VM,
-        scratch_shapes=[pltpu.SemaphoreType.DMA((1,))],
         compiler_params=pltpu.CompilerParams(vmem_limit_bytes=LIMIT),
         name="finish",
-    )(near(wide), near(moved), far(starts))
+    )(near(wide), near(moved), near(kept))
     return new, change.reshape(())
 
 

time: 77.3 us -> 77.1 us (level)
  no operation moved by 1% of the time
where the time goes in v5:
time: 77.1 us; the launch traced here: 76.8 us
  blocking collectives  41.4 us (54%)
  starting transfers between devices  18.4 us (24%)
  Pallas kernels  11.3 us (15%)
  waiting for transfers between devices  4.93 us (6%)
    all_to_all x1, blocking collectives, per_device(): lax.all_to_all(jnp.broadcast_to(gz[None], (16, 8, 16, NX)), 'space', 0, 0)  26.1 us
    all_to_all x1, blocking collectives, per_device(): gz = lax.all_to_all(pay, 'tm', 0, 0, axis_index_groups=zgroups)  15.3 us
    ppermute x1, starting transfers between devices, per_device(): ha = lax.ppermute(ha, 'space', even)  4.01 us
    pallas_call x1, Pallas kernels, per_device(): pl.pallas_call(sweep_kernel, out_shape=(pltpu.VMEM((16, 4 * NX), F32), sh...  3.91 us
    ppermute x1, starting transfers between devices, per_device(): gb = lax.ppermute(ga, 'tm', swap)  3.25 us
    ppermute x1, starting transfers between devices, per_device(): nxt = lax.ppermute(starts[0], 'tm', down)  3.1 us
    pallas_call x1, Pallas kernels, per_device(): pl.pallas_call(prep_kernel, out_shape=(pltpu.VMEM((7, NZL) + plane, F32),...  2.86 us
    ppermute x1, starting transfers between devices, per_device(): sa = lax.ppermute(ca, 'tm', swap)  2.48 us
  transfers between devices with their start and end apart: 9, of which 4 were waited for; matrix products, arithmetic and copies ran while one was open for 0% of the time, Pallas kernels for 10%

profile of v5, /device:TPU:1, one launch (start us, length us, event | category | flops | bytes accessed | tf_op | source)
XLA Modules:
  0.0 76.8 jit_solution(14996791023429607794)
XLA Ops:
  0.6 1.4 %pack.1 = (f32[10,64,128]{2,1,0:T(8,128)S(1)}, f32[10,64,128]{2,1,0:T(8,128)S(1)}, f32[6,64,128]{2,1,0:T(8,128)S(1)}, f32[6,64,128]{2,1,0:T(8,128)S(1)}) custom-call(f32[1,12,64,128]{3,2,1,0:T(8,128)} %st.5, f32[12,64,128]{2,1,0:T(8,128)} %vx.3, f32[12,64,128]{2,1,0:T(8,128)} %vy.3, f32[12,64,128]{2,1,0:T(8,128)} %vz.3, f32[12,64,128]{2,1,0:T(8,128)} %ka.3), custom_call_target="tpu_custom_call" | custom-call | tf_op jit(solution)/shard_map/pack/pallas_call | solution.py:376
  2.0 2.1 %collective-permute-start.4 = (f32[10,64,128]{2,1,0:T(8,128)S(1)}, f32[10,64,128]{2,1,0:T(8,128)S(1)}, u32[]{:S(2)}, u32[]{:S(2)}) collective-permute-start(f32[10,64,128]{2,1,0:T(8,128)S(1)} %get-tuple-element.19), channel_id=1, source_target_pairs={{0,1},{1,0},{2,3},{3,2},{4,5},{5,4},{6,7},{7,6},{8,9},{9,8},{10,11... | collective-permute-start | bytes 983048 | tf_op jit(solution)/shard_map/ppermute | solution.py:385
  4.1 0.7 collective-permute-start.1
  4.8 3.1 %collective-permute-start.6 = (f32[12,64,128]{2,1,0:T(8,128)}, f32[12,64,128]{2,1,0:T(8,128)S(1)}, u32[]{:S(2)}, u32[]{:S(2)}) collective-permute-start(f32[12,64,128]{2,1,0:T(8,128)} %bitcast.6), channel_id=1, source_target_pairs={{16,0},{32,16},{48,32},{64,48},{80,64},{96,80},{112,96},{128,112},... | collective-permute-start | bytes 1179656 | tf_op jit(solution)/shard_map/ppermute | solution.py:389
  7.9 2.4 %collective-permute-done.4.own = f32[10,64,128]{2,1,0:T(8,128)S(1)} collective-permute-done((f32[10,64,128]{2,1,0:T(8,128)S(1)}, f32[10,64,128]{2,1,0:T(8,128)S(1)}, u32[]{:S(2)}, u32[]{:S(2)}) %collective-permute-start.4) | collective-permute-done | bytes 327712 | tf_op jit(solution)/shard_map/ppermute | solution.py:385
  10.3 2.5 %collective-permute-start.5 = (f32[10,64,128]{2,1,0:T(8,128)S(1)}, f32[10,64,128]{2,1,0:T(8,128)S(1)}, u32[]{:S(2)}, u32[]{:S(2)}) collective-permute-start(f32[10,64,128]{2,1,0:T(8,128)S(1)} %collective-permute-done.4.own), channel_id=1, source_target_pairs={{0,16},{16,0},{32,48},{48,32},{64,80},{80,64},{96,112},{112,96},{1... | collective-permute-start | bytes 983048 | tf_op jit(solution)/shard_map/ppermute | solution.py:409
  12.8 0.0 collective-permute-done.1.own
  12.8 0.0 collective-permute-start.2
  12.8 4.0 %collective-permute-start.3 = (f32[6,64,128]{2,1,0:T(8,128)S(1)}, f32[6,64,128]{2,1,0:T(8,128)S(1)}, u32[]{:S(2)}, u32[]{:S(2)}) collective-permute-start(f32[6,64,128]{2,1,0:T(8,128)S(1)} %get-tuple-element.18), channel_id=1, source_target_pairs={{0,1},{1,0},{2,3},{3,2},{4,5},{5,4},{6,7},{7,6},{8,9},{9,8},{10,11... | collective-permute-start | bytes 589832 | tf_op jit(solution)/shard_map/ppermute | solution.py:387
  16.8 0.7 collective-permute-start
  17.5 2.9 %prep.1 = (f32[7,12,64,128]{3,2,1,0:T(8,128)S(1)}, f32[6,12,64,128]{3,2,1,0:T(8,128)S(1)}, f32[8,128]{1,0:T(8,128)S(1)}) custom-call(f32[1,12,64,128]{3,2,1,0:T(8,128)} %st.5, f32[12,64,128]{2,1,0:T(8,128)} %vx.3, f32[12,64,128]{2,1,0:T(8,128)} %vy.3, f32[12,64,128]{2,1,0:T(8,128)} %vz.3, f32[12,64,128]{2,1,0:T(8,128)} %ka.3), custom_call_target="tpu_custom_call" | custom-call | tf_op jit(solution)/shard_map/prep/pallas_call | solution.py:390
  20.4 1.7 %collective-permute-done.3.edge = f32[6,64,128]{2,1,0:T(8,128)S(1)} collective-permute-done((f32[6,64,128]{2,1,0:T(8,128)S(1)}, f32[6,64,128]{2,1,0:T(8,128)S(1)}, u32[]{:S(2)}, u32[]{:S(2)}) %collective-permute-start.3) | collective-permute-done | bytes 196640 | tf_op jit(solution)/shard_map/ppermute | solution.py:387
  22.1 0.0 collective-permute-done.5.other
  22.1 1.0 %first.1.half = f32[6,64,128]{2,1,0:T(8,128)S(1)} custom-call(f32[6,64,128]{2,1,0:T(8,128)S(1)} %collective-permute-done.3.edge, f32[10,64,128]{2,1,0:T(8,128)S(1)} %collective-permute-done.4.own, f32[10,64,128]{2,1,0:T(8,128)S(1)} %collective-permute-done.5.other, f32[7,12,64,128]{3,2,1,0:T(8,128)S(1)} %get-tuple-element.16.w, ...), custom_call_target="tpu_custom_call" | custom-call | tf_op jit(solution)/shard_map/first/pallas_call | solution.py:410
  23.1 0.0 collective-permute-done.edge
  23.1 0.0 collective-permute-done.6.nx
  23.1 0.0 collective-permute-done.2.other
  23.1 1.4 %second.1 = (f32[12,64,128]{2,1,0:T(8,128)S(1)}, f32[8,16,128]{2,1,0:T(8,128)S(1)}) custom-call(f32[6,64,128]{2,1,0:T(8,128)S(1)} %collective-permute-done.edge, f32[10,64,128]{2,1,0:T(8,128)S(1)} %collective-permute-done.1.own, f32[10,64,128]{2,1,0:T(8,128)S(1)} %collective-permute-done.2.other, f32[7,12,64,128]{3,2,1,0:T(8,128)S(1)} %get-tuple-element.16.w, ...), custom_call_target="tpu_custom_call" | custom-call | tf_op jit(solution)/shard_map/second/pallas_call | solution.py:420
  24.5 15.3 %all_to_all.10 = f32[8,16,128]{2,1,0:T(8,128)S(1)} all-to-all(f32[8,16,128]{2,1,0:T(8,128)S(1)} %get-tuple-element.21), channel_id=1, replica_groups={{0,32,64,96,128,160,192,224},{16,48,80,112,144,176,208,240},{1,33,65,97..., dimensions={0} | all-to-all | bytes 131072 | tf_op jit(solution)/shard_map/all_to_all | solution.py:430
  39.8 0.1 broadcast_in_dim.2
  39.9 26.1 %all_to_all.11 = f32[16,8,16,128]{3,2,1,0:T(8,128)S(1)} all-to-all(f32[16,8,16,128]{3,2,1,0:T(8,128)S(1)} %broadcast_in_dim.2), channel_id=1, replica_groups=mesh['tm'=16,'space'=16] {'space'}, dimensions={0} | all-to-all | bytes 2097152 | tf_op jit(solution)/shard_map/all_to_all | solution.py:432
  66.0 3.3 %collective-permute-start.7 = (f32[16,8,16,128]{3,2,1,0:T(8,128)S(1)}, f32[16,8,16,128]{3,2,1,0:T(8,128)S(1)}, u32[]{:S(2)}, u32[]{:S(2)}) collective-permute-start(f32[16,8,16,128]{3,2,1,0:T(8,128)S(1)} %all_to_all.11), channel_id=1, source_target_pairs={{0,16},{16,0},{32,48},{48,32},{64,80},{80,64},{96,112},{112,96},{1... | collective-permute-start | bytes 3145736 | tf_op jit(solution)/shard_map/ppermute | solution.py:433
  69.3 2.1 %collective-permute-start.8 = (f32[12,64,128]{2,1,0:T(8,128)S(1)}, f32[12,64,128]{2,1,0:T(8,128)S(1)}, u32[]{:S(2)}, u32[]{:S(2)}) collective-permute-start(f32[12,64,128]{2,1,0:T(8,128)S(1)} %get-tuple-element.23), channel_id=1, source_target_pairs={{0,16},{16,32},{32,48},{48,64},{64,80},{80,96},{96,112},{112,128},... | collective-permute-start | bytes 1179656 | tf_op jit(solution)/shard_map/ppermute | solution.py:431
  71.4 0.2 collective-permute-done.7
  71.6 3.9 %sweep.1 = (f32[16,512]{1,0:T(8,128)S(1)}, f32[1,1]{1,0:T(1,128)}, f32[12,64,128]{2,1,0:T(8,128)S(1)}) custom-call(f32[2048,128]{1,0:T(8,128)S(1)} %bitcast.4, f32[2048,128]{1,0:T(8,128)S(1)} %bitcast.5, f32[1,12,64,128]{3,2,1,0:T(8,128)} %st.5), custom_call_target="tpu_custom_call" | custom-call | tf_op jit(solution)/shard_map/sweep/pallas_call | solution.py:435
  75.5 0.6 collective-permute-done.8.fine
  76.1 0.8 %finish.1 = f32[1,12,64,128]{3,2,1,0:T(8,128)} custom-call(f32[16,512]{1,0:T(8,128)S(1)} %get-tuple-element.22.wide, f32[12,64,128]{2,1,0:T(8,128)S(1)} %collective-permute-done.8.fine, f32[12,64,128]{2,1,0:T(8,128)S(1)} %get-tuple-element.24.kept), custom_call_target="tpu_custom_call" | custom-call | tf_op jit(solution)/shard_map/finish/pallas_call | solution.py:449
Async XLA Ops:
  2.0 8.3 %collective-permute-start.4 = (f32[10,64,128]{2,1,0:T(8,128)S(1)}, f32[10,64,128]{2,1,0:T(8,128)S(1)}, u32[]{:S(2)}, u32[]{:S(2)}) collective-permute-start(f32[10,64,128]{2,1,0:T(8,128)S(1)} %get-tuple-element.19), channel_id=1, source_target_pairs={{0,1},{1,0},{2,3},{3,2},{4,5},{5,4},{6,7},{7,6},{8,9},{9,8},{10,11... | collective-permute-start | bytes 983048 | tf_op jit(solution)/shard_map/ppermute | solution.py:385
  4.1 8.7 %collective-permute-start.1 = (f32[10,64,128]{2,1,0:T(8,128)S(1)}, f32[10,64,128]{2,1,0:T(8,128)S(1)}, u32[]{:S(2)}, u32[]{:S(2)}) collective-permute-start(f32[10,64,128]{2,1,0:T(8,128)S(1)} %get-tuple-element.15), channel_id=1, source_target_pairs={{1,2},{3,4},{5,6},{7,8},{9,10},{11,12},{13,14},{2,1},{4,3},{6,5},{... | collective-permute-start | bytes 983048 | tf_op jit(solution)/shard_map/ppermute | solution.py:386
  4.8 18.3 %collective-permute-start.6 = (f32[12,64,128]{2,1,0:T(8,128)}, f32[12,64,128]{2,1,0:T(8,128)S(1)}, u32[]{:S(2)}, u32[]{:S(2)}) collective-permute-start(f32[12,64,128]{2,1,0:T(8,128)} %bitcast.6), channel_id=1, source_target_pairs={{16,0},{32,16},{48,32},{64,48},{80,64},{96,80},{112,96},{128,112},... | collective-permute-start | bytes 1179656 | tf_op jit(solution)/shard_map/ppermute | solution.py:389
  10.3 11.8 %collective-permute-start.5 = (f32[10,64,128]{2,1,0:T(8,128)S(1)}, f32[10,64,128]{2,1,0:T(8,128)S(1)}, u32[]{:S(2)}, u32[]{:S(2)}) collective-permute-start(f32[10,64,128]{2,1,0:T(8,128)S(1)} %collective-permute-done.4.own), channel_id=1, source_target_pairs={{0,16},{16,0},{32,48},{48,32},{64,80},{80,64},{96,112},{112,96},{1... | collective-permute-start | bytes 983048 | tf_op jit(solution)/shard_map/ppermute | solution.py:409
  12.8 10.3 %collective-permute-start.2 = (f32[10,64,128]{2,1,0:T(8,128)S(1)}, f32[10,64,128]{2,1,0:T(8,128)S(1)}, u32[]{:S(2)}, u32[]{:S(2)}) collective-permute-start(f32[10,64,128]{2,1,0:T(8,128)S(1)} %collective-permute-done.1.own), channel_id=1, source_target_pairs={{0,16},{16,0},{32,48},{48,32},{64,80},{80,64},{96,112},{112,96},{1... | collective-permute-start | bytes 983048 | tf_op jit(solution)/shard_map/ppermute | solution.py:419
  12.8 9.3 %collective-permute-start.3 = (f32[6,64,128]{2,1,0:T(8,128)S(1)}, f32[6,64,128]{2,1,0:T(8,128)S(1)}, u32[]{:S(2)}, u32[]{:S(2)}) collective-permute-start(f32[6,64,128]{2,1,0:T(8,128)S(1)} %get-tuple-element.18), channel_id=1, source_target_pairs={{0,1},{1,0},{2,3},{3,2},{4,5},{5,4},{6,7},{7,6},{8,9},{9,8},{10,11... | collective-permute-start | bytes 589832 | tf_op jit(solution)/shard_map/ppermute | solution.py:387
  16.8 6.2 %collective-permute-start = (f32[6,64,128]{2,1,0:T(8,128)S(1)}, f32[6,64,128]{2,1,0:T(8,128)S(1)}, u32[]{:S(2)}, u32[]{:S(2)}) collective-permute-start(f32[6,64,128]{2,1,0:T(8,128)S(1)} %get-tuple-element.14), channel_id=1, source_target_pairs={{1,2},{3,4},{5,6},{7,8},{9,10},{11,12},{13,14},{2,1},{4,3},{6,5},{... | collective-permute-start | bytes 589832 | tf_op jit(solution)/shard_map/ppermute | solution.py:388
  66.0 5.5 %collective-permute-start.7 = (f32[16,8,16,128]{3,2,1,0:T(8,128)S(1)}, f32[16,8,16,128]{3,2,1,0:T(8,128)S(1)}, u32[]{:S(2)}, u32[]{:S(2)}) collective-permute-start(f32[16,8,16,128]{3,2,1,0:T(8,128)S(1)} %all_to_all.11), channel_id=1, source_target_pairs={{0,16},{16,0},{32,48},{48,32},{64,80},{80,64},{96,112},{112,96},{1... | collective-permute-start | bytes 3145736 | tf_op jit(solution)/shard_map/ppermute | solution.py:433
  69.3 6.8 %collective-permute-start.8 = (f32[12,64,128]{2,1,0:T(8,128)S(1)}, f32[12,64,128]{2,1,0:T(8,128)S(1)}, u32[]{:S(2)}, u32[]{:S(2)}) collective-permute-start(f32[12,64,128]{2,1,0:T(8,128)S(1)} %get-tuple-element.23), channel_id=1, source_target_pairs={{0,16},{16,32},{32,48},{48,64},{64,80},{80,96},{96,112},{112,128},... | collective-permute-start | bytes 1179656 | tf_op jit(solution)/shard_map/ppermute | solution.py:431

commit v6 on v5

--- a/solution.py
+++ b/solution.py
@@ -193,12 +193,12 @@
     def put(k, q, new):
         half[k - 6] = new
 
-    wedge(1 - lax.rem(lax.axis_index("space"), 2), edge, own, other, w, lev, put, u, wk)
+    wedge(lax.rem(lax.axis_index("space"), 2), edge, own, other, w, lev, put, u, wk)
 
 
 def second_kernel(edge, own, other, w, lev, half, part, nx, fine, pay, u, wk, rows, ck):
     n = lax.axis_index("tm")
-    hi = lax.rem(lax.axis_index("space"), 2)
+    hi = 1 - lax.rem(lax.axis_index("space"), 2)
 
     def put(k, q, new):
         fine[q] = new
@@ -407,6 +407,7 @@
     )(*(far(x) for x in (starts, vel_x, vel_y, vel_z, kappa)))
     work = [pltpu.VMEM((2, 13) + plane, F32), pltpu.VMEM((7, 12) + plane, F32)]
     sa = lax.ppermute(ca, "tm", swap)
+    sb = lax.ppermute(cb, "tm", swap)
     half = pl.pallas_call(
         first_kernel,
         out_shape=pltpu.VMEM((6,) + plane, F32),
@@ -415,8 +416,7 @@
         scratch_shapes=work,
         compiler_params=pltpu.CompilerParams(vmem_limit_bytes=LIMIT),
         name="first",
-    )(near(ha), near(ca), near(sa), near(w), near(lev))
-    sb = lax.ppermute(cb, "tm", swap)
+    )(near(hb), near(cb), near(sb), near(w), near(lev))
     fine, pay = pl.pallas_call(
         second_kernel,
         out_shape=(pltpu.VMEM((NZL,) + plane, F32), pltpu.VMEM((8, 16, NX), F32)),
@@ -425,7 +425,7 @@
         scratch_shapes=work + [pltpu.VMEM((48, NX), F32), pltpu.VMEM((48, NX), F32)],
         compiler_params=pltpu.CompilerParams(vmem_limit_bytes=LIMIT),
         name="second",
-    )(near(hb), near(cb), near(sb), near(w), near(lev), near(half), near(part), near(nxt))
+    )(near(ha), near(ca), near(sa), near(w), near(lev), near(half), near(part), near(nxt))
 
     gz = lax.all_to_all(pay, "tm", 0, 0, axis_index_groups=zgroups)
     moved = lax.ppermute(fine, "tm", up)

time: 77.1 us -> 77 us (level)
  blocking collectives: 41.4 us -> 38.5 us
  starting transfers between devices: 18.4 us -> 20.3 us
  waiting for transfers between devices: 4.93 us -> 5.83 us
    all_to_all x1, blocking collectives: 26.1 us -> 23.3 us  [per_device(): lax.all_to_all(jnp.broadcast_to(gz[None], (16, 8, 16, NX)), 'space', 0, 0)]
    ppermute x1, starting transfers between devices: 2.12 us -> 4.55 us  [per_device(): ca = lax.ppermute(ca, 'space', even)]
    ppermute x1, waiting for transfers between devices: 2.4 us -> 3.9 us  [per_device(): ca = lax.ppermute(ca, 'space', even)]
    ppermute x1, starting transfers between devices: 2.48 us -> 1.52 us  [per_device(): sa = lax.ppermute(ca, 'tm', swap)]
    ppermute x1, starting transfers between devices: 3.25 us -> 4.16 us  [per_device(): gb = lax.ppermute(ga, 'tm', swap)]
where the time goes in v6:
time: 77 us; the launch traced here: 76.7 us
  blocking collectives  38.5 us (50%)
  starting transfers between devices  20.3 us (26%)
  Pallas kernels  11.3 us (15%)
  waiting for transfers between devices  5.83 us (8%)
    all_to_all x1, blocking collectives, per_device(): lax.all_to_all(jnp.broadcast_to(gz[None], (16, 8, 16, NX)), 'space', 0, 0)  23.3 us
    all_to_all x1, blocking collectives, per_device(): gz = lax.all_to_all(pay, 'tm', 0, 0, axis_index_groups=zgroups)  15.2 us
    ppermute x1, starting transfers between devices, per_device(): ca = lax.ppermute(ca, 'space', even)  4.55 us
    ppermute x1, starting transfers between devices, per_device(): gb = lax.ppermute(ga, 'tm', swap)  4.16 us
    pallas_call x1, Pallas kernels, per_device(): pl.pallas_call(sweep_kernel, out_shape=(pltpu.VMEM((16, 4 * NX), F32), sh...  3.91 us
    ppermute x1, waiting for transfers between devices, per_device(): ca = lax.ppermute(ca, 'space', even)  3.9 us
    ppermute x1, starting transfers between devices, per_device(): ha = lax.ppermute(ha, 'space', even)  3.45 us
    ppermute x1, starting transfers between devices, per_device(): nxt = lax.ppermute(starts[0], 'tm', down)  3.12 us
  transfers between devices with their start and end apart: 9, of which 4 were waited for; matrix products, arithmetic and copies ran while one was open for 0% of the time, Pallas kernels for 10%

profile of v6, /device:TPU:1, one launch (start us, length us, event | category | flops | bytes accessed | tf_op | source)
XLA Modules:
  0.0 76.7 jit_solution(11480258193403563219)
XLA Ops:
  0.6 1.4 %pack.1 = (f32[10,64,128]{2,1,0:T(8,128)S(1)}, f32[10,64,128]{2,1,0:T(8,128)S(1)}, f32[6,64,128]{2,1,0:T(8,128)S(1)}, f32[6,64,128]{2,1,0:T(8,128)S(1)}) custom-call(f32[1,12,64,128]{3,2,1,0:T(8,128)} %st.5, f32[12,64,128]{2,1,0:T(8,128)} %vx.3, f32[12,64,128]{2,1,0:T(8,128)} %vy.3, f32[12,64,128]{2,1,0:T(8,128)} %vz.3, f32[12,64,128]{2,1,0:T(8,128)} %ka.3), custom_call_target="tpu_custom_call" | custom-call | tf_op jit(solution)/shard_map/pack/pallas_call | solution.py:376
  2.0 0.7 collective-permute-start.4
  2.7 4.6 %collective-permute-start.1 = (f32[10,64,128]{2,1,0:T(8,128)S(1)}, f32[10,64,128]{2,1,0:T(8,128)S(1)}, u32[]{:S(2)}, u32[]{:S(2)}) collective-permute-start(f32[10,64,128]{2,1,0:T(8,128)S(1)} %get-tuple-element.15), channel_id=1, source_target_pairs={{0,1},{1,0},{2,3},{3,2},{4,5},{5,4},{6,7},{7,6},{8,9},{9,8},{10,11... | collective-permute-start | bytes 983048 | tf_op jit(solution)/shard_map/ppermute | solution.py:385
  7.3 3.1 %collective-permute-start.6 = (f32[12,64,128]{2,1,0:T(8,128)}, f32[12,64,128]{2,1,0:T(8,128)S(1)}, u32[]{:S(2)}, u32[]{:S(2)}) collective-permute-start(f32[12,64,128]{2,1,0:T(8,128)} %bitcast.6), channel_id=1, source_target_pairs={{16,0},{32,16},{48,32},{64,48},{80,64},{96,80},{112,96},{128,112},... | collective-permute-start | bytes 1179656 | tf_op jit(solution)/shard_map/ppermute | solution.py:389
  10.4 0.0 collective-permute-done.4.own
  10.4 0.1 collective-permute-start.5
  10.5 3.9 %collective-permute-done.1.own = f32[10,64,128]{2,1,0:T(8,128)S(1)} collective-permute-done((f32[10,64,128]{2,1,0:T(8,128)S(1)}, f32[10,64,128]{2,1,0:T(8,128)S(1)}, u32[]{:S(2)}, u32[]{:S(2)}) %collective-permute-start.1) | collective-permute-done | bytes 327712 | tf_op jit(solution)/shard_map/ppermute | solution.py:385
  14.4 1.5 %collective-permute-start.2 = (f32[10,64,128]{2,1,0:T(8,128)S(1)}, f32[10,64,128]{2,1,0:T(8,128)S(1)}, u32[]{:S(2)}, u32[]{:S(2)}) collective-permute-start(f32[10,64,128]{2,1,0:T(8,128)S(1)} %collective-permute-done.1.own), channel_id=1, source_target_pairs={{0,16},{16,0},{32,48},{48,32},{64,80},{80,64},{96,112},{112,96},{1... | collective-permute-start | bytes 983048 | tf_op jit(solution)/shard_map/ppermute | solution.py:409
  15.9 0.7 collective-permute-start.3
  16.6 3.5 %collective-permute-start = (f32[6,64,128]{2,1,0:T(8,128)S(1)}, f32[6,64,128]{2,1,0:T(8,128)S(1)}, u32[]{:S(2)}, u32[]{:S(2)}) collective-permute-start(f32[6,64,128]{2,1,0:T(8,128)S(1)} %get-tuple-element.14), channel_id=1, source_target_pairs={{0,1},{1,0},{2,3},{3,2},{4,5},{5,4},{6,7},{7,6},{8,9},{9,8},{10,11... | collective-permute-start | bytes 589832 | tf_op jit(solution)/shard_map/ppermute | solution.py:387
  20.1 2.9 %prep.1 = (f32[7,12,64,128]{3,2,1,0:T(8,128)S(1)}, f32[6,12,64,128]{3,2,1,0:T(8,128)S(1)}, f32[8,128]{1,0:T(8,128)S(1)}) custom-call(f32[1,12,64,128]{3,2,1,0:T(8,128)} %st.5, f32[12,64,128]{2,1,0:T(8,128)} %vx.3, f32[12,64,128]{2,1,0:T(8,128)} %vy.3, f32[12,64,128]{2,1,0:T(8,128)} %vz.3, f32[12,64,128]{2,1,0:T(8,128)} %ka.3), custom_call_target="tpu_custom_call" | custom-call | tf_op jit(solution)/shard_map/prep/pallas_call | solution.py:390
  22.9 0.0 collective-permute-done.3.edge
  22.9 0.0 collective-permute-done.5.other
  22.9 1.0 %first.1.half = f32[6,64,128]{2,1,0:T(8,128)S(1)} custom-call(f32[6,64,128]{2,1,0:T(8,128)S(1)} %collective-permute-done.3.edge, f32[10,64,128]{2,1,0:T(8,128)S(1)} %collective-permute-done.4.own, f32[10,64,128]{2,1,0:T(8,128)S(1)} %collective-permute-done.5.other, f32[7,12,64,128]{3,2,1,0:T(8,128)S(1)} %get-tuple-element.16.w, ...), custom_call_target="tpu_custom_call" | custom-call | tf_op jit(solution)/shard_map/first/pallas_call | solution.py:411
  23.9 1.1 %collective-permute-done.edge = f32[6,64,128]{2,1,0:T(8,128)S(1)} collective-permute-done((f32[6,64,128]{2,1,0:T(8,128)S(1)}, f32[6,64,128]{2,1,0:T(8,128)S(1)}, u32[]{:S(2)}, u32[]{:S(2)}) %collective-permute-start) | collective-permute-done | bytes 196640 | tf_op jit(solution)/shard_map/ppermute | solution.py:387
  25.1 0.0 collective-permute-done.6.nx
  25.1 0.0 collective-permute-done.2.other
  25.1 1.4 %second.1 = (f32[12,64,128]{2,1,0:T(8,128)S(1)}, f32[8,16,128]{2,1,0:T(8,128)S(1)}) custom-call(f32[6,64,128]{2,1,0:T(8,128)S(1)} %collective-permute-done.edge, f32[10,64,128]{2,1,0:T(8,128)S(1)} %collective-permute-done.1.own, f32[10,64,128]{2,1,0:T(8,128)S(1)} %collective-permute-done.2.other, f32[7,12,64,128]{3,2,1,0:T(8,128)S(1)} %get-tuple-element.16.w, ...), custom_call_target="tpu_custom_call" | custom-call | tf_op jit(solution)/shard_map/second/pallas_call | solution.py:420
  26.4 15.2 %all_to_all.10 = f32[8,16,128]{2,1,0:T(8,128)S(1)} all-to-all(f32[8,16,128]{2,1,0:T(8,128)S(1)} %get-tuple-element.21), channel_id=1, replica_groups={{0,32,64,96,128,160,192,224},{16,48,80,112,144,176,208,240},{1,33,65,97..., dimensions={0} | all-to-all | bytes 131072 | tf_op jit(solution)/shard_map/all_to_all | solution.py:430
  41.7 0.1 broadcast_in_dim.2
  41.8 23.3 %all_to_all.11 = f32[16,8,16,128]{3,2,1,0:T(8,128)S(1)} all-to-all(f32[16,8,16,128]{3,2,1,0:T(8,128)S(1)} %broadcast_in_dim.2), channel_id=1, replica_groups=mesh['tm'=16,'space'=16] {'space'}, dimensions={0} | all-to-all | bytes 2097152 | tf_op jit(solution)/shard_map/all_to_all | solution.py:432
  65.0 4.2 %collective-permute-start.7 = (f32[16,8,16,128]{3,2,1,0:T(8,128)S(1)}, f32[16,8,16,128]{3,2,1,0:T(8,128)S(1)}, u32[]{:S(2)}, u32[]{:S(2)}) collective-permute-start(f32[16,8,16,128]{3,2,1,0:T(8,128)S(1)} %all_to_all.11), channel_id=1, source_target_pairs={{0,16},{16,0},{32,48},{48,32},{64,80},{80,64},{96,112},{112,96},{1... | collective-permute-start | bytes 3145736 | tf_op jit(solution)/shard_map/ppermute | solution.py:433
  69.2 2.0 %collective-permute-start.8 = (f32[12,64,128]{2,1,0:T(8,128)S(1)}, f32[12,64,128]{2,1,0:T(8,128)S(1)}, u32[]{:S(2)}, u32[]{:S(2)}) collective-permute-start(f32[12,64,128]{2,1,0:T(8,128)S(1)} %get-tuple-element.23), channel_id=1, source_target_pairs={{0,16},{16,32},{32,48},{48,64},{64,80},{80,96},{96,112},{112,128},... | collective-permute-start | bytes 1179656 | tf_op jit(solution)/shard_map/ppermute | solution.py:431
  71.2 0.3 collective-permute-done.7
  71.5 3.9 %sweep.1 = (f32[16,512]{1,0:T(8,128)S(1)}, f32[1,1]{1,0:T(1,128)}, f32[12,64,128]{2,1,0:T(8,128)S(1)}) custom-call(f32[2048,128]{1,0:T(8,128)S(1)} %bitcast.4, f32[2048,128]{1,0:T(8,128)S(1)} %bitcast.5, f32[1,12,64,128]{3,2,1,0:T(8,128)} %st.5), custom_call_target="tpu_custom_call" | custom-call | tf_op jit(solution)/shard_map/sweep/pallas_call | solution.py:435
  75.4 0.5 collective-permute-done.8.fine
  75.9 0.8 %finish.1 = f32[1,12,64,128]{3,2,1,0:T(8,128)} custom-call(f32[16,512]{1,0:T(8,128)S(1)} %get-tuple-element.22.wide, f32[12,64,128]{2,1,0:T(8,128)S(1)} %collective-permute-done.8.fine, f32[12,64,128]{2,1,0:T(8,128)S(1)} %get-tuple-element.24.kept), custom_call_target="tpu_custom_call" | custom-call | tf_op jit(solution)/shard_map/finish/pallas_call | solution.py:449
Async XLA Ops:
  2.0 8.4 %collective-permute-start.4 = (f32[10,64,128]{2,1,0:T(8,128)S(1)}, f32[10,64,128]{2,1,0:T(8,128)S(1)}, u32[]{:S(2)}, u32[]{:S(2)}) collective-permute-start(f32[10,64,128]{2,1,0:T(8,128)S(1)} %get-tuple-element.19), channel_id=1, source_target_pairs={{1,2},{3,4},{5,6},{7,8},{9,10},{11,12},{13,14},{2,1},{4,3},{6,5},{... | collective-permute-start | bytes 983048 | tf_op jit(solution)/shard_map/ppermute | solution.py:386
  2.7 11.7 %collective-permute-start.1 = (f32[10,64,128]{2,1,0:T(8,128)S(1)}, f32[10,64,128]{2,1,0:T(8,128)S(1)}, u32[]{:S(2)}, u32[]{:S(2)}) collective-permute-start(f32[10,64,128]{2,1,0:T(8,128)S(1)} %get-tuple-element.15), channel_id=1, source_target_pairs={{0,1},{1,0},{2,3},{3,2},{4,5},{5,4},{6,7},{7,6},{8,9},{9,8},{10,11... | collective-permute-start | bytes 983048 | tf_op jit(solution)/shard_map/ppermute | solution.py:385
  7.3 17.8 %collective-permute-start.6 = (f32[12,64,128]{2,1,0:T(8,128)}, f32[12,64,128]{2,1,0:T(8,128)S(1)}, u32[]{:S(2)}, u32[]{:S(2)}) collective-permute-start(f32[12,64,128]{2,1,0:T(8,128)} %bitcast.6), channel_id=1, source_target_pairs={{16,0},{32,16},{48,32},{64,48},{80,64},{96,80},{112,96},{128,112},... | collective-permute-start | bytes 1179656 | tf_op jit(solution)/shard_map/ppermute | solution.py:389
  10.4 12.5 %collective-permute-start.5 = (f32[10,64,128]{2,1,0:T(8,128)S(1)}, f32[10,64,128]{2,1,0:T(8,128)S(1)}, u32[]{:S(2)}, u32[]{:S(2)}) collective-permute-start(f32[10,64,128]{2,1,0:T(8,128)S(1)} %collective-permute-done.4.own), channel_id=1, source_target_pairs={{0,16},{16,0},{32,48},{48,32},{64,80},{80,64},{96,112},{112,96},{1... | collective-permute-start | bytes 983048 | tf_op jit(solution)/shard_map/ppermute | solution.py:410
  14.4 10.6 %collective-permute-start.2 = (f32[10,64,128]{2,1,0:T(8,128)S(1)}, f32[10,64,128]{2,1,0:T(8,128)S(1)}, u32[]{:S(2)}, u32[]{:S(2)}) collective-permute-start(f32[10,64,128]{2,1,0:T(8,128)S(1)} %collective-permute-done.1.own), channel_id=1, source_target_pairs={{0,16},{16,0},{32,48},{48,32},{64,80},{80,64},{96,112},{112,96},{1... | collective-permute-start | bytes 983048 | tf_op jit(solution)/shard_map/ppermute | solution.py:409
  15.9 7.0 %collective-permute-start.3 = (f32[6,64,128]{2,1,0:T(8,128)S(1)}, f32[6,64,128]{2,1,0:T(8,128)S(1)}, u32[]{:S(2)}, u32[]{:S(2)}) collective-permute-start(f32[6,64,128]{2,1,0:T(8,128)S(1)} %get-tuple-element.18), channel_id=1, source_target_pairs={{1,2},{3,4},{5,6},{7,8},{9,10},{11,12},{13,14},{2,1},{4,3},{6,5},{... | collective-permute-start | bytes 589832 | tf_op jit(solution)/shard_map/ppermute | solution.py:388
  16.6 8.4 %collective-permute-start = (f32[6,64,128]{2,1,0:T(8,128)S(1)}, f32[6,64,128]{2,1,0:T(8,128)S(1)}, u32[]{:S(2)}, u32[]{:S(2)}) collective-permute-start(f32[6,64,128]{2,1,0:T(8,128)S(1)} %get-tuple-element.14), channel_id=1, source_target_pairs={{0,1},{1,0},{2,3},{3,2},{4,5},{5,4},{6,7},{7,6},{8,9},{9,8},{10,11... | collective-permute-start | bytes 589832 | tf_op jit(solution)/shard_map/ppermute | solution.py:387
  65.0 6.4 %collective-permute-start.7 = (f32[16,8,16,128]{3,2,1,0:T(8,128)S(1)}, f32[16,8,16,128]{3,2,1,0:T(8,128)S(1)}, u32[]{:S(2)}, u32[]{:S(2)}) collective-permute-start(f32[16,8,16,128]{3,2,1,0:T(8,128)S(1)} %all_to_all.11), channel_id=1, source_target_pairs={{0,16},{16,0},{32,48},{48,32},{64,80},{80,64},{96,112},{112,96},{1... | collective-permute-start | bytes 3145736 | tf_op jit(solution)/shard_map/ppermute | solution.py:433
  69.2 6.7 %collective-permute-start.8 = (f32[12,64,128]{2,1,0:T(8,128)S(1)}, f32[12,64,128]{2,1,0:T(8,128)S(1)}, u32[]{:S(2)}, u32[]{:S(2)}) collective-permute-start(f32[12,64,128]{2,1,0:T(8,128)S(1)} %get-tuple-element.23), channel_id=1, source_target_pairs={{0,16},{16,32},{32,48},{48,64},{64,80},{80,96},{96,112},{112,128},... | collective-permute-start | bytes 1179656 | tf_op jit(solution)/shard_map/ppermute | solution.py:431
